TPU v7x, 32 devices: a whole 2x2x4 slice. The times are simulated.
32 devices in a mesh: dom: 8 (over y, x, core), sub: 4 (over z).
Axes of the slice: x: 2, y: 2, z: 4, core: 2. Of those that a mesh axis runs over, the one named last changes fastest.
Arguments:
- start_dofs: float32 [140, 8192], P(None, ('dom', 'sub')), may hold values from -6 to 6
- inv_jac: float32 [9, 8192], P(None, ('dom', 'sub')), may hold values from -2 to 2
- normals: float32 [12, 8192], P(None, ('dom', 'sub')), may hold values from -3.5 to 3.5
- bulk_modulus: float32 [8192], P(('dom', 'sub')), may hold values from 0.5 to 2
- density: float32 [8192], P(('dom', 'sub')), may hold values from 0.5 to 2
- deriv_mats: float32 [3, 35, 35], replicated, may hold values from -1 to 1
- face_proj: float32 [4, 15, 35], replicated, may hold values from -1 to 1
- face_lift: float32 [4, 35, 15], replicated, may hold values from -1 to 1
- cluster: int32 [8192], P(('dom', 'sub')), may hold values from 0 to 1, as said below
- pml_flags: int32 [8192], P(('dom', 'sub')), may hold values 0 or 1
- neighbours: int32 [4, 8192], P(None, ('dom', 'sub')), may hold values from 0 to 1343, as said below
- dom_send: int32 [64, 96], P(('dom', 'sub')), may hold values from 0 to 1023, as said below
- sub_send: int32 [128, 32], P(('dom', 'sub')), may hold values from 0 to 1022, as said below
Outputs:
- final_dofs: float32 [140, 8192], P(None, ('dom', 'sub'))
Inputs may be any that keep to these rules, and one draw needn't show every extreme that they name: `cluster`: on every device the fine elements come first among its 256 elements; a device holds at most 64 of them, and some device exactly 64. `neighbours`: each face names one column of its device's trace pool. Own faces that are not listed for sending name each other in pairs. The face at place j of dom_send row 0 names place j of the block from the device before, the one at place j of row 1 place j of the block from the device after; the face at place j of the sub_send row for device b names place j of the block from b, or place j + 1 - 2 (j % 2) when b is the device itself. `dom_send`: together with its sub_send rows, the rows of one device list distinct columns of its own faces; every device lists its last face column here. `sub_send`: together with its dom_send rows, the rows of one device list distinct columns of its own faces; every device lists its second-to-last face column here.
All inputs are finite; a program needn't handle non-finite values. No bound on the sum of `pml_flags` on one device may be relied on, other than what follows from the above.
Results may differ from a plain program's by a relative error of at most 0.0003.
Values sent between devices are 32-bit elements; how exact they have to be, the bound alone decides.
No kernel may reach another device: no remote copies, remote signals or barrier semaphores. Data moves between devices by JAX's collectives and lax.ppermute only.
A program may use at most 64 MiB of HBM per device.

v0:
```python
import math

import jax
import jax.numpy as jnp
from jax import lax
from jax.sharding import PartitionSpec as P

NQ = 4
NB = 35
ORDER = 5
SUBSTEPS = 4


exact_dots = lax.Precision.HIGHEST
step_size = 0.8
sigma_pml = 1.5


def from_behind(shard, axis, by):
    peers = lax.axis_size(axis)
    pairs = [(i, i + by) for i in range(peers) if 0 <= i + by < peers]
    return lax.ppermute(shard, axis, pairs)


def apply_operator(coeffs, material):
    inv_jac, bulk_modulus, density, damping, deriv_mats = material
    n_basis = deriv_mats.shape[1]
    pressure = coeffs[0]
    velocity = coeffs[1:]
    stacked = deriv_mats.reshape(3 * n_basis, n_basis)
    d_press = jnp.dot(stacked, pressure, precision=exact_dots).reshape(3, n_basis, -1)
    jacobian = inv_jac.reshape(3, 3, -1)
    gradient = jnp.sum(jacobian[:, :, None, :] * d_press[:, None, :, :], axis=0)
    mixed_vel = jnp.sum(jacobian[:, :, None, :] * velocity[None, :, :, :], axis=1)
    joined = jnp.transpose(deriv_mats, (1, 0, 2)).reshape(n_basis, 3 * n_basis)
    diverg = jnp.dot(joined, mixed_vel.reshape(3 * n_basis, -1), precision=exact_dots)
    press_rate = -bulk_modulus * diverg - damping * pressure
    veloc_rate = -gradient / density - damping * velocity
    return jnp.concatenate([press_rate[None], veloc_rate], axis=0)


def taylor(coeffs, material):
    deriv_terms = [coeffs]
    for power in range(ORDER - 1):
        deriv_terms.append(apply_operator(deriv_terms[-1], material))
    return deriv_terms


def integrate(deriv_terms, start_time, end_time):
    summed = None
    for power, taylor_term in enumerate(deriv_terms):
        weight = (end_time ** (power + 1) - start_time ** (power + 1)) / math.factorial(power + 1)
        scaled = weight * taylor_term
        summed = scaled if summed is None else summed + scaled
    return summed


def face_traces(coeffs, face_proj):
    face_parts = []
    for face_idx in range(4):
        traced = jnp.einsum("kb,qbe->kqe", face_proj[face_idx], coeffs, precision=exact_dots)
        face_parts.append(traced.reshape(-1, coeffs.shape[2]))
    return jnp.concatenate(face_parts, axis=1)


def corrections(own_traces, nbr_traces, normals, bulk_modulus, density, face_lift):
    n_elem = normals.shape[1]
    n_face = face_lift.shape[2]
    jump_all = (nbr_traces - own_traces).reshape(n_face, 4, 4, n_elem)
    jump_press = jump_all[:, 0]
    jump_vel = jump_all[:, 1:]
    facing = jnp.transpose(normals.reshape(4, 3, n_elem), (1, 0, 2))
    normal_flow = jnp.sum(facing[None] * jump_vel, axis=1)
    sound_speed = jnp.sqrt(bulk_modulus / density)
    penalty = sound_speed * jnp.sqrt(jnp.sum(facing * facing, axis=0))
    flux_press = 0.5 * (bulk_modulus * normal_flow - penalty * jump_press)
    flux_veloc = 0.5 * (facing[None] * jump_press[:, None] / density - penalty * jump_vel)
    flux_all = jnp.concatenate([flux_press[:, None], flux_veloc], axis=1)
    return jnp.einsum("fbk,kqfe->qbe", face_lift, flux_all, precision=exact_dots)


def gather_faces(own_traces, dom_send, sub_send):
    n_chan = own_traces.shape[0]
    n_sub = sub_send.shape[0]
    sub_width = sub_send.shape[1]
    dom_out = jnp.stack(
        [jnp.take(own_traces, dom_send[0], axis=1), jnp.take(own_traces, dom_send[1], axis=1)]
    )
    sub_out = jnp.take(own_traces, sub_send.reshape(-1), axis=1).reshape(n_chan, n_sub, sub_width)
    sub_in = lax.all_to_all(sub_out, "sub", split_axis=1, concat_axis=1, tiled=True).reshape(
        n_chan, n_sub * sub_width
    )
    from_below = from_behind(dom_out[1], "dom", 1)
    from_above = from_behind(dom_out[0], "dom", -1)
    return jnp.concatenate([own_traces, from_below, from_above, sub_in], axis=1)


def body(
    start_dofs,
    inv_jac,
    normals,
    bulk_modulus,
    density,
    deriv_mats,
    face_proj,
    face_lift,
    cluster,
    pml_flags,
    neighbours,
    dom_send,
    sub_send,
):
    n_elem = start_dofs.shape[1]
    dofs_zero = start_dofs.reshape(NQ, NB, n_elem)
    damping = sigma_pml * pml_flags.astype(jnp.float32)
    fine_mask = cluster == 1
    material = (inv_jac, bulk_modulus, density, damping, deriv_mats)
    coarse_terms = taylor(dofs_zero, material)
    sub_dt = step_size / SUBSTEPS
    head_material = (inv_jac, bulk_modulus, density, damping, deriv_mats)
    work_state = jnp.where(fine_mask, dofs_zero, 0.0)
    for sub_step in range(SUBSTEPS):
        coarse_part = integrate(coarse_terms, sub_step * sub_dt, (sub_step + 1) * sub_dt)
        work_head = work_state
        fine_part = integrate(taylor(work_head, head_material), 0.0, sub_dt)
        published = jnp.where(fine_mask, fine_part, coarse_part)
        own_traces = face_traces(published, face_proj)
        trace_pool = gather_faces(own_traces, dom_send, sub_send)
        nbr_traces = jnp.take(trace_pool, neighbours.reshape(-1), axis=1)
        lifted = corrections(own_traces, nbr_traces, normals, bulk_modulus, density, face_lift)
        coarse_next = work_state + lifted
        stepped = work_head + apply_operator(fine_part, head_material) - lifted
        head_next = jnp.where(fine_mask, stepped, coarse_next)
        work_state = head_next
    full_step = integrate(coarse_terms, 0.0, step_size)
    coarse_out = dofs_zero + apply_operator(full_step, material) - work_state
    return jnp.where(fine_mask, work_state, coarse_out).reshape(NQ * NB, n_elem)


def solution(mesh):
    in_specs = (
        P(None, ("dom", "sub")),
        P(None, ("dom", "sub")),
        P(None, ("dom", "sub")),
        P(("dom", "sub")),
        P(("dom", "sub")),
        P(),
        P(),
        P(),
        P(("dom", "sub")),
        P(("dom", "sub")),
        P(None, ("dom", "sub")),
        P(("dom", "sub"), None),
        P(("dom", "sub"), None),
    )
    out_specs = P(None, ("dom", "sub"))
    return jax.shard_map(body, mesh=mesh, in_specs=in_specs, out_specs=out_specs, check_vma=False)
```

profile of v0, /device:TPU:11, one launch (start us, length us, event | category | flops | bytes accessed | tf_op | source)
XLA Modules:
  0.0 125.4 jit_solution(3070285738189939827)
XLA Ops:
  0.0 0.8 reshape.421
  0.8 0.9 reshape.662
  1.7 0.9 slice.126
  2.9 0.6 copy-done.33
  3.7 0.6 copy-done.4
  4.3 0.6 divide_sqrt_fusion
  5.0 0.6 copy-done.2
  7.1 0.8 slice-done
  9.3 0.7 copy-done.13
  10.8 0.8 multiply_reduce_fusion.1
  15.3 0.6 gather_fusion.2
  16.0 0.7 reshape.663
  16.8 4.9 %all-to-all-start = ((f32[4,1,1920]{2,1,0:T(1,128)}), f32[4,1,1920]{2,1,0:T(1,128)S(1)}, u32[]{:S(2)}, u32[]{:S(2)}) async-start(f32[4,1,1920]{2,1,0:T(1,128)} %reshape.663), calls=%async_computation | async-start | bytes 61440 | tf_op jit(solution)/shard_map/all_to_all | solution.py:90
  21.7 0.7 copy-done.29
  22.4 0.6 gather_fusion
  23.1 4.2 %collective-permute-start = (f32[60,96]{0,1:T(8,128)S(1)}, f32[60,96]{0,1:T(8,128)S(1)}, u32[]{:S(2)}, u32[]{:S(2)}) collective-permute-start(f32[60,96]{0,1:T(8,128)S(1)} %select_bitcast_fusion.7), channel_id=1, source_target_pairs={{0,4},{4,8},{8,12},{12,16},{16,20},{20,24},{24,28},{1,5},{5,9},{9,... | collective-permute-start | bytes 69128 | tf_op jit(solution)/shard_map/ppermute | solution.py:22
  27.3 0.6 gather_fusion.1
  28.0 0.7 select_bitcast_fusion.6
  28.7 1.9 %collective-permute-start.1 = (f32[60,96]{0,1:T(8,128)}, f32[60,96]{0,1:T(8,128)}, u32[]{:S(2)}, u32[]{:S(2)}) collective-permute-start(f32[60,96]{0,1:T(8,128)} %select_bitcast_fusion.6), channel_id=1, source_target_pairs={{4,0},{8,4},{12,8},{16,12},{20,16},{24,20},{28,24},{5,1},{9,5},{13... | collective-permute-start | bytes 69128 | tf_op jit(solution)/shard_map/ppermute | solution.py:22
  30.9 0.7 copy-done.19
  32.5 0.6 copy-done.30
  33.2 2.1 %collective-permute-done.1 = f32[60,96]{0,1:T(8,128)} collective-permute-done((f32[60,96]{0,1:T(8,128)}, f32[60,96]{0,1:T(8,128)}, u32[]{:S(2)}, u32[]{:S(2)}) %collective-permute-start.1) | collective-permute-done | bytes 23072 | tf_op jit(solution)/shard_map/ppermute | solution.py:22
  35.3 0.8 constant_dynamic-update-slice_fusion.1
  36.1 0.5 broadcast.471
  36.6 0.6 reduce
  37.4 2.8 %gather_fusion.3 = f32[1024,60]{1,0:T(8,128)S(1)} fusion(f32[60,1344]{0,1:T(8,128)S(1)} %constant_dynamic-update-slice_fusion, s32[1024]{0:T(1024)S(1)} %get-tuple-element.102), kind=kCustom, calls=%fused_computation.2.clone | custom fusion | bytes 495616 | tf_op jit(solution)/shard_map/jit(_take)/gather | solution.py:129
  41.0 0.7 copy-done.5
  46.6 0.7 gather_fusion.5
  47.4 0.7 gather_fusion.4
  48.1 0.8 gather_fusion.6
  49.4 0.6 copy-done.28
  50.1 0.7 reshape.665
  50.9 4.5 %all-to-all-start.1 = ((f32[4,1,1920]{2,1,0:T(1,128)}), f32[4,1,1920]{2,1,0:T(1,128)S(1)}, u32[]{:S(2)}, u32[]{:S(2)}) async-start(f32[4,1,1920]{2,1,0:T(1,128)} %reshape.665), calls=%async_computation.1 | async-start | bytes 61440 | tf_op jit(solution)/shard_map/all_to_all | solution.py:90
  55.4 3.0 %collective-permute-start.2 = (f32[60,96]{0,1:T(8,128)S(1)}, f32[60,96]{0,1:T(8,128)S(1)}, u32[]{:S(2)}, u32[]{:S(2)}) collective-permute-start(f32[60,96]{0,1:T(8,128)S(1)} %select_bitcast_fusion.5), channel_id=1, source_target_pairs={{0,4},{4,8},{8,12},{12,16},{16,20},{20,24},{24,28},{1,5},{5,9},{9,... | collective-permute-start | bytes 69128 | tf_op jit(solution)/shard_map/ppermute | solution.py:22
  58.4 1.9 %collective-permute-start.3 = (f32[60,96]{0,1:T(8,128)S(1)}, f32[60,96]{0,1:T(8,128)S(1)}, u32[]{:S(2)}, u32[]{:S(2)}) collective-permute-start(f32[60,96]{0,1:T(8,128)S(1)} %select_bitcast_fusion.4), channel_id=1, source_target_pairs={{4,0},{8,4},{12,8},{16,12},{20,16},{24,20},{28,24},{5,1},{9,5},{13... | collective-permute-start | bytes 69128 | tf_op jit(solution)/shard_map/ppermute | solution.py:22
  60.4 4.3 %collective-permute-done.3 = f32[60,96]{0,1:T(8,128)S(1)} collective-permute-done((f32[60,96]{0,1:T(8,128)S(1)}, f32[60,96]{0,1:T(8,128)S(1)}, u32[]{:S(2)}, u32[]{:S(2)}) %collective-permute-start.3) | collective-permute-done | bytes 23072 | tf_op jit(solution)/shard_map/ppermute | solution.py:22
  64.7 0.6 reduce.1
  65.5 2.8 %gather_fusion.7 = f32[1024,60]{1,0:T(8,128)S(1)} fusion(f32[60,1344]{0,1:T(8,128)S(1)} %constant_dynamic-update-slice_fusion.7, s32[1024]{0:T(1024)S(1)} %get-tuple-element.102), kind=kCustom, calls=%fused_computation.13.clone | custom fusion | bytes 495616 | tf_op jit(solution)/shard_map/jit(_take)/gather | solution.py:129
  74.1 0.7 gather_fusion.9
  74.8 0.7 gather_fusion.8
  75.6 0.8 gather_fusion.10
  76.7 0.5 copy-done.23
  77.5 0.7 reshape.667
  78.3 4.5 %all-to-all-start.2 = ((f32[4,1,1920]{2,1,0:T(1,128)}), f32[4,1,1920]{2,1,0:T(1,128)S(1)}, u32[]{:S(2)}, u32[]{:S(2)}) async-start(f32[4,1,1920]{2,1,0:T(1,128)} %reshape.667), calls=%async_computation.2 | async-start | bytes 61440 | tf_op jit(solution)/shard_map/all_to_all | solution.py:90
  82.8 2.4 %collective-permute-start.4 = (f32[60,96]{0,1:T(8,128)S(1)}, f32[60,96]{0,1:T(8,128)S(1)}, u32[]{:S(2)}, u32[]{:S(2)}) collective-permute-start(f32[60,96]{0,1:T(8,128)S(1)} %select_bitcast_fusion.3), channel_id=1, source_target_pairs={{0,4},{4,8},{8,12},{12,16},{16,20},{20,24},{24,28},{1,5},{5,9},{9,... | collective-permute-start | bytes 69128 | tf_op jit(solution)/shard_map/ppermute | solution.py:22
  85.3 1.9 %collective-permute-start.5 = (f32[60,96]{0,1:T(8,128)S(1)}, f32[60,96]{0,1:T(8,128)S(1)}, u32[]{:S(2)}, u32[]{:S(2)}) collective-permute-start(f32[60,96]{0,1:T(8,128)S(1)} %select_bitcast_fusion.2), channel_id=1, source_target_pairs={{4,0},{8,4},{12,8},{16,12},{20,16},{24,20},{28,24},{5,1},{9,5},{13... | collective-permute-start | bytes 69128 | tf_op jit(solution)/shard_map/ppermute | solution.py:22
  87.3 4.3 %collective-permute-done.5 = f32[60,96]{0,1:T(8,128)S(1)} collective-permute-done((f32[60,96]{0,1:T(8,128)S(1)}, f32[60,96]{0,1:T(8,128)S(1)}, u32[]{:S(2)}, u32[]{:S(2)}) %collective-permute-start.5) | collective-permute-done | bytes 23072 | tf_op jit(solution)/shard_map/ppermute | solution.py:22
  91.6 0.6 reduce.2
  92.4 2.8 %gather_fusion.11 = f32[1024,60]{1,0:T(8,128)S(1)} fusion(f32[60,1344]{0,1:T(8,128)S(1)} %constant_dynamic-update-slice_fusion.14, s32[1024]{0:T(1024)S(1)} %get-tuple-element.102), kind=kCustom, calls=%fused_computation.14.clone | custom fusion | bytes 495616 | tf_op jit(solution)/shard_map/jit(_take)/gather | solution.py:129
  95.9 0.7 copy-done.15
  99.7 0.5 copy-done.12
  100.4 0.5 copy-done.10
  101.1 0.5 copy-done.8
  103.1 0.7 gather_fusion.13
  103.8 0.7 gather_fusion.12
  104.5 0.8 gather_fusion.14
  106.0 0.7 reshape.669
  106.7 4.5 %all-to-all-start.3 = ((f32[4,1,1920]{2,1,0:T(1,128)}), f32[4,1,1920]{2,1,0:T(1,128)S(1)}, u32[]{:S(2)}, u32[]{:S(2)}) async-start(f32[4,1,1920]{2,1,0:T(1,128)} %reshape.669), calls=%async_computation.3 | async-start | bytes 61440 | tf_op jit(solution)/shard_map/all_to_all | solution.py:90
  111.3 2.4 %collective-permute-start.6 = (f32[60,96]{0,1:T(8,128)S(1)}, f32[60,96]{0,1:T(8,128)S(1)}, u32[]{:S(2)}, u32[]{:S(2)}) collective-permute-start(f32[60,96]{0,1:T(8,128)S(1)} %select_bitcast_fusion.1), channel_id=1, source_target_pairs={{0,4},{4,8},{8,12},{12,16},{16,20},{20,24},{24,28},{1,5},{5,9},{9,... | collective-permute-start | bytes 69128 | tf_op jit(solution)/shard_map/ppermute | solution.py:22
  113.7 1.9 %collective-permute-start.7 = (f32[60,96]{0,1:T(8,128)S(1)}, f32[60,96]{0,1:T(8,128)S(1)}, u32[]{:S(2)}, u32[]{:S(2)}) collective-permute-start(f32[60,96]{0,1:T(8,128)S(1)} %select_bitcast_fusion), channel_id=1, source_target_pairs={{4,0},{8,4},{12,8},{16,12},{20,16},{24,20},{28,24},{5,1},{9,5},{13... | collective-permute-start | bytes 69128 | tf_op jit(solution)/shard_map/ppermute | solution.py:22
  115.7 4.3 %collective-permute-done.7 = f32[60,96]{0,1:T(8,128)S(1)} collective-permute-done((f32[60,96]{0,1:T(8,128)S(1)}, f32[60,96]{0,1:T(8,128)S(1)}, u32[]{:S(2)}, u32[]{:S(2)}) %collective-permute-start.7) | collective-permute-done | bytes 23072 | tf_op jit(solution)/shard_map/ppermute | solution.py:22
  120.0 0.6 reduce.3
  120.8 2.8 %gather_fusion.15 = f32[1024,60]{1,0:T(8,128)S(1)} fusion(f32[60,1344]{0,1:T(8,128)S(1)} %constant_dynamic-update-slice_fusion.21, s32[1024]{0:T(1024)S(1)} %get-tuple-element.102), kind=kCustom, calls=%fused_computation.15.clone | custom fusion | bytes 495616 | tf_op jit(solution)/shard_map/jit(_take)/gather | solution.py:129
  124.7 0.7 reshape.447
  (368 shorter events, 28.5 us)
Async XLA Ops:
  0.8 15.2 %copy-start.27 = (pred[128]{0:T(512)(128)(4,1)}, pred[128]{0:T(512)(128)(4,1)S(1)}, u32[]{:S(2)}) copy-start(pred[128]{0:T(512)(128)(4,1)S(1)} %compare_and_fusion.1) | copy-start | bytes 388
  0.8 1.8 %copy-start.1 = (f32[140,256]{1,0:T(8,128)S(1)}, f32[140,256]{1,0:T(8,128)}, u32[]{:S(2)}) copy-start(f32[140,256]{1,0:T(8,128)} %param.19) | copy-start | bytes 430084
  1.7 0.9 copy-start
  2.9 0.7 copy-start.33
  2.9 0.7 copy-start.18
  3.6 0.7 copy-start.4
  3.6 0.7 copy-start.14
  3.7 0.7 copy-start.32
  5.0 0.7 copy-start.2
  7.0 0.9 slice-start
  9.3 0.8 copy-start.13
  9.3 0.9 copy-start.3
  10.0 5.2 %copy-start.25 = (s32[1024]{0:T(1024)}, s32[1024]{0:T(1024)S(1)}, u32[]{:S(2)}) copy-start(s32[1024]{0:T(1024)S(1)} %pad_clamp_fusion) | copy-start | bytes 12292
  10.1 62.1 %copy-start.11 = (f32[1,15,35]{2,0,1:T(1,128)}, f32[1,15,35]{2,0,1:T(1,128)S(1)}, u32[]{:S(2)}) copy-start(f32[1,15,35]{2,0,1:T(1,128)S(1)} %get-tuple-element.91) | copy-start | bytes 6304
  10.1 62.3 %copy-start.9 = (f32[1,15,35]{2,0,1:T(1,128)}, f32[1,15,35]{2,0,1:T(1,128)S(1)}, u32[]{:S(2)}) copy-start(f32[1,15,35]{2,0,1:T(1,128)S(1)} %get-tuple-element.92) | copy-start | bytes 6304
  10.1 62.5 %copy-start.7 = (f32[1,15,35]{2,0,1:T(1,128)}, f32[1,15,35]{2,0,1:T(1,128)S(1)}, u32[]{:S(2)}) copy-start(f32[1,15,35]{2,0,1:T(1,128)S(1)} %get-tuple-element.93) | copy-start | bytes 6304
  16.8 4.9 %copy-start.31 = (s32[2,96]{1,0:T(2,128)S(1)}, s32[2,96]{1,0:T(2,128)}, u32[]{:S(2)}) copy-start(s32[2,96]{1,0:T(2,128)} %param.30) | copy-start | bytes 2308
  16.8 19.3 %all-to-all-start = ((f32[4,1,1920]{2,1,0:T(1,128)}), f32[4,1,1920]{2,1,0:T(1,128)S(1)}, u32[]{:S(2)}, u32[]{:S(2)}) async-start(f32[4,1,1920]{2,1,0:T(1,128)} %reshape.663), calls=%async_computation | async-start | bytes 61440 | tf_op jit(solution)/shard_map/all_to_all | solution.py:90
  21.6 0.7 copy-start.29
  21.7 27.6 %copy-start.22 = (pred[96]{0:T(512)(128)(4,1)}, pred[96]{0:T(512)(128)(4,1)S(1)}, u32[]{:S(2)}) copy-start(pred[96]{0:T(512)(128)(4,1)S(1)} %get-tuple-element.59) | copy-start | bytes 292
  21.7 29.1 %copy-start.20 = (pred[96]{0:T(512)(128)(4,1)}, pred[96]{0:T(512)(128)(4,1)S(1)}, u32[]{:S(2)}) copy-start(pred[96]{0:T(512)(128)(4,1)S(1)} %get-tuple-element.98) | copy-start | bytes 292
  22.3 0.6 copy-start.24
  23.1 10.1 %collective-permute-start = (f32[60,96]{0,1:T(8,128)S(1)}, f32[60,96]{0,1:T(8,128)S(1)}, u32[]{:S(2)}, u32[]{:S(2)}) collective-permute-start(f32[60,96]{0,1:T(8,128)S(1)} %select_bitcast_fusion.7), channel_id=1, source_target_pairs={{0,4},{4,8},{8,12},{12,16},{16,20},{20,24},{24,28},{1,5},{5,9},{9,... | collective-permute-start | bytes 69128 | tf_op jit(solution)/shard_map/ppermute | solution.py:22
  27.3 0.6 copy-start.26
  28.7 6.6 %collective-permute-start.1 = (f32[60,96]{0,1:T(8,128)}, f32[60,96]{0,1:T(8,128)}, u32[]{:S(2)}, u32[]{:S(2)}) collective-permute-start(f32[60,96]{0,1:T(8,128)} %select_bitcast_fusion.6), channel_id=1, source_target_pairs={{4,0},{8,4},{12,8},{16,12},{20,16},{24,20},{28,24},{5,1},{9,5},{13... | collective-permute-start | bytes 69128 | tf_op jit(solution)/shard_map/ppermute | solution.py:22
  30.6 9.6 %copy-start.16 = (pred[1024]{0:T(1024)(128)(4,1)}, pred[1024]{0:T(1024)(128)(4,1)S(1)}, u32[]{:S(2)}) copy-start(pred[1024]{0:T(1024)(128)(4,1)S(1)} %compare_and_fusion) | copy-start | bytes 3076
  30.9 0.7 copy-start.19
  30.9 0.9 copy-start.6
  32.5 0.6 copy-start.30
  40.9 0.8 copy-start.5
  49.3 0.7 copy-start.28
  50.9 13.9 %all-to-all-start.1 = ((f32[4,1,1920]{2,1,0:T(1,128)}), f32[4,1,1920]{2,1,0:T(1,128)S(1)}, u32[]{:S(2)}, u32[]{:S(2)}) async-start(f32[4,1,1920]{2,1,0:T(1,128)} %reshape.665), calls=%async_computation.1 | async-start | bytes 61440 | tf_op jit(solution)/shard_map/all_to_all | solution.py:90
  55.4 5.0 %collective-permute-start.2 = (f32[60,96]{0,1:T(8,128)S(1)}, f32[60,96]{0,1:T(8,128)S(1)}, u32[]{:S(2)}, u32[]{:S(2)}) collective-permute-start(f32[60,96]{0,1:T(8,128)S(1)} %select_bitcast_fusion.5), channel_id=1, source_target_pairs={{0,4},{4,8},{8,12},{12,16},{16,20},{20,24},{24,28},{1,5},{5,9},{9,... | collective-permute-start | bytes 69128 | tf_op jit(solution)/shard_map/ppermute | solution.py:22
  58.4 6.3 %collective-permute-start.3 = (f32[60,96]{0,1:T(8,128)S(1)}, f32[60,96]{0,1:T(8,128)S(1)}, u32[]{:S(2)}, u32[]{:S(2)}) collective-permute-start(f32[60,96]{0,1:T(8,128)S(1)} %select_bitcast_fusion.4), channel_id=1, source_target_pairs={{4,0},{8,4},{12,8},{16,12},{20,16},{24,20},{28,24},{5,1},{9,5},{13... | collective-permute-start | bytes 69128 | tf_op jit(solution)/shard_map/ppermute | solution.py:22
  65.5 2.8 %copy-start.17 = (pred[1024]{0:T(1024)(128)(4,1)S(1)}, pred[1024]{0:T(1024)(128)(4,1)}, u32[]{:S(2)}) copy-start(pred[1024]{0:T(1024)(128)(4,1)} %copy-done.16) | copy-start | bytes 3076
  76.7 0.6 copy-start.23
  77.4 0.8 copy-start.21
  78.3 13.3 %all-to-all-start.2 = ((f32[4,1,1920]{2,1,0:T(1,128)}), f32[4,1,1920]{2,1,0:T(1,128)S(1)}, u32[]{:S(2)}, u32[]{:S(2)}) async-start(f32[4,1,1920]{2,1,0:T(1,128)} %reshape.667), calls=%async_computation.2 | async-start | bytes 61440 | tf_op jit(solution)/shard_map/all_to_all | solution.py:90
  82.8 4.4 %collective-permute-start.4 = (f32[60,96]{0,1:T(8,128)S(1)}, f32[60,96]{0,1:T(8,128)S(1)}, u32[]{:S(2)}, u32[]{:S(2)}) collective-permute-start(f32[60,96]{0,1:T(8,128)S(1)} %select_bitcast_fusion.3), channel_id=1, source_target_pairs={{0,4},{4,8},{8,12},{12,16},{16,20},{20,24},{24,28},{1,5},{5,9},{9,... | collective-permute-start | bytes 69128 | tf_op jit(solution)/shard_map/ppermute | solution.py:22
  85.3 6.3 %collective-permute-start.5 = (f32[60,96]{0,1:T(8,128)S(1)}, f32[60,96]{0,1:T(8,128)S(1)}, u32[]{:S(2)}, u32[]{:S(2)}) collective-permute-start(f32[60,96]{0,1:T(8,128)S(1)} %select_bitcast_fusion.2), channel_id=1, source_target_pairs={{4,0},{8,4},{12,8},{16,12},{20,16},{24,20},{28,24},{5,1},{9,5},{13... | collective-permute-start | bytes 69128 | tf_op jit(solution)/shard_map/ppermute | solution.py:22
  95.9 0.7 copy-start.15
  99.5 0.7 copy-start.12
  100.2 0.7 copy-start.10
  100.9 0.7 copy-start.8
  106.7 13.3 %all-to-all-start.3 = ((f32[4,1,1920]{2,1,0:T(1,128)}), f32[4,1,1920]{2,1,0:T(1,128)S(1)}, u32[]{:S(2)}, u32[]{:S(2)}) async-start(f32[4,1,1920]{2,1,0:T(1,128)} %reshape.669), calls=%async_computation.3 | async-start | bytes 61440 | tf_op jit(solution)/shard_map/all_to_all | solution.py:90
  111.3 4.4 %collective-permute-start.6 = (f32[60,96]{0,1:T(8,128)S(1)}, f32[60,96]{0,1:T(8,128)S(1)}, u32[]{:S(2)}, u32[]{:S(2)}) collective-permute-start(f32[60,96]{0,1:T(8,128)S(1)} %select_bitcast_fusion.1), channel_id=1, source_target_pairs={{0,4},{4,8},{8,12},{12,16},{16,20},{20,24},{24,28},{1,5},{5,9},{9,... | collective-permute-start | bytes 69128 | tf_op jit(solution)/shard_map/ppermute | solution.py:22
  113.7 6.3 %collective-permute-start.7 = (f32[60,96]{0,1:T(8,128)S(1)}, f32[60,96]{0,1:T(8,128)S(1)}, u32[]{:S(2)}, u32[]{:S(2)}) collective-permute-start(f32[60,96]{0,1:T(8,128)S(1)} %select_bitcast_fusion), channel_id=1, source_target_pairs={{4,0},{8,4},{12,8},{16,12},{20,16},{24,20},{28,24},{5,1},{9,5},{13... | collective-permute-start | bytes 69128 | tf_op jit(solution)/shard_map/ppermute | solution.py:22
where the time goes:
time: 127 us; the launch traced here: 125 us
  local copies, waits for them, and re-layouts  42.8 us (34%)
  starting transfers between devices  38.3 us (30%)
  matrix products  17.1 us (13%)
  waiting for transfers between devices  15 us (12%)
  other arithmetic  9.86 us (8%)
  between operations  2.36 us (2%)
    ppermute x8, starting transfers between devices, from_behind(): return lax.ppermute(shard, axis, pairs)  19.8 us
    all_to_all x4, starting transfers between devices, gather_faces(): lax.all_to_all(sub_out, 'sub', split_axis=1, concat_axis=1, tiled=True)  18.5 us
    ppermute x8, waiting for transfers between devices, from_behind(): return lax.ppermute(shard, axis, pairs)  15 us
    unnamed x105, local copies, waits for them, and re-layouts  13.5 us
    gather x4, local copies, waits for them, and re-layouts, body(): nbr_traces = jnp.take(trace_pool, neighbours.reshape(-1), axis=1)  11.3 us
    dot_general x25, matrix products, apply_operator(): jnp.dot(joined, mixed_vel.reshape(3 * n_basis, -1), precision=exact_dots)  6.34 us
    dot_general x25, matrix products, apply_operator(): jnp.dot(stacked, pressure, precision=exact_dots).reshape(3, n_basis, -1)  5.99 us
    dot_general x16, matrix products, face_traces(): jnp.einsum('kb,qbe->kqe', face_proj[face_idx], coeffs, precision=exact_dots)  3.34 us
  transfers between devices with their start and end apart: 12, of which 4 were waited for; matrix products, arithmetic and copies ran while one was open for 3% of the time, Pallas kernels for 0%

commit v1 on v0

v1 whole, which is shorter than its diff:
```python
import math

import jax
import jax.numpy as jnp
from jax import lax
from jax.experimental import pallas as pl
from jax.experimental.pallas import tpu as pltpu
from jax.sharding import PartitionSpec as P

NQ = 4
NB = 35
NF = 15
ORDER = 5
SUBSTEPS = 4
BR = 40
KR = 16
LANES = 128

step_size = 0.8
sigma_pml = 1.5
f32 = jnp.float32
bf16 = jnp.bfloat16


def weights(start_time, end_time):
    return [
        (end_time ** (k + 1) - start_time ** (k + 1)) / math.factorial(k + 1)
        for k in range(ORDER)
    ]


SUB_DT = step_size / SUBSTEPS


def hi_lo(x):
    hi = x.astype(bf16).astype(f32)
    return hi, x - hi


def split3(x):
    hi, lo = hi_lo(x)
    parts = [hi, lo, hi]
    pad = -3 * x.shape[0] % LANES
    if pad:
        parts.append(jnp.zeros((pad, x.shape[1]), f32))
    return jnp.concatenate(parts, axis=0).astype(bf16)


def mm(a, b):
    return jnp.dot(a, b, preferred_element_type=f32)


def apply_l(x, jac, ld, dj, width):
    part = [x[:, q * width:(q + 1) * width] for q in range(NQ)]
    damp = jac[18:19]
    d_press = mm(ld, split3(part[0]))
    mixed = []
    for r in range(3):
        w = jac[3 * r:3 * r + 1] * part[1]
        for d in range(1, 3):
            w = w + jac[3 * r + d:3 * r + d + 1] * part[1 + d]
        mixed.append(split3(w))
    diverg = mm(dj, jnp.concatenate(mixed, axis=0))[:BR]
    rates = [diverg - damp * part[0]]
    for d in range(3):
        g = jac[9 + d:10 + d] * d_press[:BR]
        for r in range(1, 3):
            g = g + jac[9 + 3 * r + d:10 + 3 * r + d] * d_press[r * BR:(r + 1) * BR]
        rates.append(g - damp * part[1 + d])
    return jnp.concatenate(rates, axis=1)


def combine(terms, start_time, end_time):
    total = None
    for w, t in zip(weights(start_time, end_time), terms):
        total = w * t if total is None else total + w * t
    return total


def traces(x, pf, width):
    t = mm(pf, split3(x))
    cols = []
    for f in range(4):
        rows = [t[f * KR:(f + 1) * KR, q * width:(q + 1) * width] for q in range(NQ)]
        cols.append(jnp.concatenate(rows, axis=0))
    return cols


def gather(x, onehot):
    hi, lo = hi_lo(x)
    out = mm(jnp.concatenate([hi, lo], axis=0).astype(bf16), onehot)
    n = x.shape[0]
    return out[:n] + out[n:]


def lift(jumps, coef, lf, width, stride):
    flux = [[] for _ in range(NQ)]
    for f in range(4):
        c = coef[:, f * stride:f * stride + width]
        jp = jumps[f][:KR]
        ju = [jumps[f][(1 + d) * KR:(2 + d) * KR] for d in range(3)]
        lam = c[6:7]
        g = c[0:1] * ju[0]
        for d in range(1, 3):
            g = g + c[d:d + 1] * ju[d]
        flux[0].append(g - lam * jp)
        for d in range(3):
            flux[1 + d].append(c[3 + d:4 + d] * jp - lam * ju[d])
    cat = jnp.concatenate([jnp.concatenate(fl, axis=0) for fl in flux], axis=1)
    return mm(lf, split3(cat))[:BR]


def send_parts(sent, sub_id):
    sub = sent[:, 2 * LANES:]
    lane = lax.broadcasted_iota(jnp.int32, sub.shape, 1) // 32
    mine = lane == sub_id
    even = sub_id % 2 == 0
    r32 = pltpu.roll(sub, 32, 1)
    r96 = pltpu.roll(sub, 96, 1)
    zero = jnp.zeros_like(sub)
    return (
        sent[:, :LANES],
        sent[:, LANES:2 * LANES],
        jnp.where(mine, jnp.where(even, r96, r32), zero),
        jnp.where(mine, pltpu.roll(sub, 64, 1), zero),
        jnp.where(mine, jnp.where(even, r32, r96), zero),
        jnp.where(mine, sub, zero),
    )


def write_parts(refs, sent, sub_id):
    for ref, part in zip(refs, send_parts(sent, sub_id)):
        ref[...] = part


def received(refs, dom_id, n_dom):
    a, w, s1, s2, s3, own = [r[...] for r in refs]
    inner = jnp.logical_and(dom_id > 0, dom_id < n_dom - 1)
    w = jnp.where(inner, w, jnp.zeros_like(w))
    return jnp.concatenate([a, w, (s1 + s2) + (s3 + own)], axis=1)


def first_kernel(n_elem,
                 ids, start, inv_jac, normals, bulk, density, deriv, proj, liftm, cluster, pml,
                 dom_send, sub_send,
                 o_ld, o_dj, o_pf, o_lf, o_coef, o_jac, o_soh, o_x, o_p0, o_c1, o_c2, o_cs,
                 o_t0, m_a, m_w, m_1, m_2, m_3, m_own,
                 pad, lists):
    dom_id, sub_id = ids[0], ids[1]
    pad[...] = jnp.zeros_like(pad)
    for r in range(3):
        pad[r * BR:r * BR + NB, :NB] = deriv[r]
    hi, lo = hi_lo(pad[:3 * BR])
    left = hi + pltpu.roll(hi, BR, 1) + pltpu.roll(lo, 2 * BR, 1)
    zero8 = jnp.zeros((8, LANES), f32)
    ld = jnp.concatenate([left, zero8], axis=0).astype(bf16)
    dj = jnp.concatenate(
        [jnp.concatenate([left[r * BR:(r + 1) * BR], zero8], axis=0) for r in range(3)], axis=1
    ).astype(bf16)
    pad[...] = jnp.zeros_like(pad)
    for f in range(4):
        pad[f * KR:f * KR + NF, :NB] = proj[f]
    hi, lo = hi_lo(pad[:4 * KR])
    pf = (hi + pltpu.roll(hi, BR, 1) + pltpu.roll(lo, 2 * BR, 1)).astype(bf16)
    pad[...] = jnp.zeros_like(pad)
    for f in range(4):
        pad[f * 48:f * 48 + NB, :NF] = liftm[f]
    full = pad[:48]
    for f in range(1, 4):
        full = full + pltpu.roll(pad[f * 48:(f + 1) * 48], f * KR, 1)
    hi, lo = hi_lo(full)
    lf = jnp.concatenate([hi + pltpu.roll(hi, 64, 1), lo], axis=1).astype(bf16)
    o_ld[...] = ld
    o_dj[...] = dj
    o_pf[...] = pf
    o_lf[...] = lf
    bulk_row = bulk[...].reshape(1, n_elem)
    dens_row = density[...].reshape(1, n_elem)
    fine = jnp.where(cluster[...].reshape(1, n_elem) == 1, 1.0, 0.0).astype(f32)
    damp = sigma_pml * pml[...].reshape(1, n_elem).astype(f32)
    jac_in = inv_jac[...]
    o_jac[0:9] = -bulk_row * jac_in
    o_jac[9:18] = -jac_in / dens_row
    o_jac[18:19] = damp
    o_jac[19:20] = fine
    o_jac[20:24] = jnp.zeros((4, n_elem), f32)
    speed = jnp.sqrt(bulk_row / dens_row)
    for f in range(4):
        n = normals[3 * f:3 * f + 3]
        lanes = pl.ds(f * n_elem, n_elem)
        o_coef[0:3, lanes] = 0.5 * bulk_row * n
        o_coef[3:6, lanes] = 0.5 * n / dens_row
        o_coef[6:7, lanes] = 0.5 * speed * jnp.sqrt(jnp.sum(n * n, axis=0, keepdims=True))
        o_coef[7:8, lanes] = jnp.zeros((1, n_elem), f32)
    o_x[...] = jnp.zeros_like(o_x)
    for q in range(NQ):
        o_x[:NB, q * n_elem:(q + 1) * n_elem] = start[q * NB:(q + 1) * NB]
    x = o_x[...]
    jac = o_jac[...]
    terms = [x]
    for _ in range(ORDER - 1):
        terms.append(apply_l(terms[-1], jac, ld, dj, n_elem))
    p0 = combine(terms, 0.0, SUB_DT)
    o_p0[...] = p0
    o_c1[...] = combine(terms, SUB_DT, 2 * SUB_DT)
    o_c2[...] = combine(terms, 2 * SUB_DT, 3 * SUB_DT)
    o_cs[...] = combine(terms, 0.0, step_size)
    t0 = jnp.concatenate(traces(p0, pf, n_elem), axis=1)
    o_t0[...] = t0
    lists[...] = jnp.full(lists.shape, -1, jnp.int32)
    even = dom_id % 2 == 0
    before, after = dom_send[0:1], dom_send[1:2]
    n_halo = before.shape[1]
    lists[0:1, :n_halo] = jnp.where(even, after, before)
    lists[0:1, LANES:LANES + n_halo] = jnp.where(even, before, after)
    for b in range(4):
        lists[0:1, 2 * LANES + 32 * b:2 * LANES + 32 * (b + 1)] = sub_send[b:b + 1]
    names = lists[0:1]
    n_face = 4 * n_elem
    step = 256
    for j in range(0, n_face, step):
        row = j + lax.broadcasted_iota(jnp.int32, (step, 3 * LANES), 0)
        o_soh[j:j + step] = jnp.where(row == names, 1.0, 0.0).astype(bf16)
    write_parts((m_a, m_w, m_1, m_2, m_3, m_own), gather(t0, o_soh[...]), sub_id)


def fine_base(state, pub, t, roh, coef, jac, ld, dj, lf, n_elem):
    tile = LANES
    jumps = []
    for f in range(4):
        own = t[:, f * n_elem:f * n_elem + tile]
        got = gather(t, roh[:4 * n_elem, f * n_elem:f * n_elem + tile])
        jumps.append(got - own)
    corr = lift(jumps, coef, lf, tile, n_elem)
    return state + apply_l(pub, jac, ld, dj, tile) - corr


def head(x, n_elem):
    return jnp.concatenate(
        [x[:, q * n_elem:q * n_elem + LANES] for q in range(NQ)], axis=1
    )


def table_kernel(n_elem, n_halo, ids, neighbours, roh):
    dom_id = ids[0]
    n_face = 4 * n_elem
    even = dom_id % 2 == 0
    nbr = neighbours[...]
    before_at = jnp.where(even, n_face + LANES, n_face)
    after_at = jnp.where(even, n_face, n_face + LANES)
    at = jnp.where(
        nbr < n_face,
        nbr,
        jnp.where(
            nbr < n_face + n_halo,
            nbr - n_face + before_at,
            jnp.where(
                nbr < n_face + 2 * n_halo,
                nbr - (n_face + n_halo) + after_at,
                nbr - (n_face + 2 * n_halo) + n_face + 2 * LANES,
            ),
        ),
    )
    step = 128
    for f in range(4):
        col = at[f:f + 1]
        for j in range(0, n_face + 3 * LANES, step):
            row = j + lax.broadcasted_iota(jnp.int32, (step, n_elem), 0)
            roh[j:j + step, f * n_elem:(f + 1) * n_elem] = jnp.where(row == col, 1.0, 0.0).astype(bf16)


def window0_kernel(n_elem, x, p0, c1, c2, cs, t0, roh, soh, coef, jac, ld, dj, pf, lf,
                   o_base, o_t1, o_t2, o_ts, o_s1, o_s2, o_ss):
    jac_h = jac[:, :LANES]
    o_base[...] = fine_base(head(x[...], n_elem), head(p0[...], n_elem), t0[...], roh, coef[...],
                            jac_h, ld[...], dj[...], lf[...], n_elem)
    fine = jac[19:20]
    fine4 = jnp.concatenate([fine] * 4, axis=1)
    for c, o_t, o_s in ((c1, o_t1, o_s1), (c2, o_t2, o_s2), (cs, o_ts, o_ss)):
        t = jnp.concatenate(traces(c[...], pf[...], n_elem), axis=1)
        t = jnp.where(fine4 > 0.5, 0.0, t)
        o_t[...] = t
        o_s[...] = gather(t, soh[...])


def step_kernel(n_elem, n_dom, last,
                ids, r_a, r_w, r_1, r_2, r_3, r_own, base, p_sum, t_coarse, s_coarse,
                roh, soh, coef, jac, ld, dj, pf, lf,
                o_state, o_pub, o_sum, o_t, m_a, m_w, m_1, m_2, m_3, m_own):
    dom_id, sub_id = ids[0], ids[1]
    n_face = 4 * n_elem
    tile = LANES
    got = received((r_a, r_w, r_1, r_2, r_3, r_own), dom_id, n_dom)
    jumps = [gather(got, roh[n_face:, f * n_elem:f * n_elem + tile]) for f in range(4)]
    state = base[...] - lift(jumps, coef[...], lf[...], tile, n_elem)
    jac_h = jac[:, :tile]
    terms = [state]
    for _ in range(ORDER - 1):
        terms.append(apply_l(terms[-1], jac_h, ld[...], dj[...], tile))
    pub = combine(terms, 0.0, SUB_DT)
    total = p_sum[...] + pub
    o_state[...] = state
    o_pub[...] = pub
    o_sum[...] = total
    fine = jac_h[19:20] > 0.5
    zero = jnp.zeros((4 * KR, tile), f32)
    fine_t = [jnp.where(fine, t, zero) for t in traces(total if last else pub, pf[...], tile)]
    o_t[...] = t_coarse[...]
    for f in range(4):
        o_t[:, f * n_elem:f * n_elem + tile] += fine_t[f]
    sent = s_coarse[...]
    for f in range(4):
        sent = sent + gather(fine_t[f], soh[f * n_elem:f * n_elem + tile])
    write_parts((m_a, m_w, m_1, m_2, m_3, m_own), sent, sub_id)


def window_kernel(n_elem, state, pub, t, roh, coef, jac, ld, dj, lf, o_base):
    o_base[...] = fine_base(state[...], pub[...], t[...], roh, coef[...], jac[:, :LANES], ld[...],
                            dj[...], lf[...], n_elem)


def window3_kernel(n_elem, x, cs, total, t, roh, coef, jac, ld, dj, lf, o_base):
    fine = jac[19:20, :LANES] > 0.5
    parts = []
    for q in range(NQ):
        c = cs[:, q * n_elem:(q + 1) * n_elem]
        parts.append(jnp.where(fine, total[:, q * LANES:(q + 1) * LANES], c[:, :LANES]))
        parts.append(c[:, LANES:])
    pub = jnp.concatenate(parts, axis=1)
    tv = t[...]
    jumps = []
    for f in range(4):
        lanes = slice(f * n_elem, (f + 1) * n_elem)
        jumps.append(gather(tv, roh[:4 * n_elem, lanes]) - tv[:, lanes])
    corr = lift(jumps, coef[...], lf[...], n_elem, n_elem)
    o_base[...] = x[...] + apply_l(pub, jac[...], ld[...], dj[...], n_elem) - corr


def last_kernel(n_elem, n_dom, ids, r_a, r_w, r_1, r_2, r_3, r_own, base, roh, coef, lf, out):
    n_face = 4 * n_elem
    got = received((r_a, r_w, r_1, r_2, r_3, r_own), ids[0], n_dom)
    jumps = [gather(got, roh[n_face:, f * n_elem:(f + 1) * n_elem]) for f in range(4)]
    res = base[...] - lift(jumps, coef[...], lf[...], n_elem, n_elem)
    for q in range(NQ):
        out[q * NB:(q + 1) * NB] = res[:NB, q * n_elem:(q + 1) * n_elem]


def call(kernel, name, outs, args, scratch=(), raw=(), hbm_out=False, flops=0):
    vm = pl.BlockSpec(memory_space=pltpu.VMEM)
    sm = pl.BlockSpec(memory_space=pltpu.SMEM)
    specs, ops = [], []
    for i, a in enumerate(args):
        if a.ndim == 1 and a.shape[0] == 2:
            specs.append(sm)
            ops.append(a)
        elif i in raw:
            specs.append(vm)
            ops.append(a)
        else:
            specs.append(vm)
            ops.append(pltpu.with_memory_space_constraint(a, pltpu.VMEM))
    shapes = [
        jax.ShapeDtypeStruct(s, d) if hbm_out else pltpu.VMEM(s, d) for s, d in outs
    ]
    return pl.pallas_call(
        kernel,
        in_specs=specs,
        out_specs=[vm] * len(shapes),
        out_shape=shapes,
        scratch_shapes=list(scratch),
        name=name,
        compiler_params=pltpu.CompilerParams(vmem_limit_bytes=16 << 20),
        cost_estimate=pl.CostEstimate(flops=flops, bytes_accessed=1 << 16, transcendentals=0),
    )(*ops)


def exchange(parts, n_dom):
    a, w, s1, s2, s3, own = parts
    other = [(i, ((i + 1) ^ 1) - 1 if 0 < i < n_dom - 1 else n_dom - 1 - i) for i in range(n_dom)]
    r1 = lax.ppermute(s1, "sub", [(i, i ^ 1) for i in range(4)])
    ra = lax.ppermute(a, "dom", [(i, i ^ 1) for i in range(n_dom)])
    r3 = lax.ppermute(s3, "sub", [(i, i ^ 3) for i in range(4)])
    rw = lax.ppermute(w, "dom", other)
    r2 = lax.ppermute(s2, "sub", [(i, i ^ 2) for i in range(4)])
    return ra, rw, r1, r2, r3, own


def make_body(n_dom, n_sub):
    assert n_dom % 2 == 0 and n_sub == 4

    def body(start_dofs, inv_jac, normals, bulk_modulus, density, deriv_mats, face_proj, face_lift,
             cluster, pml_flags, neighbours, dom_send, sub_send):
        n_elem = start_dofs.shape[1]
        n_halo = dom_send.shape[1]
        n_face = 4 * n_elem
        ids = jnp.stack([lax.axis_index("dom"), lax.axis_index("sub")]).astype(jnp.int32)
        wide = ((BR, NQ * n_elem), f32)
        slim = ((BR, NQ * LANES), f32)
        trace = ((4 * KR, n_face), f32)
        listed = ((4 * KR, 3 * LANES), f32)
        msg = ((4 * KR, LANES), f32)
        first = call(
            lambda *r: first_kernel(n_elem, *r), "first",
            [((128, 128), bf16), ((48, 384), bf16), ((64, 128), bf16), ((48, 256), bf16),
             ((8, n_face), f32), ((24, n_elem), f32), ((n_face, 3 * LANES), bf16)]
            + [wide] * 5 + [trace] + [msg] * 6,
            [ids, start_dofs, inv_jac, normals, bulk_modulus, density, deriv_mats, face_proj,
             face_lift, cluster, pml_flags, dom_send, sub_send],
            raw=range(13),
            scratch=[pltpu.VMEM((192, LANES), f32), pltpu.VMEM((8, 3 * LANES), jnp.int32)],
        )
        ld, dj, pf, lf, coef, jac, soh, x, p0, c1, c2, cs, t0 = first[:13]
        (roh,) = call(
            lambda *r: table_kernel(n_elem, n_halo, *r), "table",
            [((n_face + 3 * LANES, n_face), bf16)], [ids, neighbours], raw=(1,), flops=1 << 28,
        )
        got = exchange(first[13:], n_dom)
        base, t1, t2, ts, s1, s2, ss = call(
            lambda *r: window0_kernel(n_elem, *r), "window0",
            [slim] + [trace] * 3 + [listed] * 3,
            [x, p0, c1, c2, cs, t0, roh, soh, coef, jac, ld, dj, pf, lf], flops=1 << 29,
        )
        total = jnp.concatenate(
            [p0[:, q * n_elem:q * n_elem + LANES] for q in range(NQ)], axis=1
        )
        for s, (t_c, s_c) in enumerate(((t1, s1), (t2, s2), (ts, ss))):
            last = s == 2
            outs = call(
                lambda *r, last=last: step_kernel(n_elem, n_dom, last, *r), "step",
                [slim] * 3 + [trace] + [msg] * 6,
                [ids, *got, base, total, t_c, s_c, roh, soh, coef, jac, ld, dj, pf, lf],
            )
            state, pub, total, t = outs[:4]
            got = exchange(outs[4:], n_dom)
            if last:
                (base,) = call(
                    lambda *r: window3_kernel(n_elem, *r), "window3", [wide],
                    [x, cs, total, t, roh, coef, jac, ld, dj, lf], flops=1 << 29,
                )
            else:
                (base,) = call(
                    lambda *r: window_kernel(n_elem, *r), "window", [slim],
                    [state, pub, t, roh, coef, jac, ld, dj, lf], flops=1 << 28,
                )
        (out,) = call(
            lambda *r: last_kernel(n_elem, n_dom, *r), "last",
            [((NQ * NB, n_elem), f32)], [ids, *got, base, roh, coef, lf], hbm_out=True,
        )
        return out

    return body


def solution(mesh):
    in_specs = (
        P(None, ("dom", "sub")),
        P(None, ("dom", "sub")),
        P(None, ("dom", "sub")),
        P(("dom", "sub")),
        P(("dom", "sub")),
        P(),
        P(),
        P(),
        P(("dom", "sub")),
        P(("dom", "sub")),
        P(None, ("dom", "sub")),
        P(("dom", "sub"), None),
        P(("dom", "sub"), None),
    )
    out_specs = P(None, ("dom", "sub"))
    body = make_body(mesh.shape["dom"], mesh.shape["sub"])
    return jax.shard_map(body, mesh=mesh, in_specs=in_specs, out_specs=out_specs, check_vma=False)
```

time: 127 us -> 61.3 us (0.48)
  the two profiles are of different devices: /device:TPU:11 before, /device:TPU:0 now
where the time goes in v1:
time: 61.3 us; the launch traced here: 60.8 us
  starting transfers between devices  24.6 us (40%)
  Pallas kernels  15.4 us (25%)
  waiting for transfers between devices  10.9 us (18%)
  local copies, waits for them, and re-layouts  9.56 us (16%)
    pallas_call x10, Pallas kernels, call(): pl.pallas_call(kernel, in_specs=specs, out_specs=[vm] * len(shapes), out_...  15.4 us
    ppermute x4, waiting for transfers between devices, exchange(): r3 = lax.ppermute(s3, 'sub', [(i, i ^ 3) for i in range(4)])  10.6 us
    ppermute x4, starting transfers between devices, exchange(): r2 = lax.ppermute(s2, 'sub', [(i, i ^ 2) for i in range(4)])  9.66 us
    unnamed x24, local copies, waits for them, and re-layouts  9.55 us
    ppermute x4, starting transfers between devices, exchange(): rw = lax.ppermute(w, 'dom', other)  6.41 us
    ppermute x4, starting transfers between devices, exchange(): r3 = lax.ppermute(s3, 'sub', [(i, i ^ 3) for i in range(4)])  6.31 us
    ppermute x4, starting transfers between devices, exchange(): r1 = lax.ppermute(s1, 'sub', [(i, i ^ 1) for i in range(4)])  1.58 us
  transfers between devices with their start and end apart: 20, of which 6 were waited for; matrix products, arithmetic and copies ran while one was open for 0% of the time, Pallas kernels for 8%

profile of v1, /device:TPU:0, one launch (start us, length us, event | category | flops | bytes accessed | tf_op | source)
XLA Modules:
  0.0 60.8 jit_solution(6627039899746163433)
XLA Ops:
  0.0 0.9 %copy.15.r_8_ = f32[4,35,15]{2,1,0:T(8,128)S(1)} copy(f32[4,35,15]{1,0,2:T(4,128)} %param.20) | data formatting | bytes 16800 | tf_op args[7]
  0.9 0.8 %copy.14.r_7_ = f32[4,15,35]{2,1,0:T(8,128)S(1)} copy(f32[4,15,35]{2,0,1:T(4,128)} %param.19) | data formatting | bytes 16800 | tf_op args[6]
  1.6 0.1 pad_add_fusion.r_0_
  1.7 0.9 %copy-done = f32[140,256]{1,0:T(8,128)S(1)} copy-done((f32[140,256]{1,0:T(8,128)S(1)}, f32[140,256]{1,0:T(8,128)}, u32[]{:S(2)}) %copy-start) | copy-done | bytes 143384
  2.6 0.8 %copy-done.1 = f32[3,35,35]{2,1,0:T(8,128)S(1)} copy-done((f32[3,35,35]{2,1,0:T(8,128)S(1)}, f32[3,35,35]{2,1,0:T(8,128)}, u32[]{:S(2)}) %copy-start.1) | copy-done | bytes 14724
  3.4 0.7 %copy-done.2 = f32[9,256]{1,0:T(8,128)S(1)} copy-done((f32[9,256]{1,0:T(8,128)S(1)}, f32[9,256]{1,0:T(8,128)}, u32[]{:S(2)}) %copy-start.2) | copy-done | bytes 9240
  4.2 0.7 %copy-done.3 = f32[12,256]{1,0:T(8,128)S(1)} copy-done((f32[12,256]{1,0:T(8,128)S(1)}, f32[12,256]{1,0:T(8,128)}, u32[]{:S(2)}) %copy-start.3) | copy-done | bytes 12312
  4.9 0.7 %copy-done.5 = s32[4,32]{1,0:T(4,128)S(1)} copy-done((s32[4,32]{1,0:T(4,128)S(1)}, s32[4,32]{1,0:T(4,128)}, u32[]{:S(2)}) %copy-start.5) | copy-done | bytes 536
  5.6 0.7 %copy-done.6 = f32[256]{0:T(256)S(1)} copy-done((f32[256]{0:T(256)S(1)}, f32[256]{0:T(256)}, u32[]{:S(2)}) %copy-start.6) | copy-done | bytes 1048
  6.2 0.7 %copy-done.7 = f32[256]{0:T(256)S(1)} copy-done((f32[256]{0:T(256)S(1)}, f32[256]{0:T(256)}, u32[]{:S(2)}) %copy-start.7) | copy-done | bytes 1048
  6.9 0.7 %copy-done.8 = s32[256]{0:T(256)S(1)} copy-done((s32[256]{0:T(256)S(1)}, s32[256]{0:T(256)}, u32[]{:S(2)}) %copy-start.8) | copy-done | bytes 1048
  7.6 0.7 %copy-done.9 = s32[256]{0:T(256)S(1)} copy-done((s32[256]{0:T(256)S(1)}, s32[256]{0:T(256)}, u32[]{:S(2)}) %copy-start.9) | copy-done | bytes 1048
  8.3 0.7 %copy-done.10 = s32[2,96]{1,0:T(2,128)S(1)} copy-done((s32[2,96]{1,0:T(2,128)S(1)}, s32[2,96]{1,0:T(2,128)}, u32[]{:S(2)}) %copy-start.10) | copy-done | bytes 792
  9.0 2.0 %first.1 = (bf16[128,128]{1,0:T(8,128)(2,1)S(1)}, bf16[48,384]{1,0:T(8,128)(2,1)S(1)}, bf16[64,128]{1,0:T(8,128)(2,1)S(1)}, bf16[48,256]{1,0:T(8,128)(2,1)S(1)},...) custom-call(s32[2]{0:T(128)S(1)} %pad_add_fusion.r_0_, ...), custom_call_target="tpu_custom_call" | custom-call | bytes 65536 | tf_op jit(solution)/shard_map/first/pallas_call | solution.py:365
  11.0 0.5 collective-permute-start
  11.5 3.6 %collective-permute-start.1 = (f32[64,128]{1,0:T(8,128)S(1)}, f32[64,128]{1,0:T(8,128)S(1)}, u32[]{:S(2)}, u32[]{:S(2)}) collective-permute-start(f32[64,128]{1,0:T(8,128)S(1)} %get-tuple-element.60), channel_id=1, source_target_pairs={{0,28},{4,8},{8,4},{12,16},{16,12},{20,24},{24,20},{28,0},{1,29},{... | collective-permute-start | bytes 98312 | tf_op jit(solution)/shard_map/ppermute | solution.py:383
  15.0 1.6 %collective-permute-start.2 = (f32[64,128]{1,0:T(8,128)S(1)}, f32[64,128]{1,0:T(8,128)S(1)}, u32[]{:S(2)}, u32[]{:S(2)}) collective-permute-start(f32[64,128]{1,0:T(8,128)S(1)} %get-tuple-element.61), channel_id=1, source_target_pairs={{0,1},{1,0},{2,3},{3,2},{4,5},{5,4},{6,7},{7,6},{8,9},{9,8},{10,11... | collective-permute-start | bytes 98312 | tf_op jit(solution)/shard_map/ppermute | solution.py:380
  16.6 2.6 %collective-permute-start.3 = (f32[64,128]{1,0:T(8,128)S(1)}, f32[64,128]{1,0:T(8,128)S(1)}, u32[]{:S(2)}, u32[]{:S(2)}) collective-permute-start(f32[64,128]{1,0:T(8,128)S(1)} %get-tuple-element.62), channel_id=1, source_target_pairs={{0,2},{1,3},{2,0},{3,1},{4,6},{5,7},{6,4},{7,5},{8,10},{9,11},{10,... | collective-permute-start | bytes 98312 | tf_op jit(solution)/shard_map/ppermute | solution.py:384
  19.2 0.2 collective-permute-start.4
  19.4 0.7 %copy-done.4 = s32[4,256]{1,0:T(4,128)S(1)} copy-done((s32[4,256]{1,0:T(4,128)S(1)}, s32[4,256]{1,0:T(4,128)}, u32[]{:S(2)}) %copy-start.4) | copy-done | bytes 4120
  20.1 1.1 %table.1.r_6_.r_11_.r_3_.r_4_.r_8_ = bf16[1408,1024]{1,0:T(8,128)(2,1)S(1)} custom-call(s32[2]{0:T(128)S(1)} %pad_add_fusion.r_0_, s32[4,256]{1,0:T(4,128)S(1)} %copy-done.4), custom_call_target="tpu_custom_call" | custom-call | flops 268435456 | bytes 65536 | tf_op jit(solution)/shard_map/table/pallas_call | solution.py:365
  21.2 1.6 %window0.1 = (f32[40,512]{1,0:T(8,128)S(1)}, f32[64,1024]{1,0:T(8,128)S(1)}, f32[64,1024]{1,0:T(8,128)S(1)}, f32[64,1024]{1,0:T(8,128)S(1)}, f32[64,384]{1,0:T(8...) custom-call(f32[40,1024]{1,0:T(8,128)S(1)} %get-tuple-element.65.r_0_, f32[40,1024]{1,0:T(8,128)S(1)} %get-tuple-element.66.r_1_, ...), custom_call_target="tpu_custom_call" | custom-call | flops 536870912 | bytes 65536 | tf_op jit(solution)/shard_map/window0/pallas_call | solution.py:365
  22.9 0.0 collective-permute-done.r_1_
  22.9 0.0 collective-permute-done.1.r_2_
  22.9 0.0 collective-permute-done.2.r_3_
  22.9 0.0 collective-permute-done.3.r_4_
  22.9 2.0 %collective-permute-done.4.r_5_ = f32[64,128]{1,0:T(8,128)S(1)} collective-permute-done((f32[64,128]{1,0:T(8,128)S(1)}, f32[64,128]{1,0:T(8,128)S(1)}, u32[]{:S(2)}, u32[]{:S(2)}) %collective-permute-start.4) | collective-permute-done | bytes 32800 | tf_op jit(solution)/shard_map/ppermute | solution.py:382
  24.9 2.1 %step.3 = (f32[40,512]{1,0:T(8,128)S(1)}, f32[40,512]{1,0:T(8,128)S(1)}, f32[40,512]{1,0:T(8,128)S(1)}, f32[64,1024]{1,0:T(8,128)S(1)}, f32[64,128]{1,0:T(8,128)...) custom-call(s32[2]{0:T(128)S(1)} %pad_add_fusion.r_0_, ...), custom_call_target="tpu_custom_call" | custom-call | bytes 65536 | tf_op jit(solution)/shard_map/step/pallas_call | solution.py:365
  27.0 0.1 collective-permute-start.5
  27.1 0.6 %collective-permute-start.6 = (f32[64,128]{1,0:T(8,128)S(1)}, f32[64,128]{1,0:T(8,128)S(1)}, u32[]{:S(2)}, u32[]{:S(2)}) collective-permute-start(f32[64,128]{1,0:T(8,128)S(1)} %get-tuple-element.82), channel_id=1, source_target_pairs={{0,28},{4,8},{8,4},{12,16},{16,12},{20,24},{24,20},{28,0},{1,29},{... | collective-permute-start | bytes 98312 | tf_op jit(solution)/shard_map/ppermute | solution.py:383
  27.8 0.0 collective-permute-start.7
  27.8 2.1 %collective-permute-start.8 = (f32[64,128]{1,0:T(8,128)S(1)}, f32[64,128]{1,0:T(8,128)S(1)}, u32[]{:S(2)}, u32[]{:S(2)}) collective-permute-start(f32[64,128]{1,0:T(8,128)S(1)} %get-tuple-element.84), channel_id=1, source_target_pairs={{0,2},{1,3},{2,0},{3,1},{4,6},{5,7},{6,4},{7,5},{8,10},{9,11},{10,... | collective-permute-start | bytes 98312 | tf_op jit(solution)/shard_map/ppermute | solution.py:384
  29.9 2.2 %collective-permute-start.9 = (f32[64,128]{1,0:T(8,128)S(1)}, f32[64,128]{1,0:T(8,128)S(1)}, u32[]{:S(2)}, u32[]{:S(2)}) collective-permute-start(f32[64,128]{1,0:T(8,128)S(1)} %get-tuple-element.85), channel_id=1, source_target_pairs={{0,3},{1,2},{2,1},{3,0},{4,7},{5,6},{6,5},{7,4},{8,11},{9,10},{10,... | collective-permute-start | bytes 98312 | tf_op jit(solution)/shard_map/ppermute | solution.py:382
  32.1 0.7 %window.2.r_7_ = f32[40,512]{1,0:T(8,128)S(1)} custom-call(f32[40,512]{1,0:T(8,128)S(1)} %get-tuple-element.87.r_0_, f32[40,512]{1,0:T(8,128)S(1)} %get-tuple-element.88.r_1_, f32[64,1024]{1,0:T(8,128)S(1)} %get-tuple-element.89.r_2_, bf16[1408,1024]{1,0:T(8,128)(2,1)S(1)} %table.1.r_6_.r_11_.r_3_.r_4_.r_8_, ...), custom_call_target="tpu_custom_call" | custom-call | flops 268435456 | bytes 65536 | tf_op jit(solution)/shard_map/window/pallas_call | solution.py:365
  32.8 0.0 collective-permute-done.5.r_1_
  32.8 0.0 collective-permute-done.6.r_2_
  32.9 0.0 collective-permute-done.7.r_3_
  32.9 0.1 collective-permute-done.8.r_4_
  32.9 2.7 %collective-permute-done.9.r_5_ = f32[64,128]{1,0:T(8,128)S(1)} collective-permute-done((f32[64,128]{1,0:T(8,128)S(1)}, f32[64,128]{1,0:T(8,128)S(1)}, u32[]{:S(2)}, u32[]{:S(2)}) %collective-permute-start.9) | collective-permute-done | bytes 32800 | tf_op jit(solution)/shard_map/ppermute | solution.py:382
  35.6 2.1 %step.4 = (f32[40,512]{1,0:T(8,128)S(1)}, f32[40,512]{1,0:T(8,128)S(1)}, f32[40,512]{1,0:T(8,128)S(1)}, f32[64,1024]{1,0:T(8,128)S(1)}, f32[64,128]{1,0:T(8,128)...) custom-call(s32[2]{0:T(128)S(1)} %pad_add_fusion.r_0_, ...), custom_call_target="tpu_custom_call" | custom-call | bytes 65536 | tf_op jit(solution)/shard_map/step/pallas_call | solution.py:365
  37.7 0.1 collective-permute-start.10
  37.8 1.6 %collective-permute-start.11 = (f32[64,128]{1,0:T(8,128)S(1)}, f32[64,128]{1,0:T(8,128)S(1)}, u32[]{:S(2)}, u32[]{:S(2)}) collective-permute-start(f32[64,128]{1,0:T(8,128)S(1)} %get-tuple-element.94), channel_id=1, source_target_pairs={{0,28},{4,8},{8,4},{12,16},{16,12},{20,24},{24,20},{28,0},{1,29},{... | collective-permute-start | bytes 98312 | tf_op jit(solution)/shard_map/ppermute | solution.py:383
  39.4 0.0 collective-permute-start.12
  39.4 2.8 %collective-permute-start.13 = (f32[64,128]{1,0:T(8,128)S(1)}, f32[64,128]{1,0:T(8,128)S(1)}, u32[]{:S(2)}, u32[]{:S(2)}) collective-permute-start(f32[64,128]{1,0:T(8,128)S(1)} %get-tuple-element.96), channel_id=1, source_target_pairs={{0,2},{1,3},{2,0},{3,1},{4,6},{5,7},{6,4},{7,5},{8,10},{9,11},{10,... | collective-permute-start | bytes 98312 | tf_op jit(solution)/shard_map/ppermute | solution.py:384
  42.1 1.6 %collective-permute-start.14 = (f32[64,128]{1,0:T(8,128)S(1)}, f32[64,128]{1,0:T(8,128)S(1)}, u32[]{:S(2)}, u32[]{:S(2)}) collective-permute-start(f32[64,128]{1,0:T(8,128)S(1)} %get-tuple-element.97), channel_id=1, source_target_pairs={{0,3},{1,2},{2,1},{3,0},{4,7},{5,6},{6,5},{7,4},{8,11},{9,10},{10,... | collective-permute-start | bytes 98312 | tf_op jit(solution)/shard_map/ppermute | solution.py:382
  43.8 0.7 %window.3.r_7_ = f32[40,512]{1,0:T(8,128)S(1)} custom-call(f32[40,512]{1,0:T(8,128)S(1)} %get-tuple-element.99.r_0_, f32[40,512]{1,0:T(8,128)S(1)} %get-tuple-element.100.r_1_, f32[64,1024]{1,0:T(8,128)S(1)} %get-tuple-element.101.r_2_, bf16[1408,1024]{1,0:T(8,128)(2,1)S(1)} %table.1.r_6_.r_11_.r_3_.r_4_.r_8_, ...), custom_call_target="tpu_custom_call" | custom-call | flops 268435456 | bytes 65536 | tf_op jit(solution)/shard_map/window/pallas_call | solution.py:365
  44.5 0.0 collective-permute-done.10.r_1_
  44.5 0.0 collective-permute-done.11.r_2_
  44.5 0.0 collective-permute-done.12.r_3_
  44.5 0.2 collective-permute-done.13.r_4_
  44.7 3.2 %collective-permute-done.14.r_5_ = f32[64,128]{1,0:T(8,128)S(1)} collective-permute-done((f32[64,128]{1,0:T(8,128)S(1)}, f32[64,128]{1,0:T(8,128)S(1)}, u32[]{:S(2)}, u32[]{:S(2)}) %collective-permute-start.14) | collective-permute-done | bytes 32800 | tf_op jit(solution)/shard_map/ppermute | solution.py:382
  47.9 2.7 %step.5 = (f32[40,512]{1,0:T(8,128)}, f32[40,512]{1,0:T(8,128)}, f32[40,512]{1,0:T(8,128)S(1)}, f32[64,1024]{1,0:T(8,128)S(1)}, f32[64,128]{1,0:T(8,128)S(1)}, /...) custom-call(s32[2]{0:T(128)S(1)} %pad_add_fusion.r_0_, ...), custom_call_target="tpu_custom_call" | custom-call | bytes 65536 | tf_op jit(solution)/shard_map/step/pallas_call | solution.py:365
  50.5 0.0 collective-permute-start.15
  50.5 0.7 %collective-permute-start.16 = (f32[64,128]{1,0:T(8,128)S(1)}, f32[64,128]{1,0:T(8,128)S(1)}, u32[]{:S(2)}, u32[]{:S(2)}) collective-permute-start(f32[64,128]{1,0:T(8,128)S(1)} %get-tuple-element.106), channel_id=1, source_target_pairs={{0,28},{4,8},{8,4},{12,16},{16,12},{20,24},{24,20},{28,0},{1,29},{... | collective-permute-start | bytes 98312 | tf_op jit(solution)/shard_map/ppermute | solution.py:383
  51.2 0.0 collective-permute-start.17
  51.2 2.2 %collective-permute-start.18 = (f32[64,128]{1,0:T(8,128)S(1)}, f32[64,128]{1,0:T(8,128)S(1)}, u32[]{:S(2)}, u32[]{:S(2)}) collective-permute-start(f32[64,128]{1,0:T(8,128)S(1)} %get-tuple-element.108), channel_id=1, source_target_pairs={{0,2},{1,3},{2,0},{3,1},{4,6},{5,7},{6,4},{7,5},{8,10},{9,11},{10,... | collective-permute-start | bytes 98312 | tf_op jit(solution)/shard_map/ppermute | solution.py:384
  53.3 2.2 %collective-permute-start.19 = (f32[64,128]{1,0:T(8,128)S(1)}, f32[64,128]{1,0:T(8,128)S(1)}, u32[]{:S(2)}, u32[]{:S(2)}) collective-permute-start(f32[64,128]{1,0:T(8,128)S(1)} %get-tuple-element.109), channel_id=1, source_target_pairs={{0,3},{1,2},{2,1},{3,0},{4,7},{5,6},{6,5},{7,4},{8,11},{9,10},{10,... | collective-permute-start | bytes 98312 | tf_op jit(solution)/shard_map/ppermute | solution.py:382
  55.6 0.7 %window3.1.r_7_ = f32[40,1024]{1,0:T(8,128)S(1)} custom-call(f32[40,1024]{1,0:T(8,128)S(1)} %get-tuple-element.65.r_0_, f32[40,1024]{1,0:T(8,128)S(1)} %get-tuple-element.69.r_4_.r_1_, f32[40,512]{1,0:T(8,128)S(1)} %get-tuple-element.111.r_2_, f32[64,1024]{1,0:T(8,128)S(1)} %get-tuple-element.112.r_3_, ...), custom_call_target="tpu_custom_call" | custom-call | flops 536870912 | bytes 65536 | tf_op jit(solution)/shard_map/window3/pallas_call | solution.py:365
  56.3 0.0 collective-permute-done.15.r_1_
  56.3 0.0 collective-permute-done.16.r_2_
  56.3 0.0 collective-permute-done.17.r_3_
  56.3 0.0 collective-permute-done.18.r_4_
  56.3 2.7 %collective-permute-done.19.r_5_ = f32[64,128]{1,0:T(8,128)S(1)} collective-permute-done((f32[64,128]{1,0:T(8,128)S(1)}, f32[64,128]{1,0:T(8,128)S(1)}, u32[]{:S(2)}, u32[]{:S(2)}) %collective-permute-start.19) | collective-permute-done | bytes 32800 | tf_op jit(solution)/shard_map/ppermute | solution.py:382
  59.0 1.7 %last.1 = f32[140,256]{1,0:T(8,128)} custom-call(s32[2]{0:T(128)S(1)} %pad_add_fusion.r_0_, f32[64,128]{1,0:T(8,128)S(1)} %collective-permute-done.15.r_1_, f32[64,128]{1,0:T(8,128)S(1)} %collective-permute-done.16.r_2_, f32[64,128]{1,0:T(8,128)S(1)} %collective-permute-done.17.r_3_, f32[64,128]{1,0:T(8,128)S(1)} %collective-permute-done.18.r_4_, ...), custom_call_target="tpu_custom_call" | custom-call | bytes 65536 | tf_op jit(solution)/shard_map/last/pallas_call | solution.py:365
  (13 shorter events, 0.0 us)
Async XLA Ops:
  1.7 0.9 %copy-start = (f32[140,256]{1,0:T(8,128)S(1)}, f32[140,256]{1,0:T(8,128)}, u32[]{:S(2)}) copy-start(f32[140,256]{1,0:T(8,128)} %r_1_.2) | copy-start | bytes 430084
  2.6 0.8 %copy-start.1 = (f32[3,35,35]{2,1,0:T(8,128)S(1)}, f32[3,35,35]{2,1,0:T(8,128)}, u32[]{:S(2)}) copy-start(f32[3,35,35]{2,1,0:T(8,128)} %r_6_.1) | copy-start | bytes 44104
  3.4 0.7 %copy-start.2 = (f32[9,256]{1,0:T(8,128)S(1)}, f32[9,256]{1,0:T(8,128)}, u32[]{:S(2)}) copy-start(f32[9,256]{1,0:T(8,128)} %r_2_.1) | copy-start | bytes 27652
  4.2 0.7 %copy-start.3 = (f32[12,256]{1,0:T(8,128)S(1)}, f32[12,256]{1,0:T(8,128)}, u32[]{:S(2)}) copy-start(f32[12,256]{1,0:T(8,128)} %r_3_.1) | copy-start | bytes 36868
  4.9 0.7 %copy-start.5 = (s32[4,32]{1,0:T(4,128)S(1)}, s32[4,32]{1,0:T(4,128)}, u32[]{:S(2)}) copy-start(s32[4,32]{1,0:T(4,128)} %r_12_.1) | copy-start | bytes 1540
  5.6 0.7 %copy-start.6 = (f32[256]{0:T(256)S(1)}, f32[256]{0:T(256)}, u32[]{:S(2)}) copy-start(f32[256]{0:T(256)} %r_4_.1) | copy-start | bytes 3076
  6.2 0.7 %copy-start.7 = (f32[256]{0:T(256)S(1)}, f32[256]{0:T(256)}, u32[]{:S(2)}) copy-start(f32[256]{0:T(256)} %r_5_.1) | copy-start | bytes 3076
  6.9 0.7 %copy-start.8 = (s32[256]{0:T(256)S(1)}, s32[256]{0:T(256)}, u32[]{:S(2)}) copy-start(s32[256]{0:T(256)} %r_9_.1) | copy-start | bytes 3076
  7.6 0.7 %copy-start.9 = (s32[256]{0:T(256)S(1)}, s32[256]{0:T(256)}, u32[]{:S(2)}) copy-start(s32[256]{0:T(256)} %r_10_.1) | copy-start | bytes 3076
  8.3 0.7 %copy-start.10 = (s32[2,96]{1,0:T(2,128)S(1)}, s32[2,96]{1,0:T(2,128)}, u32[]{:S(2)}) copy-start(s32[2,96]{1,0:T(2,128)} %r_11_.1) | copy-start | bytes 2308
  11.0 11.9 %collective-permute-start = (f32[64,128]{1,0:T(8,128)S(1)}, f32[64,128]{1,0:T(8,128)S(1)}, u32[]{:S(2)}, u32[]{:S(2)}) collective-permute-start(f32[64,128]{1,0:T(8,128)S(1)} %get-tuple-element.59), channel_id=1, source_target_pairs={{0,4},{4,0},{8,12},{12,8},{16,20},{20,16},{24,28},{28,24},{1,5},{5... | collective-permute-start | bytes 98312 | tf_op jit(solution)/shard_map/ppermute | solution.py:381
  11.5 11.4 %collective-permute-start.1 = (f32[64,128]{1,0:T(8,128)S(1)}, f32[64,128]{1,0:T(8,128)S(1)}, u32[]{:S(2)}, u32[]{:S(2)}) collective-permute-start(f32[64,128]{1,0:T(8,128)S(1)} %get-tuple-element.60), channel_id=1, source_target_pairs={{0,28},{4,8},{8,4},{12,16},{16,12},{20,24},{24,20},{28,0},{1,29},{... | collective-permute-start | bytes 98312 | tf_op jit(solution)/shard_map/ppermute | solution.py:383
  15.0 7.8 %collective-permute-start.2 = (f32[64,128]{1,0:T(8,128)S(1)}, f32[64,128]{1,0:T(8,128)S(1)}, u32[]{:S(2)}, u32[]{:S(2)}) collective-permute-start(f32[64,128]{1,0:T(8,128)S(1)} %get-tuple-element.61), channel_id=1, source_target_pairs={{0,1},{1,0},{2,3},{3,2},{4,5},{5,4},{6,7},{7,6},{8,9},{9,8},{10,11... | collective-permute-start | bytes 98312 | tf_op jit(solution)/shard_map/ppermute | solution.py:380
  16.6 6.3 %collective-permute-start.3 = (f32[64,128]{1,0:T(8,128)S(1)}, f32[64,128]{1,0:T(8,128)S(1)}, u32[]{:S(2)}, u32[]{:S(2)}) collective-permute-start(f32[64,128]{1,0:T(8,128)S(1)} %get-tuple-element.62), channel_id=1, source_target_pairs={{0,2},{1,3},{2,0},{3,1},{4,6},{5,7},{6,4},{7,5},{8,10},{9,11},{10,... | collective-permute-start | bytes 98312 | tf_op jit(solution)/shard_map/ppermute | solution.py:384
  19.2 5.7 %collective-permute-start.4 = (f32[64,128]{1,0:T(8,128)S(1)}, f32[64,128]{1,0:T(8,128)S(1)}, u32[]{:S(2)}, u32[]{:S(2)}) collective-permute-start(f32[64,128]{1,0:T(8,128)S(1)} %get-tuple-element.63), channel_id=1, source_target_pairs={{0,3},{1,2},{2,1},{3,0},{4,7},{5,6},{6,5},{7,4},{8,11},{9,10},{10,... | collective-permute-start | bytes 98312 | tf_op jit(solution)/shard_map/ppermute | solution.py:382
  19.4 0.7 %copy-start.4 = (s32[4,256]{1,0:T(4,128)S(1)}, s32[4,256]{1,0:T(4,128)}, u32[]{:S(2)}) copy-start(s32[4,256]{1,0:T(4,128)} %r_1_.3) | copy-start | bytes 12292
  27.0 5.8 %collective-permute-start.5 = (f32[64,128]{1,0:T(8,128)S(1)}, f32[64,128]{1,0:T(8,128)S(1)}, u32[]{:S(2)}, u32[]{:S(2)}) collective-permute-start(f32[64,128]{1,0:T(8,128)S(1)} %get-tuple-element.81), channel_id=1, source_target_pairs={{0,4},{4,0},{8,12},{12,8},{16,20},{20,16},{24,28},{28,24},{1,5},{5... | collective-permute-start | bytes 98312 | tf_op jit(solution)/shard_map/ppermute | solution.py:381
  27.1 5.7 %collective-permute-start.6 = (f32[64,128]{1,0:T(8,128)S(1)}, f32[64,128]{1,0:T(8,128)S(1)}, u32[]{:S(2)}, u32[]{:S(2)}) collective-permute-start(f32[64,128]{1,0:T(8,128)S(1)} %get-tuple-element.82), channel_id=1, source_target_pairs={{0,28},{4,8},{8,4},{12,16},{16,12},{20,24},{24,20},{28,0},{1,29},{... | collective-permute-start | bytes 98312 | tf_op jit(solution)/shard_map/ppermute | solution.py:383
  27.8 5.1 %collective-permute-start.7 = (f32[64,128]{1,0:T(8,128)S(1)}, f32[64,128]{1,0:T(8,128)S(1)}, u32[]{:S(2)}, u32[]{:S(2)}) collective-permute-start(f32[64,128]{1,0:T(8,128)S(1)} %get-tuple-element.83), channel_id=1, source_target_pairs={{0,1},{1,0},{2,3},{3,2},{4,5},{5,4},{6,7},{7,6},{8,9},{9,8},{10,11... | collective-permute-start | bytes 98312 | tf_op jit(solution)/shard_map/ppermute | solution.py:380
  27.8 5.2 %collective-permute-start.8 = (f32[64,128]{1,0:T(8,128)S(1)}, f32[64,128]{1,0:T(8,128)S(1)}, u32[]{:S(2)}, u32[]{:S(2)}) collective-permute-start(f32[64,128]{1,0:T(8,128)S(1)} %get-tuple-element.84), channel_id=1, source_target_pairs={{0,2},{1,3},{2,0},{3,1},{4,6},{5,7},{6,4},{7,5},{8,10},{9,11},{10,... | collective-permute-start | bytes 98312 | tf_op jit(solution)/shard_map/ppermute | solution.py:384
  29.9 5.7 %collective-permute-start.9 = (f32[64,128]{1,0:T(8,128)S(1)}, f32[64,128]{1,0:T(8,128)S(1)}, u32[]{:S(2)}, u32[]{:S(2)}) collective-permute-start(f32[64,128]{1,0:T(8,128)S(1)} %get-tuple-element.85), channel_id=1, source_target_pairs={{0,3},{1,2},{2,1},{3,0},{4,7},{5,6},{6,5},{7,4},{8,11},{9,10},{10,... | collective-permute-start | bytes 98312 | tf_op jit(solution)/shard_map/ppermute | solution.py:382
  37.7 6.7 %collective-permute-start.10 = (f32[64,128]{1,0:T(8,128)S(1)}, f32[64,128]{1,0:T(8,128)S(1)}, u32[]{:S(2)}, u32[]{:S(2)}) collective-permute-start(f32[64,128]{1,0:T(8,128)S(1)} %get-tuple-element.93), channel_id=1, source_target_pairs={{0,4},{4,0},{8,12},{12,8},{16,20},{20,16},{24,28},{28,24},{1,5},{5... | collective-permute-start | bytes 98312 | tf_op jit(solution)/shard_map/ppermute | solution.py:381
  37.8 6.7 %collective-permute-start.11 = (f32[64,128]{1,0:T(8,128)S(1)}, f32[64,128]{1,0:T(8,128)S(1)}, u32[]{:S(2)}, u32[]{:S(2)}) collective-permute-start(f32[64,128]{1,0:T(8,128)S(1)} %get-tuple-element.94), channel_id=1, source_target_pairs={{0,28},{4,8},{8,4},{12,16},{16,12},{20,24},{24,20},{28,0},{1,29},{... | collective-permute-start | bytes 98312 | tf_op jit(solution)/shard_map/ppermute | solution.py:383
  39.4 5.1 %collective-permute-start.12 = (f32[64,128]{1,0:T(8,128)S(1)}, f32[64,128]{1,0:T(8,128)S(1)}, u32[]{:S(2)}, u32[]{:S(2)}) collective-permute-start(f32[64,128]{1,0:T(8,128)S(1)} %get-tuple-element.95), channel_id=1, source_target_pairs={{0,1},{1,0},{2,3},{3,2},{4,5},{5,4},{6,7},{7,6},{8,9},{9,8},{10,11... | collective-permute-start | bytes 98312 | tf_op jit(solution)/shard_map/ppermute | solution.py:380
  39.4 5.3 %collective-permute-start.13 = (f32[64,128]{1,0:T(8,128)S(1)}, f32[64,128]{1,0:T(8,128)S(1)}, u32[]{:S(2)}, u32[]{:S(2)}) collective-permute-start(f32[64,128]{1,0:T(8,128)S(1)} %get-tuple-element.96), channel_id=1, source_target_pairs={{0,2},{1,3},{2,0},{3,1},{4,6},{5,7},{6,4},{7,5},{8,10},{9,11},{10,... | collective-permute-start | bytes 98312 | tf_op jit(solution)/shard_map/ppermute | solution.py:384
  42.1 5.7 %collective-permute-start.14 = (f32[64,128]{1,0:T(8,128)S(1)}, f32[64,128]{1,0:T(8,128)S(1)}, u32[]{:S(2)}, u32[]{:S(2)}) collective-permute-start(f32[64,128]{1,0:T(8,128)S(1)} %get-tuple-element.97), channel_id=1, source_target_pairs={{0,3},{1,2},{2,1},{3,0},{4,7},{5,6},{6,5},{7,4},{8,11},{9,10},{10,... | collective-permute-start | bytes 98312 | tf_op jit(solution)/shard_map/ppermute | solution.py:382
  50.5 5.8 %collective-permute-start.15 = (f32[64,128]{1,0:T(8,128)S(1)}, f32[64,128]{1,0:T(8,128)S(1)}, u32[]{:S(2)}, u32[]{:S(2)}) collective-permute-start(f32[64,128]{1,0:T(8,128)S(1)} %get-tuple-element.105), channel_id=1, source_target_pairs={{0,4},{4,0},{8,12},{12,8},{16,20},{20,16},{24,28},{28,24},{1,5},{5... | collective-permute-start | bytes 98312 | tf_op jit(solution)/shard_map/ppermute | solution.py:381
  50.5 5.8 %collective-permute-start.16 = (f32[64,128]{1,0:T(8,128)S(1)}, f32[64,128]{1,0:T(8,128)S(1)}, u32[]{:S(2)}, u32[]{:S(2)}) collective-permute-start(f32[64,128]{1,0:T(8,128)S(1)} %get-tuple-element.106), channel_id=1, source_target_pairs={{0,28},{4,8},{8,4},{12,16},{16,12},{20,24},{24,20},{28,0},{1,29},{... | collective-permute-start | bytes 98312 | tf_op jit(solution)/shard_map/ppermute | solution.py:383
  51.2 5.1 %collective-permute-start.17 = (f32[64,128]{1,0:T(8,128)S(1)}, f32[64,128]{1,0:T(8,128)S(1)}, u32[]{:S(2)}, u32[]{:S(2)}) collective-permute-start(f32[64,128]{1,0:T(8,128)S(1)} %get-tuple-element.107), channel_id=1, source_target_pairs={{0,1},{1,0},{2,3},{3,2},{4,5},{5,4},{6,7},{7,6},{8,9},{9,8},{10,11... | collective-permute-start | bytes 98312 | tf_op jit(solution)/shard_map/ppermute | solution.py:380
  51.2 5.2 %collective-permute-start.18 = (f32[64,128]{1,0:T(8,128)S(1)}, f32[64,128]{1,0:T(8,128)S(1)}, u32[]{:S(2)}, u32[]{:S(2)}) collective-permute-start(f32[64,128]{1,0:T(8,128)S(1)} %get-tuple-element.108), channel_id=1, source_target_pairs={{0,2},{1,3},{2,0},{3,1},{4,6},{5,7},{6,4},{7,5},{8,10},{9,11},{10,... | collective-permute-start | bytes 98312 | tf_op jit(solution)/shard_map/ppermute | solution.py:384
  53.3 5.7 %collective-permute-start.19 = (f32[64,128]{1,0:T(8,128)S(1)}, f32[64,128]{1,0:T(8,128)S(1)}, u32[]{:S(2)}, u32[]{:S(2)}) collective-permute-start(f32[64,128]{1,0:T(8,128)S(1)} %get-tuple-element.109), channel_id=1, source_target_pairs={{0,3},{1,2},{2,1},{3,0},{4,7},{5,6},{6,5},{7,4},{8,11},{9,10},{10,... | collective-permute-start | bytes 98312 | tf_op jit(solution)/shard_map/ppermute | solution.py:382

commit v2 on v1

--- a/solution.py
+++ b/solution.py
@@ -110,44 +110,59 @@
     return mm(lf, split3(cat))[:BR]
 
 
-def send_parts(sent, sub_id):
+def block_mask(shape, block):
+    return lax.broadcasted_iota(jnp.int32, shape, 1) // 32 == block
+
+
+def turn(x, blocks):
+    blocks %= 4
+    return pltpu.roll(x, 32 * blocks, 1) if blocks else x
+
+
+def write_parts(refs, sent):
+    m_a, m_w, m_1, m_2, m_3, m_own = refs
+    m_a[...] = sent[:, :LANES]
+    m_w[...] = sent[:, LANES:2 * LANES]
     sub = sent[:, 2 * LANES:]
-    lane = lax.broadcasted_iota(jnp.int32, sub.shape, 1) // 32
-    mine = lane == sub_id
-    even = sub_id % 2 == 0
-    r32 = pltpu.roll(sub, 32, 1)
-    r96 = pltpu.roll(sub, 96, 1)
-    zero = jnp.zeros_like(sub)
-    return (
-        sent[:, :LANES],
-        sent[:, LANES:2 * LANES],
-        jnp.where(mine, jnp.where(even, r96, r32), zero),
-        jnp.where(mine, pltpu.roll(sub, 64, 1), zero),
-        jnp.where(mine, jnp.where(even, r32, r96), zero),
-        jnp.where(mine, sub, zero),
-    )
-
-
-def write_parts(refs, sent, sub_id):
-    for ref, part in zip(refs, send_parts(sent, sub_id)):
-        ref[...] = part
+    for k, ref in ((1, m_1), (2, m_2), (3, m_3)):
+        msg = turn(sub[:KR], -k)
+        for q in range(1, NQ):
+            msg = jnp.where(block_mask(msg.shape, q), turn(sub[q * KR:(q + 1) * KR], q - k), msg)
+        ref[...] = msg
+    m_own[...] = sub
 
 
 def received(refs, dom_id, n_dom):
-    a, w, s1, s2, s3, own = [r[...] for r in refs]
+    a, w, s1, s2, s3 = [refs[TAKEN.index(i)][...] for i in range(5)]
+    own = refs[5][...]
     inner = jnp.logical_and(dom_id > 0, dom_id < n_dom - 1)
     w = jnp.where(inner, w, jnp.zeros_like(w))
-    return jnp.concatenate([a, w, (s1 + s2) + (s3 + own)], axis=1)
-
-
-def first_kernel(n_elem,
-                 ids, start, inv_jac, normals, bulk, density, deriv, proj, liftm, cluster, pml,
-                 dom_send, sub_send,
-                 o_ld, o_dj, o_pf, o_lf, o_coef, o_jac, o_soh, o_x, o_p0, o_c1, o_c2, o_cs,
-                 o_t0, m_a, m_w, m_1, m_2, m_3, m_own,
-                 pad, lists):
+    rows = []
+    for q in range(NQ):
+        row = own[q * KR:(q + 1) * KR]
+        for k, msg in ((1, s1), (2, s2), (3, s3)):
+            row = jnp.where(block_mask(row.shape, k), turn(msg, k - q), row)
+        rows.append(row)
+    return jnp.concatenate([a, w, jnp.concatenate(rows, axis=0)], axis=1)
+
+
+def first_kernel(n_elem, *refs):
+    ids, raw = refs[0], refs[1:14]
+    (o_ld, o_dj, o_pf, o_lf, o_coef, o_jac, o_soh, o_at, o_x, o_xh, o_ph, o_c1, o_c2, o_cs,
+     o_t0, m_a, m_w, m_1, m_2, m_3, m_own) = refs[14:35]
+    held, sem, pad, lists = refs[35:48], refs[48], refs[49], refs[50]
+    copies = [
+        pltpu.make_async_copy(src, dst, sem.at[i]) for i, (src, dst) in enumerate(zip(raw, held))
+    ]
+    for c in copies:
+        c.start()
+    (start, inv_jac, normals, bulk, density, deriv, proj, liftm, cluster, pml, neighbours,
+     dom_send, sub_send) = held
+    pad[...] = jnp.zeros_like(pad)
+    o_x[...] = jnp.zeros_like(o_x)
+    for c in copies:
+        c.wait()
     dom_id, sub_id = ids[0], ids[1]
-    pad[...] = jnp.zeros_like(pad)
     for r in range(3):
         pad[r * BR:r * BR + NB, :NB] = deriv[r]
     hi, lo = hi_lo(pad[:3 * BR])
@@ -159,15 +174,13 @@
     ).astype(bf16)
     pad[...] = jnp.zeros_like(pad)
     for f in range(4):
-        pad[f * KR:f * KR + NF, :NB] = proj[f]
+        pad[f * KR:f * KR + NF, :NB] = proj[:, f, :]
     hi, lo = hi_lo(pad[:4 * KR])
     pf = (hi + pltpu.roll(hi, BR, 1) + pltpu.roll(lo, 2 * BR, 1)).astype(bf16)
     pad[...] = jnp.zeros_like(pad)
     for f in range(4):
-        pad[f * 48:f * 48 + NB, :NF] = liftm[f]
-    full = pad[:48]
-    for f in range(1, 4):
-        full = full + pltpu.roll(pad[f * 48:(f + 1) * 48], f * KR, 1)
+        pad[f * KR:f * KR + NF, :NB] = liftm[:, f, :]
+    full = jnp.transpose(pad[:LANES])[:48]
     hi, lo = hi_lo(full)
     lf = jnp.concatenate([hi + pltpu.roll(hi, 64, 1), lo], axis=1).astype(bf16)
     o_ld[...] = ld
@@ -192,7 +205,6 @@
         o_coef[3:6, lanes] = 0.5 * n / dens_row
         o_coef[6:7, lanes] = 0.5 * speed * jnp.sqrt(jnp.sum(n * n, axis=0, keepdims=True))
         o_coef[7:8, lanes] = jnp.zeros((1, n_elem), f32)
-    o_x[...] = jnp.zeros_like(o_x)
     for q in range(NQ):
         o_x[:NB, q * n_elem:(q + 1) * n_elem] = start[q * NB:(q + 1) * NB]
     x = o_x[...]
@@ -201,7 +213,8 @@
     for _ in range(ORDER - 1):
         terms.append(apply_l(terms[-1], jac, ld, dj, n_elem))
     p0 = combine(terms, 0.0, SUB_DT)
-    o_p0[...] = p0
+    o_xh[...] = head(x, n_elem)
+    o_ph[...] = head(p0, n_elem)
     o_c1[...] = combine(terms, SUB_DT, 2 * SUB_DT)
     o_c2[...] = combine(terms, 2 * SUB_DT, 3 * SUB_DT)
     o_cs[...] = combine(terms, 0.0, step_size)
@@ -214,41 +227,19 @@
     lists[0:1, :n_halo] = jnp.where(even, after, before)
     lists[0:1, LANES:LANES + n_halo] = jnp.where(even, before, after)
     for b in range(4):
-        lists[0:1, 2 * LANES + 32 * b:2 * LANES + 32 * (b + 1)] = sub_send[b:b + 1]
+        lists[0:1, 2 * LANES + 32 * b:2 * LANES + 32 * (b + 1)] = sub_send[pl.ds(sub_id ^ b, 1)]
     names = lists[0:1]
     n_face = 4 * n_elem
     step = 256
     for j in range(0, n_face, step):
         row = j + lax.broadcasted_iota(jnp.int32, (step, 3 * LANES), 0)
         o_soh[j:j + step] = jnp.where(row == names, 1.0, 0.0).astype(bf16)
-    write_parts((m_a, m_w, m_1, m_2, m_3, m_own), gather(t0, o_soh[...]), sub_id)
-
-
-def fine_base(state, pub, t, roh, coef, jac, ld, dj, lf, n_elem):
-    tile = LANES
-    jumps = []
-    for f in range(4):
-        own = t[:, f * n_elem:f * n_elem + tile]
-        got = gather(t, roh[:4 * n_elem, f * n_elem:f * n_elem + tile])
-        jumps.append(got - own)
-    corr = lift(jumps, coef, lf, tile, n_elem)
-    return state + apply_l(pub, jac, ld, dj, tile) - corr
-
-
-def head(x, n_elem):
-    return jnp.concatenate(
-        [x[:, q * n_elem:q * n_elem + LANES] for q in range(NQ)], axis=1
-    )
-
-
-def table_kernel(n_elem, n_halo, ids, neighbours, roh):
-    dom_id = ids[0]
-    n_face = 4 * n_elem
-    even = dom_id % 2 == 0
+    write_parts((m_a, m_w, m_1, m_2, m_3, m_own), gather(t0, o_soh[...]))
     nbr = neighbours[...]
     before_at = jnp.where(even, n_face + LANES, n_face)
     after_at = jnp.where(even, n_face, n_face + LANES)
-    at = jnp.where(
+    slot = nbr - (n_face + 2 * n_halo)
+    o_at[...] = jnp.where(
         nbr < n_face,
         nbr,
         jnp.where(
@@ -257,41 +248,62 @@
             jnp.where(
                 nbr < n_face + 2 * n_halo,
                 nbr - (n_face + n_halo) + after_at,
-                nbr - (n_face + 2 * n_halo) + n_face + 2 * LANES,
+                n_face + 2 * LANES + 32 * ((slot >> 5) ^ sub_id) + (slot & 31),
             ),
         ),
     )
+
+
+def fine_base(state, pub, t, roh, coef, jac, ld, dj, lf, n_elem):
+    tile = LANES
+    jumps = []
+    for f in range(4):
+        own = t[:, f * n_elem:f * n_elem + tile]
+        got = gather(t, roh[:4 * n_elem, f * tile:(f + 1) * tile])
+        jumps.append(got - own)
+    corr = lift(jumps, coef, lf, tile, n_elem)
+    return state + apply_l(pub, jac, ld, dj, tile) - corr
+
+
+def head(x, n_elem):
+    return jnp.concatenate(
+        [x[:, q * n_elem:q * n_elem + LANES] for q in range(NQ)], axis=1
+    )
+
+
+def table(at, roh, n_elem, first, count):
     step = 128
     for f in range(4):
-        col = at[f:f + 1]
-        for j in range(0, n_face + 3 * LANES, step):
-            row = j + lax.broadcasted_iota(jnp.int32, (step, n_elem), 0)
-            roh[j:j + step, f * n_elem:(f + 1) * n_elem] = jnp.where(row == col, 1.0, 0.0).astype(bf16)
-
-
-def window0_kernel(n_elem, x, p0, c1, c2, cs, t0, roh, soh, coef, jac, ld, dj, pf, lf,
-                   o_base, o_t1, o_t2, o_ts, o_s1, o_s2, o_ss):
-    jac_h = jac[:, :LANES]
-    o_base[...] = fine_base(head(x[...], n_elem), head(p0[...], n_elem), t0[...], roh, coef[...],
-                            jac_h, ld[...], dj[...], lf[...], n_elem)
-    fine = jac[19:20]
-    fine4 = jnp.concatenate([fine] * 4, axis=1)
-    for c, o_t, o_s in ((c1, o_t1, o_s1), (c2, o_t2, o_s2), (cs, o_ts, o_ss)):
-        t = jnp.concatenate(traces(c[...], pf[...], n_elem), axis=1)
-        t = jnp.where(fine4 > 0.5, 0.0, t)
-        o_t[...] = t
-        o_s[...] = gather(t, soh[...])
+        col = at[f:f + 1, first:first + count]
+        for j in range(0, roh.shape[0], step):
+            row = j + lax.broadcasted_iota(jnp.int32, (step, count), 0)
+            roh[j:j + step, f * count:(f + 1) * count] = jnp.where(row == col, 1.0, 0.0).astype(bf16)
+
+
+def coarse_traces(c, soh, jac, pf, o_t, o_s, n_elem):
+    fine4 = jnp.concatenate([jac[19:20]] * 4, axis=1)
+    t = jnp.concatenate(traces(c[...], pf[...], n_elem), axis=1)
+    t = jnp.where(fine4 > 0.5, 0.0, t)
+    o_t[...] = t
+    o_s[...] = gather(t, soh[...])
+
+
+def window0_kernel(n_elem, at, xh, ph, c1, t0, soh, coef, jac, ld, dj, pf, lf,
+                   roh, o_base, o_t1, o_s1):
+    table(at, roh, n_elem, 0, LANES)
+    o_base[...] = fine_base(xh[...], ph[...], t0[...], roh, coef[...], jac[:, :LANES], ld[...],
+                            dj[...], lf[...], n_elem)
+    coarse_traces(c1, soh, jac, pf, o_t1, o_s1, n_elem)
 
 
 def step_kernel(n_elem, n_dom, last,
                 ids, r_a, r_w, r_1, r_2, r_3, r_own, base, p_sum, t_coarse, s_coarse,
                 roh, soh, coef, jac, ld, dj, pf, lf,
                 o_state, o_pub, o_sum, o_t, m_a, m_w, m_1, m_2, m_3, m_own):
-    dom_id, sub_id = ids[0], ids[1]
     n_face = 4 * n_elem
     tile = LANES
-    got = received((r_a, r_w, r_1, r_2, r_3, r_own), dom_id, n_dom)
-    jumps = [gather(got, roh[n_face:, f * n_elem:f * n_elem + tile]) for f in range(4)]
+    got = received((r_a, r_w, r_1, r_2, r_3, r_own), ids[0], n_dom)
+    jumps = [gather(got, roh[n_face:, f * tile:(f + 1) * tile]) for f in range(4)]
     state = base[...] - lift(jumps, coef[...], lf[...], tile, n_elem)
     jac_h = jac[:, :tile]
     terms = [state]
@@ -311,15 +323,27 @@
     sent = s_coarse[...]
     for f in range(4):
         sent = sent + gather(fine_t[f], soh[f * n_elem:f * n_elem + tile])
-    write_parts((m_a, m_w, m_1, m_2, m_3, m_own), sent, sub_id)
-
-
-def window_kernel(n_elem, state, pub, t, roh, coef, jac, ld, dj, lf, o_base):
+    write_parts((m_a, m_w, m_1, m_2, m_3, m_own), sent)
+
+
+def window_kernel(n_elem, tabled, at, state, pub, t, c, roh, soh, coef, jac, ld, dj, pf, lf,
+                  o_base, o_t, o_s, *o_roh):
     o_base[...] = fine_base(state[...], pub[...], t[...], roh, coef[...], jac[:, :LANES], ld[...],
                             dj[...], lf[...], n_elem)
-
-
-def window3_kernel(n_elem, x, cs, total, t, roh, coef, jac, ld, dj, lf, o_base):
+    coarse_traces(c, soh, jac, pf, o_t, o_s, n_elem)
+    if tabled:
+        table(at, o_roh[0], n_elem, LANES, n_elem - LANES)
+
+
+def split_gather(x, roh, roh2, rows, f, n_elem):
+    rest = n_elem - LANES
+    return jnp.concatenate(
+        [gather(x, roh[rows, f * LANES:(f + 1) * LANES]), gather(x, roh2[rows, f * rest:(f + 1) * rest])],
+        axis=1,
+    )
+
+
+def window3_kernel(n_elem, x, cs, total, t, roh, roh2, coef, jac, ld, dj, lf, o_base):
     fine = jac[19:20, :LANES] > 0.5
     parts = []
     for q in range(NQ):
@@ -328,18 +352,19 @@
         parts.append(c[:, LANES:])
     pub = jnp.concatenate(parts, axis=1)
     tv = t[...]
-    jumps = []
-    for f in range(4):
-        lanes = slice(f * n_elem, (f + 1) * n_elem)
-        jumps.append(gather(tv, roh[:4 * n_elem, lanes]) - tv[:, lanes])
+    rows = slice(0, 4 * n_elem)
+    jumps = [
+        split_gather(tv, roh, roh2, rows, f, n_elem) - tv[:, f * n_elem:(f + 1) * n_elem]
+        for f in range(4)
+    ]
     corr = lift(jumps, coef[...], lf[...], n_elem, n_elem)
     o_base[...] = x[...] + apply_l(pub, jac[...], ld[...], dj[...], n_elem) - corr
 
 
-def last_kernel(n_elem, n_dom, ids, r_a, r_w, r_1, r_2, r_3, r_own, base, roh, coef, lf, out):
-    n_face = 4 * n_elem
+def last_kernel(n_elem, n_dom, ids, r_a, r_w, r_1, r_2, r_3, r_own, base, roh, roh2, coef, lf, out):
     got = received((r_a, r_w, r_1, r_2, r_3, r_own), ids[0], n_dom)
-    jumps = [gather(got, roh[n_face:, f * n_elem:(f + 1) * n_elem]) for f in range(4)]
+    rows = slice(4 * n_elem, 4 * n_elem + 3 * LANES)
+    jumps = [split_gather(got, roh, roh2, rows, f, n_elem) for f in range(4)]
     res = base[...] - lift(jumps, coef[...], lf[...], n_elem, n_elem)
     for q in range(NQ):
         out[q * NB:(q + 1) * NB] = res[:NB, q * n_elem:(q + 1) * n_elem]
@@ -354,8 +379,8 @@
             specs.append(sm)
             ops.append(a)
         elif i in raw:
-            specs.append(vm)
-            ops.append(a)
+            specs.append(pl.BlockSpec(memory_space=pltpu.HBM))
+            ops.append(pltpu.with_memory_space_constraint(a, pltpu.HBM))
         else:
             specs.append(vm)
             ops.append(pltpu.with_memory_space_constraint(a, pltpu.VMEM))
@@ -374,6 +399,9 @@
     )(*ops)
 
 
+TAKEN = (4, 3, 2, 1, 0)
+
+
 def exchange(parts, n_dom):
     a, w, s1, s2, s3, own = parts
     other = [(i, ((i + 1) ^ 1) - 1 if 0 < i < n_dom - 1 else n_dom - 1 - i) for i in range(n_dom)]
@@ -382,7 +410,8 @@
     r3 = lax.ppermute(s3, "sub", [(i, i ^ 3) for i in range(4)])
     rw = lax.ppermute(w, "dom", other)
     r2 = lax.ppermute(s2, "sub", [(i, i ^ 2) for i in range(4)])
-    return ra, rw, r1, r2, r3, own
+    got = (ra, rw, r1, r2, r3)
+    return tuple(got[i] for i in TAKEN) + (own,)
 
 
 def make_body(n_dom, n_sub):
@@ -399,35 +428,35 @@
         trace = ((4 * KR, n_face), f32)
         listed = ((4 * KR, 3 * LANES), f32)
         msg = ((4 * KR, LANES), f32)
+        small = ((KR, LANES), f32)
+        msgs = [msg, msg, small, small, small, msg]
+        half = ((n_face + 3 * LANES, 4 * LANES), bf16)
+        rest = ((n_face + 3 * LANES, 4 * (n_elem - LANES)), bf16)
+        raw = [start_dofs, inv_jac, normals, bulk_modulus, density, deriv_mats,
+               jnp.transpose(face_proj, (1, 0, 2)), jnp.transpose(face_lift, (2, 0, 1)),
+               cluster, pml_flags, neighbours, dom_send, sub_send]
         first = call(
             lambda *r: first_kernel(n_elem, *r), "first",
             [((128, 128), bf16), ((48, 384), bf16), ((64, 128), bf16), ((48, 256), bf16),
-             ((8, n_face), f32), ((24, n_elem), f32), ((n_face, 3 * LANES), bf16)]
-            + [wide] * 5 + [trace] + [msg] * 6,
-            [ids, start_dofs, inv_jac, normals, bulk_modulus, density, deriv_mats, face_proj,
-             face_lift, cluster, pml_flags, dom_send, sub_send],
-            raw=range(13),
-            scratch=[pltpu.VMEM((192, LANES), f32), pltpu.VMEM((8, 3 * LANES), jnp.int32)],
+             ((8, n_face), f32), ((24, n_elem), f32), ((n_face, 3 * LANES), bf16),
+             ((4, n_elem), jnp.int32), wide, slim, slim, wide, wide, wide, trace] + msgs,
+            [ids] + raw, raw=range(1, 14),
+            scratch=[pltpu.VMEM(a.shape, a.dtype) for a in raw]
+            + [pltpu.SemaphoreType.DMA((len(raw),)), pltpu.VMEM((128, LANES), f32),
+               pltpu.VMEM((8, 3 * LANES), jnp.int32)],
         )
-        ld, dj, pf, lf, coef, jac, soh, x, p0, c1, c2, cs, t0 = first[:13]
-        (roh,) = call(
-            lambda *r: table_kernel(n_elem, n_halo, *r), "table",
-            [((n_face + 3 * LANES, n_face), bf16)], [ids, neighbours], raw=(1,), flops=1 << 28,
+        ld, dj, pf, lf, coef, jac, soh, at, x, xh, total, c1, c2, cs, t = first[:15]
+        got = exchange(first[15:], n_dom)
+        roh, base, t_c, s_c = call(
+            lambda *r: window0_kernel(n_elem, *r), "window0", [half, slim, trace, listed],
+            [at, xh, total, c1, t, soh, coef, jac, ld, dj, pf, lf], flops=1 << 28,
         )
-        got = exchange(first[13:], n_dom)
-        base, t1, t2, ts, s1, s2, ss = call(
-            lambda *r: window0_kernel(n_elem, *r), "window0",
-            [slim] + [trace] * 3 + [listed] * 3,
-            [x, p0, c1, c2, cs, t0, roh, soh, coef, jac, ld, dj, pf, lf], flops=1 << 29,
-        )
-        total = jnp.concatenate(
-            [p0[:, q * n_elem:q * n_elem + LANES] for q in range(NQ)], axis=1
-        )
-        for s, (t_c, s_c) in enumerate(((t1, s1), (t2, s2), (ts, ss))):
-            last = s == 2
+        roh2 = None
+        for s in range(SUBSTEPS - 1):
+            last = s == SUBSTEPS - 2
             outs = call(
                 lambda *r, last=last: step_kernel(n_elem, n_dom, last, *r), "step",
-                [slim] * 3 + [trace] + [msg] * 6,
+                [slim] * 3 + [trace] + msgs,
                 [ids, *got, base, total, t_c, s_c, roh, soh, coef, jac, ld, dj, pf, lf],
             )
             state, pub, total, t = outs[:4]
@@ -435,16 +464,21 @@
             if last:
                 (base,) = call(
                     lambda *r: window3_kernel(n_elem, *r), "window3", [wide],
-                    [x, cs, total, t, roh, coef, jac, ld, dj, lf], flops=1 << 29,
+                    [x, cs, total, t, roh, roh2, coef, jac, ld, dj, lf], flops=1 << 28,
                 )
             else:
-                (base,) = call(
-                    lambda *r: window_kernel(n_elem, *r), "window", [slim],
-                    [state, pub, t, roh, coef, jac, ld, dj, lf], flops=1 << 28,
+                res = call(
+                    lambda *r, s=s: window_kernel(n_elem, s == 0, *r), "window",
+                    [slim, trace, listed] + ([rest] if s == 0 else []),
+                    [at, state, pub, t, (c2, cs)[s], roh, soh, coef, jac, ld, dj, pf, lf],
+                    flops=1 << 28,
                 )
+                base, t_c, s_c = res[:3]
+                if s == 0:
+                    roh2 = res[3]
         (out,) = call(
             lambda *r: last_kernel(n_elem, n_dom, *r), "last",
-            [((NQ * NB, n_elem), f32)], [ids, *got, base, roh, coef, lf], hbm_out=True,
+            [((NQ * NB, n_elem), f32)], [ids, *got, base, roh, roh2, coef, lf], hbm_out=True,
         )
         return out
 

time: 61.3 us -> 46.7 us (0.76)
  local copies, waits for them, and re-layouts: 9.56 us -> 0 us
  waiting for transfers between devices: 10.9 us -> 5.48 us
  Pallas kernels: 15.4 us -> 16.2 us
    ppermute x4, waiting for transfers between devices: 10.6 us -> 0.19 us  [exchange(): r3 = lax.ppermute(s3, 'sub', [(i, i ^ 3) for i in range(4)])]
    unnamed x24 -> x0, local copies, waits for them, and re-layouts: 9.55 us -> none
    ppermute x4, starting transfers between devices: 9.66 us -> 2.48 us  [exchange(): r2 = lax.ppermute(s2, 'sub', [(i, i ^ 2) for i in range(4)])]
    ppermute x4, waiting for transfers between devices: 0.26 us -> 5.01 us  [exchange(): r2 = lax.ppermute(s2, 'sub', [(i, i ^ 2) for i in range(4)])]
    ppermute x4, starting transfers between devices: 1.58 us -> 6.15 us  [exchange(): r1 = lax.ppermute(s1, 'sub', [(i, i ^ 1) for i in range(4)])]
    ppermute x4, starting transfers between devices: 0.66 us -> 3.32 us  [exchange(): ra = lax.ppermute(a, 'dom', [(i, i ^ 1) for i in range(n_dom)])]
    ppermute x4, starting transfers between devices: 6.41 us -> 3.76 us  [exchange(): rw = lax.ppermute(w, 'dom', other)]
    ppermute x4, starting transfers between devices: 6.31 us -> 8.92 us  [exchange(): r3 = lax.ppermute(s3, 'sub', [(i, i ^ 3) for i in range(4)])]
  transfers between devices with their start and end apart: 20 -> 20, of which waited for: 6 -> 9; matrix products, arithmetic and copies ran while one was open for 0% -> 0% of each run, Pallas kernels for 8% -> 9%
where the time goes in v2:
time: 46.7 us; the launch traced here: 46.5 us
  starting transfers between devices  24.6 us (53%)
  Pallas kernels  16.2 us (35%)
  waiting for transfers between devices  5.48 us (12%)
    pallas_call x9, Pallas kernels, call(): pl.pallas_call(kernel, in_specs=specs, out_specs=[vm] * len(shapes), out_...  16.2 us
    ppermute x4, starting transfers between devices, exchange(): r3 = lax.ppermute(s3, 'sub', [(i, i ^ 3) for i in range(4)])  8.92 us
    ppermute x4, starting transfers between devices, exchange(): r1 = lax.ppermute(s1, 'sub', [(i, i ^ 1) for i in range(4)])  6.15 us
    ppermute x4, waiting for transfers between devices, exchange(): r2 = lax.ppermute(s2, 'sub', [(i, i ^ 2) for i in range(4)])  5.01 us
    ppermute x4, starting transfers between devices, exchange(): rw = lax.ppermute(w, 'dom', other)  3.76 us
    ppermute x4, starting transfers between devices, exchange(): ra = lax.ppermute(a, 'dom', [(i, i ^ 1) for i in range(n_dom)])  3.32 us
    ppermute x4, starting transfers between devices, exchange(): r2 = lax.ppermute(s2, 'sub', [(i, i ^ 2) for i in range(4)])  2.48 us
  transfers between devices with their start and end apart: 20, of which 9 were waited for; matrix products, arithmetic and copies ran while one was open for 0% of the time, Pallas kernels for 9%

profile of v2, /device:TPU:0, one launch (start us, length us, event | category | flops | bytes accessed | tf_op | source)
XLA Modules:
  0.0 46.5 jit_solution(5640841445798865272)
XLA Ops:
  0.0 0.1 pad_add_fusion.r_0_
  0.1 3.1 %first.1 = (bf16[128,128]{1,0:T(8,128)(2,1)S(1)}, bf16[48,384]{1,0:T(8,128)(2,1)S(1)}, bf16[64,128]{1,0:T(8,128)(2,1)S(1)}, bf16[48,256]{1,0:T(8,128)(2,1)S(1)},...) custom-call(s32[2]{0:T(128)S(1)} %pad_add_fusion.r_0_, ...), custom_call_target="tpu_custom_call" | custom-call | bytes 65536 | tf_op jit(solution)/shard_map/first/pallas_call | solution.py:390
  3.2 3.4 %collective-permute-start.3 = (f32[64,128]{1,0:T(8,128)S(1)}, f32[64,128]{1,0:T(8,128)S(1)}, u32[]{:S(2)}, u32[]{:S(2)}) collective-permute-start(f32[64,128]{1,0:T(8,128)S(1)} %get-tuple-element.68), channel_id=1, source_target_pairs={{0,28},{4,8},{8,4},{12,16},{16,12},{20,24},{24,20},{28,0},{1,29},{... | collective-permute-start | bytes 98312 | tf_op jit(solution)/shard_map/ppermute | solution.py:411
  6.6 0.0 collective-permute-start.4
  6.6 3.6 %collective-permute-start = (f32[16,128]{1,0:T(8,128)S(1)}, f32[16,128]{1,0:T(8,128)S(1)}, u32[]{:S(2)}, u32[]{:S(2)}) collective-permute-start(f32[16,128]{1,0:T(8,128)S(1)} %get-tuple-element.65), channel_id=1, source_target_pairs={{0,3},{1,2},{2,1},{3,0},{4,7},{5,6},{6,5},{7,4},{8,11},{9,10},{10,... | collective-permute-start | bytes 24584 | tf_op jit(solution)/shard_map/ppermute | solution.py:410
  10.2 0.0 collective-permute-start.1
  10.2 0.8 %collective-permute-start.2 = (f32[16,128]{1,0:T(8,128)S(1)}, f32[16,128]{1,0:T(8,128)S(1)}, u32[]{:S(2)}, u32[]{:S(2)}) collective-permute-start(f32[16,128]{1,0:T(8,128)S(1)} %get-tuple-element.67), channel_id=1, source_target_pairs={{0,1},{1,0},{2,3},{3,2},{4,5},{5,4},{6,7},{7,6},{8,9},{9,8},{10,11... | collective-permute-start | bytes 24584 | tf_op jit(solution)/shard_map/ppermute | solution.py:408
  11.0 1.2 %window0.1 = (bf16[1408,512]{1,0:T(8,128)(2,1)S(1)}, f32[40,512]{1,0:T(8,128)S(1)}, f32[64,1024]{1,0:T(8,128)S(1)}, f32[64,384]{1,0:T(8,128)S(1)}) custom-call(s32[4,256]{1,0:T(4,128)S(1)} %get-tuple-element.71.r_0_, f32[40,512]{1,0:T(8,128)S(1)} %get-tuple-element.72.r_1_, f32[40,512]{1,0:T(8,128)S(1)} %get-tuple-element.73.r_2_.r_8_, ...), custom_call_target="tpu_custom_call" | custom-call | flops 268435456 | bytes 65536 | tf_op jit(solution)/shard_map/window0/pallas_call | solution.py:390
  12.2 0.0 collective-permute-done.r_1_
  12.2 2.6 %collective-permute-done.1.r_2_ = f32[16,128]{1,0:T(8,128)S(1)} collective-permute-done((f32[16,128]{1,0:T(8,128)S(1)}, f32[16,128]{1,0:T(8,128)S(1)}, u32[]{:S(2)}, u32[]{:S(2)}) %collective-permute-start.1) | collective-permute-done | bytes 8224 | tf_op jit(solution)/shard_map/ppermute | solution.py:412
  14.8 0.0 collective-permute-done.2.r_3_
  14.8 0.0 collective-permute-done.3.r_4_
  14.8 0.0 collective-permute-done.4.r_5_
  14.8 2.2 %step.3 = (f32[40,512]{1,0:T(8,128)S(1)}, f32[40,512]{1,0:T(8,128)S(1)}, f32[40,512]{1,0:T(8,128)S(1)}, f32[64,1024]{1,0:T(8,128)S(1)}, f32[64,128]{1,0:T(8,128)...) custom-call(s32[2]{0:T(128)S(1)} %pad_add_fusion.r_0_, ...), custom_call_target="tpu_custom_call" | custom-call | bytes 65536 | tf_op jit(solution)/shard_map/step/pallas_call | solution.py:390
  17.0 0.1 collective-permute-start.8
  17.0 1.3 %collective-permute-start.9 = (f32[64,128]{1,0:T(8,128)S(1)}, f32[64,128]{1,0:T(8,128)S(1)}, u32[]{:S(2)}, u32[]{:S(2)}) collective-permute-start(f32[64,128]{1,0:T(8,128)S(1)} %get-tuple-element.91), channel_id=1, source_target_pairs={{0,4},{4,0},{8,12},{12,8},{16,20},{20,16},{24,28},{28,24},{1,5},{5... | collective-permute-start | bytes 98312 | tf_op jit(solution)/shard_map/ppermute | solution.py:409
  18.3 1.4 %collective-permute-start.5 = (f32[16,128]{1,0:T(8,128)S(1)}, f32[16,128]{1,0:T(8,128)S(1)}, u32[]{:S(2)}, u32[]{:S(2)}) collective-permute-start(f32[16,128]{1,0:T(8,128)S(1)} %get-tuple-element.87), channel_id=1, source_target_pairs={{0,3},{1,2},{2,1},{3,0},{4,7},{5,6},{6,5},{7,4},{8,11},{9,10},{10,... | collective-permute-start | bytes 24584 | tf_op jit(solution)/shard_map/ppermute | solution.py:410
  19.8 0.6 %collective-permute-start.6 = (f32[16,128]{1,0:T(8,128)S(1)}, f32[16,128]{1,0:T(8,128)S(1)}, u32[]{:S(2)}, u32[]{:S(2)}) collective-permute-start(f32[16,128]{1,0:T(8,128)S(1)} %get-tuple-element.88), channel_id=1, source_target_pairs={{0,2},{1,3},{2,0},{3,1},{4,6},{5,7},{6,4},{7,5},{8,10},{9,11},{10,... | collective-permute-start | bytes 24584 | tf_op jit(solution)/shard_map/ppermute | solution.py:412
  20.3 2.4 %collective-permute-start.7 = (f32[16,128]{1,0:T(8,128)S(1)}, f32[16,128]{1,0:T(8,128)S(1)}, u32[]{:S(2)}, u32[]{:S(2)}) collective-permute-start(f32[16,128]{1,0:T(8,128)S(1)} %get-tuple-element.89), channel_id=1, source_target_pairs={{0,1},{1,0},{2,3},{3,2},{4,5},{5,4},{6,7},{7,6},{8,9},{9,8},{10,11... | collective-permute-start | bytes 24584 | tf_op jit(solution)/shard_map/ppermute | solution.py:408
  22.7 1.2 %window.2 = (f32[40,512]{1,0:T(8,128)S(1)}, f32[64,1024]{1,0:T(8,128)S(1)}, f32[64,384]{1,0:T(8,128)S(1)}, bf16[1408,512]{1,0:T(8,128)(2,1)S(1)}) custom-call(s32[4,256]{1,0:T(4,128)S(1)} %get-tuple-element.71.r_0_, f32[40,512]{1,0:T(8,128)S(1)} %get-tuple-element.93.r_1_, f32[40,512]{1,0:T(8,128)S(1)} %get-tuple-element.94.r_2_, ...), custom_call_target="tpu_custom_call" | custom-call | flops 268435456 | bytes 65536 | tf_op jit(solution)/shard_map/window/pallas_call | solution.py:390
  24.0 0.0 collective-permute-done.5.r_1_
  24.0 0.3 collective-permute-done.6.r_2_
  24.3 0.1 collective-permute-done.7.r_3_
  24.4 0.0 collective-permute-done.8.r_4_
  24.4 0.0 collective-permute-done.9.r_5_
  24.4 2.1 %step.4 = (f32[40,512]{1,0:T(8,128)S(1)}, f32[40,512]{1,0:T(8,128)S(1)}, f32[40,512]{1,0:T(8,128)S(1)}, f32[64,1024]{1,0:T(8,128)S(1)}, f32[64,128]{1,0:T(8,128)...) custom-call(s32[2]{0:T(128)S(1)} %pad_add_fusion.r_0_, ...), custom_call_target="tpu_custom_call" | custom-call | bytes 65536 | tf_op jit(solution)/shard_map/step/pallas_call | solution.py:390
  26.6 0.3 collective-permute-start.13
  26.8 1.4 %collective-permute-start.14 = (f32[64,128]{1,0:T(8,128)S(1)}, f32[64,128]{1,0:T(8,128)S(1)}, u32[]{:S(2)}, u32[]{:S(2)}) collective-permute-start(f32[64,128]{1,0:T(8,128)S(1)} %get-tuple-element.105), channel_id=1, source_target_pairs={{0,4},{4,0},{8,12},{12,8},{16,20},{20,16},{24,28},{28,24},{1,5},{5... | collective-permute-start | bytes 98312 | tf_op jit(solution)/shard_map/ppermute | solution.py:409
  28.2 2.5 %collective-permute-start.10 = (f32[16,128]{1,0:T(8,128)S(1)}, f32[16,128]{1,0:T(8,128)S(1)}, u32[]{:S(2)}, u32[]{:S(2)}) collective-permute-start(f32[16,128]{1,0:T(8,128)S(1)} %get-tuple-element.101), channel_id=1, source_target_pairs={{0,3},{1,2},{2,1},{3,0},{4,7},{5,6},{6,5},{7,4},{8,11},{9,10},{10,... | collective-permute-start | bytes 24584 | tf_op jit(solution)/shard_map/ppermute | solution.py:410
  30.7 0.9 %collective-permute-start.11 = (f32[16,128]{1,0:T(8,128)S(1)}, f32[16,128]{1,0:T(8,128)S(1)}, u32[]{:S(2)}, u32[]{:S(2)}) collective-permute-start(f32[16,128]{1,0:T(8,128)S(1)} %get-tuple-element.102), channel_id=1, source_target_pairs={{0,2},{1,3},{2,0},{3,1},{4,6},{5,7},{6,4},{7,5},{8,10},{9,11},{10,... | collective-permute-start | bytes 24584 | tf_op jit(solution)/shard_map/ppermute | solution.py:412
  31.7 1.0 %collective-permute-start.12 = (f32[16,128]{1,0:T(8,128)S(1)}, f32[16,128]{1,0:T(8,128)S(1)}, u32[]{:S(2)}, u32[]{:S(2)}) collective-permute-start(f32[16,128]{1,0:T(8,128)S(1)} %get-tuple-element.103), channel_id=1, source_target_pairs={{0,1},{1,0},{2,3},{3,2},{4,5},{5,4},{6,7},{7,6},{8,9},{9,8},{10,11... | collective-permute-start | bytes 24584 | tf_op jit(solution)/shard_map/ppermute | solution.py:408
  32.6 0.9 %window.3 = (f32[40,512]{1,0:T(8,128)S(1)}, f32[64,1024]{1,0:T(8,128)S(1)}, f32[64,384]{1,0:T(8,128)S(1)}) custom-call(s32[4,256]{1,0:T(4,128)S(1)} %get-tuple-element.71.r_0_, f32[40,512]{1,0:T(8,128)S(1)} %get-tuple-element.107.r_1_, f32[40,512]{1,0:T(8,128)S(1)} %get-tuple-element.108.r_2_, f32[64,1024]{1,0:T(8,128)S(1)} %get-tuple-element.109.r_3_, ...), custom_call_target="tpu_custom_call" | custom-call | flops 268435456 | bytes 65536 | tf_op jit(solution)/shard_map/window/pallas_call | solution.py:390
  33.6 0.1 collective-permute-done.10.r_1_
  33.7 1.6 %collective-permute-done.11.r_2_ = f32[16,128]{1,0:T(8,128)S(1)} collective-permute-done((f32[16,128]{1,0:T(8,128)S(1)}, f32[16,128]{1,0:T(8,128)S(1)}, u32[]{:S(2)}, u32[]{:S(2)}) %collective-permute-start.11) | collective-permute-done | bytes 8224 | tf_op jit(solution)/shard_map/ppermute | solution.py:412
  35.3 0.1 collective-permute-done.12.r_3_
  35.4 0.0 collective-permute-done.13.r_4_
  35.4 0.0 collective-permute-done.14.r_5_
  35.4 2.7 %step.5 = (f32[40,512]{1,0:T(8,128)}, f32[40,512]{1,0:T(8,128)}, f32[40,512]{1,0:T(8,128)S(1)}, f32[64,1024]{1,0:T(8,128)S(1)}, f32[64,128]{1,0:T(8,128)S(1)}, /...) custom-call(s32[2]{0:T(128)S(1)} %pad_add_fusion.r_0_, ...), custom_call_target="tpu_custom_call" | custom-call | bytes 65536 | tf_op jit(solution)/shard_map/step/pallas_call | solution.py:390
  38.1 0.0 collective-permute-start.18
  38.1 0.6 %collective-permute-start.19 = (f32[64,128]{1,0:T(8,128)S(1)}, f32[64,128]{1,0:T(8,128)S(1)}, u32[]{:S(2)}, u32[]{:S(2)}) collective-permute-start(f32[64,128]{1,0:T(8,128)S(1)} %get-tuple-element.119), channel_id=1, source_target_pairs={{0,4},{4,0},{8,12},{12,8},{16,20},{20,16},{24,28},{28,24},{1,5},{5... | collective-permute-start | bytes 98312 | tf_op jit(solution)/shard_map/ppermute | solution.py:409
  38.7 1.4 %collective-permute-start.15 = (f32[16,128]{1,0:T(8,128)S(1)}, f32[16,128]{1,0:T(8,128)S(1)}, u32[]{:S(2)}, u32[]{:S(2)}) collective-permute-start(f32[16,128]{1,0:T(8,128)S(1)} %get-tuple-element.115), channel_id=1, source_target_pairs={{0,3},{1,2},{2,1},{3,0},{4,7},{5,6},{6,5},{7,4},{8,11},{9,10},{10,... | collective-permute-start | bytes 24584 | tf_op jit(solution)/shard_map/ppermute | solution.py:410
  40.1 1.0 %collective-permute-start.16 = (f32[16,128]{1,0:T(8,128)S(1)}, f32[16,128]{1,0:T(8,128)S(1)}, u32[]{:S(2)}, u32[]{:S(2)}) collective-permute-start(f32[16,128]{1,0:T(8,128)S(1)} %get-tuple-element.116), channel_id=1, source_target_pairs={{0,2},{1,3},{2,0},{3,1},{4,6},{5,7},{6,4},{7,5},{8,10},{9,11},{10,... | collective-permute-start | bytes 24584 | tf_op jit(solution)/shard_map/ppermute | solution.py:412
  41.1 2.0 %collective-permute-start.17 = (f32[16,128]{1,0:T(8,128)S(1)}, f32[16,128]{1,0:T(8,128)S(1)}, u32[]{:S(2)}, u32[]{:S(2)}) collective-permute-start(f32[16,128]{1,0:T(8,128)S(1)} %get-tuple-element.117), channel_id=1, source_target_pairs={{0,1},{1,0},{2,3},{3,2},{4,5},{5,4},{6,7},{7,6},{8,9},{9,8},{10,11... | collective-permute-start | bytes 24584 | tf_op jit(solution)/shard_map/ppermute | solution.py:408
  43.1 1.0 %window3.1.r_7_ = f32[40,1024]{1,0:T(8,128)S(1)} custom-call(f32[40,1024]{1,0:T(8,128)S(1)} %get-tuple-element.121.r_0_, f32[40,1024]{1,0:T(8,128)S(1)} %get-tuple-element.110.r_4_.r_1_, f32[40,512]{1,0:T(8,128)S(1)} %get-tuple-element.122.r_2_, f32[64,1024]{1,0:T(8,128)S(1)} %get-tuple-element.123.r_3_, ...), custom_call_target="tpu_custom_call" | custom-call | flops 268435456 | bytes 65536 | tf_op jit(solution)/shard_map/window3/pallas_call | solution.py:390
  44.1 0.1 collective-permute-done.15.r_1_
  44.1 0.5 %collective-permute-done.16.r_2_ = f32[16,128]{1,0:T(8,128)S(1)} collective-permute-done((f32[16,128]{1,0:T(8,128)S(1)}, f32[16,128]{1,0:T(8,128)S(1)}, u32[]{:S(2)}, u32[]{:S(2)}) %collective-permute-start.16) | collective-permute-done | bytes 8224 | tf_op jit(solution)/shard_map/ppermute | solution.py:412
  44.6 0.1 collective-permute-done.17.r_3_
  44.7 0.0 collective-permute-done.18.r_4_
  44.7 0.0 collective-permute-done.19.r_5_
  44.7 1.8 %last.1 = f32[140,256]{1,0:T(8,128)} custom-call(s32[2]{0:T(128)S(1)} %pad_add_fusion.r_0_, f32[16,128]{1,0:T(8,128)S(1)} %collective-permute-done.15.r_1_, f32[16,128]{1,0:T(8,128)S(1)} %collective-permute-done.16.r_2_, f32[16,128]{1,0:T(8,128)S(1)} %collective-permute-done.17.r_3_, f32[64,128]{1,0:T(8,128)S(1)} %collective-permute-done.18.r_4_, ...), custom_call_target="tpu_custom_call" | custom-call | bytes 65536 | tf_op jit(solution)/shard_map/last/pallas_call | solution.py:390
Async XLA Ops:
  3.2 11.6 %collective-permute-start.3 = (f32[64,128]{1,0:T(8,128)S(1)}, f32[64,128]{1,0:T(8,128)S(1)}, u32[]{:S(2)}, u32[]{:S(2)}) collective-permute-start(f32[64,128]{1,0:T(8,128)S(1)} %get-tuple-element.68), channel_id=1, source_target_pairs={{0,28},{4,8},{8,4},{12,16},{16,12},{20,24},{24,20},{28,0},{1,29},{... | collective-permute-start | bytes 98312 | tf_op jit(solution)/shard_map/ppermute | solution.py:411
  6.6 8.2 %collective-permute-start.4 = (f32[64,128]{1,0:T(8,128)S(1)}, f32[64,128]{1,0:T(8,128)S(1)}, u32[]{:S(2)}, u32[]{:S(2)}) collective-permute-start(f32[64,128]{1,0:T(8,128)S(1)} %get-tuple-element.69), channel_id=1, source_target_pairs={{0,4},{4,0},{8,12},{12,8},{16,20},{20,16},{24,28},{28,24},{1,5},{5... | collective-permute-start | bytes 98312 | tf_op jit(solution)/shard_map/ppermute | solution.py:409
  6.6 5.6 %collective-permute-start = (f32[16,128]{1,0:T(8,128)S(1)}, f32[16,128]{1,0:T(8,128)S(1)}, u32[]{:S(2)}, u32[]{:S(2)}) collective-permute-start(f32[16,128]{1,0:T(8,128)S(1)} %get-tuple-element.65), channel_id=1, source_target_pairs={{0,3},{1,2},{2,1},{3,0},{4,7},{5,6},{6,5},{7,4},{8,11},{9,10},{10,... | collective-permute-start | bytes 24584 | tf_op jit(solution)/shard_map/ppermute | solution.py:410
  10.2 4.5 %collective-permute-start.1 = (f32[16,128]{1,0:T(8,128)S(1)}, f32[16,128]{1,0:T(8,128)S(1)}, u32[]{:S(2)}, u32[]{:S(2)}) collective-permute-start(f32[16,128]{1,0:T(8,128)S(1)} %get-tuple-element.66), channel_id=1, source_target_pairs={{0,2},{1,3},{2,0},{3,1},{4,6},{5,7},{6,4},{7,5},{8,10},{9,11},{10,... | collective-permute-start | bytes 24584 | tf_op jit(solution)/shard_map/ppermute | solution.py:412
  10.2 4.5 %collective-permute-start.2 = (f32[16,128]{1,0:T(8,128)S(1)}, f32[16,128]{1,0:T(8,128)S(1)}, u32[]{:S(2)}, u32[]{:S(2)}) collective-permute-start(f32[16,128]{1,0:T(8,128)S(1)} %get-tuple-element.67), channel_id=1, source_target_pairs={{0,1},{1,0},{2,3},{3,2},{4,5},{5,4},{6,7},{7,6},{8,9},{9,8},{10,11... | collective-permute-start | bytes 24584 | tf_op jit(solution)/shard_map/ppermute | solution.py:408
  17.0 7.5 %collective-permute-start.8 = (f32[64,128]{1,0:T(8,128)S(1)}, f32[64,128]{1,0:T(8,128)S(1)}, u32[]{:S(2)}, u32[]{:S(2)}) collective-permute-start(f32[64,128]{1,0:T(8,128)S(1)} %get-tuple-element.90), channel_id=1, source_target_pairs={{0,28},{4,8},{8,4},{12,16},{16,12},{20,24},{24,20},{28,0},{1,29},{... | collective-permute-start | bytes 98312 | tf_op jit(solution)/shard_map/ppermute | solution.py:411
  17.0 7.4 %collective-permute-start.9 = (f32[64,128]{1,0:T(8,128)S(1)}, f32[64,128]{1,0:T(8,128)S(1)}, u32[]{:S(2)}, u32[]{:S(2)}) collective-permute-start(f32[64,128]{1,0:T(8,128)S(1)} %get-tuple-element.91), channel_id=1, source_target_pairs={{0,4},{4,0},{8,12},{12,8},{16,20},{20,16},{24,28},{28,24},{1,5},{5... | collective-permute-start | bytes 98312 | tf_op jit(solution)/shard_map/ppermute | solution.py:409
  18.3 5.6 %collective-permute-start.5 = (f32[16,128]{1,0:T(8,128)S(1)}, f32[16,128]{1,0:T(8,128)S(1)}, u32[]{:S(2)}, u32[]{:S(2)}) collective-permute-start(f32[16,128]{1,0:T(8,128)S(1)} %get-tuple-element.87), channel_id=1, source_target_pairs={{0,3},{1,2},{2,1},{3,0},{4,7},{5,6},{6,5},{7,4},{8,11},{9,10},{10,... | collective-permute-start | bytes 24584 | tf_op jit(solution)/shard_map/ppermute | solution.py:410
  19.8 4.6 %collective-permute-start.6 = (f32[16,128]{1,0:T(8,128)S(1)}, f32[16,128]{1,0:T(8,128)S(1)}, u32[]{:S(2)}, u32[]{:S(2)}) collective-permute-start(f32[16,128]{1,0:T(8,128)S(1)} %get-tuple-element.88), channel_id=1, source_target_pairs={{0,2},{1,3},{2,0},{3,1},{4,6},{5,7},{6,4},{7,5},{8,10},{9,11},{10,... | collective-permute-start | bytes 24584 | tf_op jit(solution)/shard_map/ppermute | solution.py:412
  20.3 4.1 %collective-permute-start.7 = (f32[16,128]{1,0:T(8,128)S(1)}, f32[16,128]{1,0:T(8,128)S(1)}, u32[]{:S(2)}, u32[]{:S(2)}) collective-permute-start(f32[16,128]{1,0:T(8,128)S(1)} %get-tuple-element.89), channel_id=1, source_target_pairs={{0,1},{1,0},{2,3},{3,2},{4,5},{5,4},{6,7},{7,6},{8,9},{9,8},{10,11... | collective-permute-start | bytes 24584 | tf_op jit(solution)/shard_map/ppermute | solution.py:408
  26.6 8.8 %collective-permute-start.13 = (f32[64,128]{1,0:T(8,128)S(1)}, f32[64,128]{1,0:T(8,128)S(1)}, u32[]{:S(2)}, u32[]{:S(2)}) collective-permute-start(f32[64,128]{1,0:T(8,128)S(1)} %get-tuple-element.104), channel_id=1, source_target_pairs={{0,28},{4,8},{8,4},{12,16},{16,12},{20,24},{24,20},{28,0},{1,29},{... | collective-permute-start | bytes 98312 | tf_op jit(solution)/shard_map/ppermute | solution.py:411
  26.8 8.6 %collective-permute-start.14 = (f32[64,128]{1,0:T(8,128)S(1)}, f32[64,128]{1,0:T(8,128)S(1)}, u32[]{:S(2)}, u32[]{:S(2)}) collective-permute-start(f32[64,128]{1,0:T(8,128)S(1)} %get-tuple-element.105), channel_id=1, source_target_pairs={{0,4},{4,0},{8,12},{12,8},{16,20},{20,16},{24,28},{28,24},{1,5},{5... | collective-permute-start | bytes 98312 | tf_op jit(solution)/shard_map/ppermute | solution.py:409
  28.2 5.4 %collective-permute-start.10 = (f32[16,128]{1,0:T(8,128)S(1)}, f32[16,128]{1,0:T(8,128)S(1)}, u32[]{:S(2)}, u32[]{:S(2)}) collective-permute-start(f32[16,128]{1,0:T(8,128)S(1)} %get-tuple-element.101), channel_id=1, source_target_pairs={{0,3},{1,2},{2,1},{3,0},{4,7},{5,6},{6,5},{7,4},{8,11},{9,10},{10,... | collective-permute-start | bytes 24584 | tf_op jit(solution)/shard_map/ppermute | solution.py:410
  30.7 4.6 %collective-permute-start.11 = (f32[16,128]{1,0:T(8,128)S(1)}, f32[16,128]{1,0:T(8,128)S(1)}, u32[]{:S(2)}, u32[]{:S(2)}) collective-permute-start(f32[16,128]{1,0:T(8,128)S(1)} %get-tuple-element.102), channel_id=1, source_target_pairs={{0,2},{1,3},{2,0},{3,1},{4,6},{5,7},{6,4},{7,5},{8,10},{9,11},{10,... | collective-permute-start | bytes 24584 | tf_op jit(solution)/shard_map/ppermute | solution.py:412
  31.7 3.7 %collective-permute-start.12 = (f32[16,128]{1,0:T(8,128)S(1)}, f32[16,128]{1,0:T(8,128)S(1)}, u32[]{:S(2)}, u32[]{:S(2)}) collective-permute-start(f32[16,128]{1,0:T(8,128)S(1)} %get-tuple-element.103), channel_id=1, source_target_pairs={{0,1},{1,0},{2,3},{3,2},{4,5},{5,4},{6,7},{7,6},{8,9},{9,8},{10,11... | collective-permute-start | bytes 24584 | tf_op jit(solution)/shard_map/ppermute | solution.py:408
  38.1 6.6 %collective-permute-start.18 = (f32[64,128]{1,0:T(8,128)S(1)}, f32[64,128]{1,0:T(8,128)S(1)}, u32[]{:S(2)}, u32[]{:S(2)}) collective-permute-start(f32[64,128]{1,0:T(8,128)S(1)} %get-tuple-element.118), channel_id=1, source_target_pairs={{0,28},{4,8},{8,4},{12,16},{16,12},{20,24},{24,20},{28,0},{1,29},{... | collective-permute-start | bytes 98312 | tf_op jit(solution)/shard_map/ppermute | solution.py:411
  38.1 6.6 %collective-permute-start.19 = (f32[64,128]{1,0:T(8,128)S(1)}, f32[64,128]{1,0:T(8,128)S(1)}, u32[]{:S(2)}, u32[]{:S(2)}) collective-permute-start(f32[64,128]{1,0:T(8,128)S(1)} %get-tuple-element.119), channel_id=1, source_target_pairs={{0,4},{4,0},{8,12},{12,8},{16,20},{20,16},{24,28},{28,24},{1,5},{5... | collective-permute-start | bytes 98312 | tf_op jit(solution)/shard_map/ppermute | solution.py:409
  38.7 5.4 %collective-permute-start.15 = (f32[16,128]{1,0:T(8,128)S(1)}, f32[16,128]{1,0:T(8,128)S(1)}, u32[]{:S(2)}, u32[]{:S(2)}) collective-permute-start(f32[16,128]{1,0:T(8,128)S(1)} %get-tuple-element.115), channel_id=1, source_target_pairs={{0,3},{1,2},{2,1},{3,0},{4,7},{5,6},{6,5},{7,4},{8,11},{9,10},{10,... | collective-permute-start | bytes 24584 | tf_op jit(solution)/shard_map/ppermute | solution.py:410
  40.1 4.5 %collective-permute-start.16 = (f32[16,128]{1,0:T(8,128)S(1)}, f32[16,128]{1,0:T(8,128)S(1)}, u32[]{:S(2)}, u32[]{:S(2)}) collective-permute-start(f32[16,128]{1,0:T(8,128)S(1)} %get-tuple-element.116), channel_id=1, source_target_pairs={{0,2},{1,3},{2,0},{3,1},{4,6},{5,7},{6,4},{7,5},{8,10},{9,11},{10,... | collective-permute-start | bytes 24584 | tf_op jit(solution)/shard_map/ppermute | solution.py:412
  41.1 3.7 %collective-permute-start.17 = (f32[16,128]{1,0:T(8,128)S(1)}, f32[16,128]{1,0:T(8,128)S(1)}, u32[]{:S(2)}, u32[]{:S(2)}) collective-permute-start(f32[16,128]{1,0:T(8,128)S(1)} %get-tuple-element.117), channel_id=1, source_target_pairs={{0,1},{1,0},{2,3},{3,2},{4,5},{5,4},{6,7},{7,6},{8,9},{9,8},{10,11... | collective-permute-start | bytes 24584 | tf_op jit(solution)/shard_map/ppermute | solution.py:408

commit v3 on v2

--- a/solution.py
+++ b/solution.py
@@ -132,11 +132,10 @@
     m_own[...] = sub
 
 
-def received(refs, dom_id, n_dom):
+def received(refs, inner):
     a, w, s1, s2, s3 = [refs[TAKEN.index(i)][...] for i in range(5)]
     own = refs[5][...]
-    inner = jnp.logical_and(dom_id > 0, dom_id < n_dom - 1)
-    w = jnp.where(inner, w, jnp.zeros_like(w))
+    w = jnp.where(inner[0:1] > 0.5, w, jnp.zeros_like(w))
     rows = []
     for q in range(NQ):
         row = own[q * KR:(q + 1) * KR]
@@ -146,10 +145,10 @@
     return jnp.concatenate([a, w, jnp.concatenate(rows, axis=0)], axis=1)
 
 
-def first_kernel(n_elem, *refs):
-    ids, raw = refs[0], refs[1:14]
-    (o_ld, o_dj, o_pf, o_lf, o_coef, o_jac, o_soh, o_at, o_x, o_xh, o_ph, o_c1, o_c2, o_cs,
-     o_t0, m_a, m_w, m_1, m_2, m_3, m_own) = refs[14:35]
+def first_kernel(n_elem, n_dom, *refs):
+    raw = refs[:13]
+    (o_ld, o_dj, o_pf, o_lf, o_coef, o_jac, o_soh, o_at, o_in, o_x, o_xh, o_ph, o_c1, o_c2, o_cs,
+     o_t0, m_a, m_w, m_1, m_2, m_3, m_own) = refs[13:35]
     held, sem, pad, lists = refs[35:48], refs[48], refs[49], refs[50]
     copies = [
         pltpu.make_async_copy(src, dst, sem.at[i]) for i, (src, dst) in enumerate(zip(raw, held))
@@ -162,7 +161,9 @@
     o_x[...] = jnp.zeros_like(o_x)
     for c in copies:
         c.wait()
-    dom_id, sub_id = ids[0], ids[1]
+    dom_id, sub_id = lax.axis_index("dom"), lax.axis_index("sub")
+    inner = jnp.logical_and(dom_id > 0, dom_id < n_dom - 1)
+    o_in[...] = jnp.full(o_in.shape, jnp.where(inner, 1.0, 0.0).astype(f32), f32)
     for r in range(3):
         pad[r * BR:r * BR + NB, :NB] = deriv[r]
     hi, lo = hi_lo(pad[:3 * BR])
@@ -296,13 +297,14 @@
     coarse_traces(c1, soh, jac, pf, o_t1, o_s1, n_elem)
 
 
-def step_kernel(n_elem, n_dom, last,
-                ids, r_a, r_w, r_1, r_2, r_3, r_own, base, p_sum, t_coarse, s_coarse,
+def step_kernel(n_elem, last,
+                inner, r_a, r_w, r_1, r_2, r_3, r_own, base, p_sum, t_coarse, s_coarse,
                 roh, soh, coef, jac, ld, dj, pf, lf,
-                o_state, o_pub, o_sum, o_t, m_a, m_w, m_1, m_2, m_3, m_own):
+                *outs):
+    o_sum, o_t, m_a, m_w, m_1, m_2, m_3, m_own = outs[:8]
     n_face = 4 * n_elem
     tile = LANES
-    got = received((r_a, r_w, r_1, r_2, r_3, r_own), ids[0], n_dom)
+    got = received((r_a, r_w, r_1, r_2, r_3, r_own), inner[...])
     jumps = [gather(got, roh[n_face:, f * tile:(f + 1) * tile]) for f in range(4)]
     state = base[...] - lift(jumps, coef[...], lf[...], tile, n_elem)
     jac_h = jac[:, :tile]
@@ -311,9 +313,10 @@
         terms.append(apply_l(terms[-1], jac_h, ld[...], dj[...], tile))
     pub = combine(terms, 0.0, SUB_DT)
     total = p_sum[...] + pub
-    o_state[...] = state
-    o_pub[...] = pub
     o_sum[...] = total
+    if not last:
+        outs[8][...] = state
+        outs[9][...] = pub
     fine = jac_h[19:20] > 0.5
     zero = jnp.zeros((4 * KR, tile), f32)
     fine_t = [jnp.where(fine, t, zero) for t in traces(total if last else pub, pf[...], tile)]
@@ -361,8 +364,8 @@
     o_base[...] = x[...] + apply_l(pub, jac[...], ld[...], dj[...], n_elem) - corr
 
 
-def last_kernel(n_elem, n_dom, ids, r_a, r_w, r_1, r_2, r_3, r_own, base, roh, roh2, coef, lf, out):
-    got = received((r_a, r_w, r_1, r_2, r_3, r_own), ids[0], n_dom)
+def last_kernel(n_elem, inner, r_a, r_w, r_1, r_2, r_3, r_own, base, roh, roh2, coef, lf, out):
+    got = received((r_a, r_w, r_1, r_2, r_3, r_own), inner[...])
     rows = slice(4 * n_elem, 4 * n_elem + 3 * LANES)
     jumps = [split_gather(got, roh, roh2, rows, f, n_elem) for f in range(4)]
     res = base[...] - lift(jumps, coef[...], lf[...], n_elem, n_elem)
@@ -372,13 +375,9 @@
 
 def call(kernel, name, outs, args, scratch=(), raw=(), hbm_out=False, flops=0):
     vm = pl.BlockSpec(memory_space=pltpu.VMEM)
-    sm = pl.BlockSpec(memory_space=pltpu.SMEM)
     specs, ops = [], []
     for i, a in enumerate(args):
-        if a.ndim == 1 and a.shape[0] == 2:
-            specs.append(sm)
-            ops.append(a)
-        elif i in raw:
+        if i in raw:
             specs.append(pl.BlockSpec(memory_space=pltpu.HBM))
             ops.append(pltpu.with_memory_space_constraint(a, pltpu.HBM))
         else:
@@ -422,13 +421,13 @@
         n_elem = start_dofs.shape[1]
         n_halo = dom_send.shape[1]
         n_face = 4 * n_elem
-        ids = jnp.stack([lax.axis_index("dom"), lax.axis_index("sub")]).astype(jnp.int32)
         wide = ((BR, NQ * n_elem), f32)
         slim = ((BR, NQ * LANES), f32)
         trace = ((4 * KR, n_face), f32)
         listed = ((4 * KR, 3 * LANES), f32)
         msg = ((4 * KR, LANES), f32)
         small = ((KR, LANES), f32)
+        msg_row = ((8, LANES), f32)
         msgs = [msg, msg, small, small, small, msg]
         half = ((n_face + 3 * LANES, 4 * LANES), bf16)
         rest = ((n_face + 3 * LANES, 4 * (n_elem - LANES)), bf16)
@@ -436,17 +435,17 @@
                jnp.transpose(face_proj, (1, 0, 2)), jnp.transpose(face_lift, (2, 0, 1)),
                cluster, pml_flags, neighbours, dom_send, sub_send]
         first = call(
-            lambda *r: first_kernel(n_elem, *r), "first",
+            lambda *r: first_kernel(n_elem, n_dom, *r), "first",
             [((128, 128), bf16), ((48, 384), bf16), ((64, 128), bf16), ((48, 256), bf16),
              ((8, n_face), f32), ((24, n_elem), f32), ((n_face, 3 * LANES), bf16),
-             ((4, n_elem), jnp.int32), wide, slim, slim, wide, wide, wide, trace] + msgs,
-            [ids] + raw, raw=range(1, 14),
+             ((4, n_elem), jnp.int32), msg_row, wide, slim, slim, wide, wide, wide, trace] + msgs,
+            raw, raw=range(13),
             scratch=[pltpu.VMEM(a.shape, a.dtype) for a in raw]
             + [pltpu.SemaphoreType.DMA((len(raw),)), pltpu.VMEM((128, LANES), f32),
                pltpu.VMEM((8, 3 * LANES), jnp.int32)],
         )
-        ld, dj, pf, lf, coef, jac, soh, at, x, xh, total, c1, c2, cs, t = first[:15]
-        got = exchange(first[15:], n_dom)
+        ld, dj, pf, lf, coef, jac, soh, at, inner, x, xh, total, c1, c2, cs, t = first[:16]
+        got = exchange(first[16:], n_dom)
         roh, base, t_c, s_c = call(
             lambda *r: window0_kernel(n_elem, *r), "window0", [half, slim, trace, listed],
             [at, xh, total, c1, t, soh, coef, jac, ld, dj, pf, lf], flops=1 << 28,
@@ -455,12 +454,12 @@
         for s in range(SUBSTEPS - 1):
             last = s == SUBSTEPS - 2
             outs = call(
-                lambda *r, last=last: step_kernel(n_elem, n_dom, last, *r), "step",
-                [slim] * 3 + [trace] + msgs,
-                [ids, *got, base, total, t_c, s_c, roh, soh, coef, jac, ld, dj, pf, lf],
+                lambda *r, last=last: step_kernel(n_elem, last, *r), "step",
+                [slim, trace] + msgs + ([] if last else [slim] * 2),
+                [inner, *got, base, total, t_c, s_c, roh, soh, coef, jac, ld, dj, pf, lf],
             )
-            state, pub, total, t = outs[:4]
-            got = exchange(outs[4:], n_dom)
+            total, t = outs[:2]
+            got = exchange(outs[2:8], n_dom)
             if last:
                 (base,) = call(
                     lambda *r: window3_kernel(n_elem, *r), "window3", [wide],
@@ -470,15 +469,15 @@
                 res = call(
                     lambda *r, s=s: window_kernel(n_elem, s == 0, *r), "window",
                     [slim, trace, listed] + ([rest] if s == 0 else []),
-                    [at, state, pub, t, (c2, cs)[s], roh, soh, coef, jac, ld, dj, pf, lf],
+                    [at, outs[8], outs[9], t, (c2, cs)[s], roh, soh, coef, jac, ld, dj, pf, lf],
                     flops=1 << 28,
                 )
                 base, t_c, s_c = res[:3]
                 if s == 0:
                     roh2 = res[3]
         (out,) = call(
-            lambda *r: last_kernel(n_elem, n_dom, *r), "last",
-            [((NQ * NB, n_elem), f32)], [ids, *got, base, roh, roh2, coef, lf], hbm_out=True,
+            lambda *r: last_kernel(n_elem, *r), "last",
+            [((NQ * NB, n_elem), f32)], [inner, *got, base, roh, roh2, coef, lf], hbm_out=True,
         )
         return out
 

time: 46.7 us -> 43.4 us (0.929)
  Pallas kernels: 16.2 us -> 13 us
    pallas_call x9, Pallas kernels: 16.2 us -> 13 us  [call(): pl.pallas_call(kernel, in_specs=specs, out_specs=[vm] * len(shapes), out_...]
  transfers between devices with their start and end apart: 20 -> 20, of which waited for: 9 -> 9; matrix products, arithmetic and copies ran while one was open for 0% -> 0% of each run, Pallas kernels for 9% -> 10%
where the time goes in v3:
time: 43.4 us; the launch traced here: 43.2 us
  starting transfers between devices  24.7 us (57%)
  Pallas kernels  13 us (30%)
  waiting for transfers between devices  5.49 us (13%)
    pallas_call x9, Pallas kernels, call(): pl.pallas_call(kernel, in_specs=specs, out_specs=[vm] * len(shapes), out_...  13 us
    ppermute x4, starting transfers between devices, exchange(): r3 = lax.ppermute(s3, 'sub', [(i, i ^ 3) for i in range(4)])  8.93 us
    ppermute x4, starting transfers between devices, exchange(): r1 = lax.ppermute(s1, 'sub', [(i, i ^ 1) for i in range(4)])  6.14 us
    ppermute x4, waiting for transfers between devices, exchange(): r2 = lax.ppermute(s2, 'sub', [(i, i ^ 2) for i in range(4)])  5.01 us
    ppermute x4, starting transfers between devices, exchange(): rw = lax.ppermute(w, 'dom', other)  3.8 us
    ppermute x4, starting transfers between devices, exchange(): ra = lax.ppermute(a, 'dom', [(i, i ^ 1) for i in range(n_dom)])  3.3 us
    ppermute x4, starting transfers between devices, exchange(): r2 = lax.ppermute(s2, 'sub', [(i, i ^ 2) for i in range(4)])  2.47 us
  transfers between devices with their start and end apart: 20, of which 9 were waited for; matrix products, arithmetic and copies ran while one was open for 0% of the time, Pallas kernels for 10%

profile of v3, /device:TPU:0, one launch (start us, length us, event | category | flops | bytes accessed | tf_op | source)
XLA Modules:
  0.0 43.2 jit_solution(4094570445902944562)
XLA Ops:
  0.0 2.6 %first.1 = (bf16[128,128]{1,0:T(8,128)(2,1)S(1)}, bf16[48,384]{1,0:T(8,128)(2,1)S(1)}, bf16[64,128]{1,0:T(8,128)(2,1)S(1)}, bf16[48,256]{1,0:T(8,128)(2,1)S(1)},...) custom-call(f32[140,256]{1,0:T(8,128)} %r_0_.1, ...), custom_call_target="tpu_custom_call" | custom-call | bytes 65536 | tf_op jit(solution)/shard_map/first/pallas_call | solution.py:389
  2.6 3.4 %collective-permute-start.3 = (f32[64,128]{1,0:T(8,128)S(1)}, f32[64,128]{1,0:T(8,128)S(1)}, u32[]{:S(2)}, u32[]{:S(2)}) collective-permute-start(f32[64,128]{1,0:T(8,128)S(1)} %get-tuple-element.70), channel_id=1, source_target_pairs={{0,28},{4,8},{8,4},{12,16},{16,12},{20,24},{24,20},{28,0},{1,29},{... | collective-permute-start | bytes 98312 | tf_op jit(solution)/shard_map/ppermute | solution.py:410
  6.0 0.0 collective-permute-start.4
  6.0 3.6 %collective-permute-start = (f32[16,128]{1,0:T(8,128)S(1)}, f32[16,128]{1,0:T(8,128)S(1)}, u32[]{:S(2)}, u32[]{:S(2)}) collective-permute-start(f32[16,128]{1,0:T(8,128)S(1)} %get-tuple-element.67), channel_id=1, source_target_pairs={{0,3},{1,2},{2,1},{3,0},{4,7},{5,6},{6,5},{7,4},{8,11},{9,10},{10,... | collective-permute-start | bytes 24584 | tf_op jit(solution)/shard_map/ppermute | solution.py:409
  9.6 0.0 collective-permute-start.1
  9.6 0.8 %collective-permute-start.2 = (f32[16,128]{1,0:T(8,128)S(1)}, f32[16,128]{1,0:T(8,128)S(1)}, u32[]{:S(2)}, u32[]{:S(2)}) collective-permute-start(f32[16,128]{1,0:T(8,128)S(1)} %get-tuple-element.69), channel_id=1, source_target_pairs={{0,1},{1,0},{2,3},{3,2},{4,5},{5,4},{6,7},{7,6},{8,9},{9,8},{10,11... | collective-permute-start | bytes 24584 | tf_op jit(solution)/shard_map/ppermute | solution.py:407
  10.4 1.2 %window0.1 = (bf16[1408,512]{1,0:T(8,128)(2,1)S(1)}, f32[40,512]{1,0:T(8,128)S(1)}, f32[64,1024]{1,0:T(8,128)S(1)}, f32[64,384]{1,0:T(8,128)S(1)}) custom-call(s32[4,256]{1,0:T(4,128)S(1)} %get-tuple-element.73.r_0_, f32[40,512]{1,0:T(8,128)S(1)} %get-tuple-element.74.r_1_, f32[40,512]{1,0:T(8,128)S(1)} %get-tuple-element.75.r_2_.r_8_, ...), custom_call_target="tpu_custom_call" | custom-call | flops 268435456 | bytes 65536 | tf_op jit(solution)/shard_map/window0/pallas_call | solution.py:389
  11.6 0.0 collective-permute-done.r_1_
  11.6 2.6 %collective-permute-done.1.r_2_ = f32[16,128]{1,0:T(8,128)S(1)} collective-permute-done((f32[16,128]{1,0:T(8,128)S(1)}, f32[16,128]{1,0:T(8,128)S(1)}, u32[]{:S(2)}, u32[]{:S(2)}) %collective-permute-start.1) | collective-permute-done | bytes 8224 | tf_op jit(solution)/shard_map/ppermute | solution.py:411
  14.1 0.0 collective-permute-done.2.r_3_
  14.1 0.0 collective-permute-done.3.r_4_
  14.1 0.0 collective-permute-done.4.r_5_
  14.2 1.6 %step.3 = (f32[40,512]{1,0:T(8,128)S(1)}, f32[64,1024]{1,0:T(8,128)S(1)}, f32[64,128]{1,0:T(8,128)S(1)}, f32[64,128]{1,0:T(8,128)S(1)}, f32[16,128]{1,0:T(8,128)...) custom-call(f32[8,128]{1,0:T(8,128)S(1)} %get-tuple-element.66.r_0_,, ...), custom_call_target="tpu_custom_call" | custom-call | bytes 65536 | tf_op jit(solution)/shard_map/step/pallas_call | solution.py:389
  15.8 0.1 collective-permute-start.8
  15.8 1.3 %collective-permute-start.9 = (f32[64,128]{1,0:T(8,128)S(1)}, f32[64,128]{1,0:T(8,128)S(1)}, u32[]{:S(2)}, u32[]{:S(2)}) collective-permute-start(f32[64,128]{1,0:T(8,128)S(1)} %get-tuple-element.93), channel_id=1, source_target_pairs={{0,4},{4,0},{8,12},{12,8},{16,20},{20,16},{24,28},{28,24},{1,5},{5... | collective-permute-start | bytes 98312 | tf_op jit(solution)/shard_map/ppermute | solution.py:408
  17.2 1.4 %collective-permute-start.5 = (f32[16,128]{1,0:T(8,128)S(1)}, f32[16,128]{1,0:T(8,128)S(1)}, u32[]{:S(2)}, u32[]{:S(2)}) collective-permute-start(f32[16,128]{1,0:T(8,128)S(1)} %get-tuple-element.89), channel_id=1, source_target_pairs={{0,3},{1,2},{2,1},{3,0},{4,7},{5,6},{6,5},{7,4},{8,11},{9,10},{10,... | collective-permute-start | bytes 24584 | tf_op jit(solution)/shard_map/ppermute | solution.py:409
  18.6 0.6 %collective-permute-start.6 = (f32[16,128]{1,0:T(8,128)S(1)}, f32[16,128]{1,0:T(8,128)S(1)}, u32[]{:S(2)}, u32[]{:S(2)}) collective-permute-start(f32[16,128]{1,0:T(8,128)S(1)} %get-tuple-element.90), channel_id=1, source_target_pairs={{0,2},{1,3},{2,0},{3,1},{4,6},{5,7},{6,4},{7,5},{8,10},{9,11},{10,... | collective-permute-start | bytes 24584 | tf_op jit(solution)/shard_map/ppermute | solution.py:411
  19.2 2.4 %collective-permute-start.7 = (f32[16,128]{1,0:T(8,128)S(1)}, f32[16,128]{1,0:T(8,128)S(1)}, u32[]{:S(2)}, u32[]{:S(2)}) collective-permute-start(f32[16,128]{1,0:T(8,128)S(1)} %get-tuple-element.91), channel_id=1, source_target_pairs={{0,1},{1,0},{2,3},{3,2},{4,5},{5,4},{6,7},{7,6},{8,9},{9,8},{10,11... | collective-permute-start | bytes 24584 | tf_op jit(solution)/shard_map/ppermute | solution.py:407
  21.5 1.3 %window.2 = (f32[40,512]{1,0:T(8,128)S(1)}, f32[64,1024]{1,0:T(8,128)S(1)}, f32[64,384]{1,0:T(8,128)S(1)}, bf16[1408,512]{1,0:T(8,128)(2,1)S(1)}) custom-call(s32[4,256]{1,0:T(4,128)S(1)} %get-tuple-element.73.r_0_, f32[40,512]{1,0:T(8,128)S(1)} %get-tuple-element.95.r_1_, f32[40,512]{1,0:T(8,128)S(1)} %get-tuple-element.96.r_2_, ...), custom_call_target="tpu_custom_call" | custom-call | flops 268435456 | bytes 65536 | tf_op jit(solution)/shard_map/window/pallas_call | solution.py:389
  22.8 0.0 collective-permute-done.5.r_1_
  22.8 0.3 collective-permute-done.6.r_2_
  23.2 0.1 collective-permute-done.7.r_3_
  23.2 0.0 collective-permute-done.8.r_4_
  23.2 0.0 collective-permute-done.9.r_5_
  23.2 1.6 %step.4 = (f32[40,512]{1,0:T(8,128)S(1)}, f32[64,1024]{1,0:T(8,128)S(1)}, f32[64,128]{1,0:T(8,128)S(1)}, f32[64,128]{1,0:T(8,128)S(1)}, f32[16,128]{1,0:T(8,128)...) custom-call(f32[8,128]{1,0:T(8,128)S(1)} %get-tuple-element.66.r_0_,, ...), custom_call_target="tpu_custom_call" | custom-call | bytes 65536 | tf_op jit(solution)/shard_map/step/pallas_call | solution.py:389
  24.8 0.3 collective-permute-start.13
  25.1 1.4 %collective-permute-start.14 = (f32[64,128]{1,0:T(8,128)S(1)}, f32[64,128]{1,0:T(8,128)S(1)}, u32[]{:S(2)}, u32[]{:S(2)}) collective-permute-start(f32[64,128]{1,0:T(8,128)S(1)} %get-tuple-element.107), channel_id=1, source_target_pairs={{0,4},{4,0},{8,12},{12,8},{16,20},{20,16},{24,28},{28,24},{1,5},{5... | collective-permute-start | bytes 98312 | tf_op jit(solution)/shard_map/ppermute | solution.py:408
  26.5 2.5 %collective-permute-start.10 = (f32[16,128]{1,0:T(8,128)S(1)}, f32[16,128]{1,0:T(8,128)S(1)}, u32[]{:S(2)}, u32[]{:S(2)}) collective-permute-start(f32[16,128]{1,0:T(8,128)S(1)} %get-tuple-element.103), channel_id=1, source_target_pairs={{0,3},{1,2},{2,1},{3,0},{4,7},{5,6},{6,5},{7,4},{8,11},{9,10},{10,... | collective-permute-start | bytes 24584 | tf_op jit(solution)/shard_map/ppermute | solution.py:409
  29.0 0.9 %collective-permute-start.11 = (f32[16,128]{1,0:T(8,128)S(1)}, f32[16,128]{1,0:T(8,128)S(1)}, u32[]{:S(2)}, u32[]{:S(2)}) collective-permute-start(f32[16,128]{1,0:T(8,128)S(1)} %get-tuple-element.104), channel_id=1, source_target_pairs={{0,2},{1,3},{2,0},{3,1},{4,6},{5,7},{6,4},{7,5},{8,10},{9,11},{10,... | collective-permute-start | bytes 24584 | tf_op jit(solution)/shard_map/ppermute | solution.py:411
  29.9 1.0 %collective-permute-start.12 = (f32[16,128]{1,0:T(8,128)S(1)}, f32[16,128]{1,0:T(8,128)S(1)}, u32[]{:S(2)}, u32[]{:S(2)}) collective-permute-start(f32[16,128]{1,0:T(8,128)S(1)} %get-tuple-element.105), channel_id=1, source_target_pairs={{0,1},{1,0},{2,3},{3,2},{4,5},{5,4},{6,7},{7,6},{8,9},{9,8},{10,11... | collective-permute-start | bytes 24584 | tf_op jit(solution)/shard_map/ppermute | solution.py:407
  30.9 0.9 %window.3 = (f32[40,512]{1,0:T(8,128)S(1)}, f32[64,1024]{1,0:T(8,128)S(1)}, f32[64,384]{1,0:T(8,128)S(1)}) custom-call(s32[4,256]{1,0:T(4,128)S(1)} %get-tuple-element.73.r_0_, f32[40,512]{1,0:T(8,128)S(1)} %get-tuple-element.109.r_1_, f32[40,512]{1,0:T(8,128)S(1)} %get-tuple-element.110.r_2_, f32[64,1024]{1,0:T(8,128)S(1)} %get-tuple-element.111.r_3_, ...), custom_call_target="tpu_custom_call" | custom-call | flops 268435456 | bytes 65536 | tf_op jit(solution)/shard_map/window/pallas_call | solution.py:389
  31.8 0.1 collective-permute-done.10.r_1_
  32.0 1.6 %collective-permute-done.11.r_2_ = f32[16,128]{1,0:T(8,128)S(1)} collective-permute-done((f32[16,128]{1,0:T(8,128)S(1)}, f32[16,128]{1,0:T(8,128)S(1)}, u32[]{:S(2)}, u32[]{:S(2)}) %collective-permute-start.11) | collective-permute-done | bytes 8224 | tf_op jit(solution)/shard_map/ppermute | solution.py:411
  33.6 0.1 collective-permute-done.12.r_3_
  33.7 0.0 collective-permute-done.13.r_4_
  33.7 0.0 collective-permute-done.14.r_5_
  33.7 1.6 %step.5 = (f32[40,512]{1,0:T(8,128)S(1)}, f32[64,1024]{1,0:T(8,128)S(1)}, f32[64,128]{1,0:T(8,128)S(1)}, f32[64,128]{1,0:T(8,128)S(1)}, f32[16,128]{1,0:T(8,128)...) custom-call(f32[8,128]{1,0:T(8,128)S(1)} %get-tuple-element.66.r_0_, ...), custom_call_target="tpu_custom_call" | custom-call | bytes 65536 | tf_op jit(solution)/shard_map/step/pallas_call | solution.py:389
  35.3 0.1 collective-permute-start.18
  35.4 0.6 %collective-permute-start.19 = (f32[64,128]{1,0:T(8,128)S(1)}, f32[64,128]{1,0:T(8,128)S(1)}, u32[]{:S(2)}, u32[]{:S(2)}) collective-permute-start(f32[64,128]{1,0:T(8,128)S(1)} %get-tuple-element.121), channel_id=1, source_target_pairs={{0,4},{4,0},{8,12},{12,8},{16,20},{20,16},{24,28},{28,24},{1,5},{5... | collective-permute-start | bytes 98312 | tf_op jit(solution)/shard_map/ppermute | solution.py:408
  35.9 1.4 %collective-permute-start.15 = (f32[16,128]{1,0:T(8,128)S(1)}, f32[16,128]{1,0:T(8,128)S(1)}, u32[]{:S(2)}, u32[]{:S(2)}) collective-permute-start(f32[16,128]{1,0:T(8,128)S(1)} %get-tuple-element.117), channel_id=1, source_target_pairs={{0,3},{1,2},{2,1},{3,0},{4,7},{5,6},{6,5},{7,4},{8,11},{9,10},{10,... | collective-permute-start | bytes 24584 | tf_op jit(solution)/shard_map/ppermute | solution.py:409
  37.3 1.0 %collective-permute-start.16 = (f32[16,128]{1,0:T(8,128)S(1)}, f32[16,128]{1,0:T(8,128)S(1)}, u32[]{:S(2)}, u32[]{:S(2)}) collective-permute-start(f32[16,128]{1,0:T(8,128)S(1)} %get-tuple-element.118), channel_id=1, source_target_pairs={{0,2},{1,3},{2,0},{3,1},{4,6},{5,7},{6,4},{7,5},{8,10},{9,11},{10,... | collective-permute-start | bytes 24584 | tf_op jit(solution)/shard_map/ppermute | solution.py:411
  38.3 2.0 %collective-permute-start.17 = (f32[16,128]{1,0:T(8,128)S(1)}, f32[16,128]{1,0:T(8,128)S(1)}, u32[]{:S(2)}, u32[]{:S(2)}) collective-permute-start(f32[16,128]{1,0:T(8,128)S(1)} %get-tuple-element.119), channel_id=1, source_target_pairs={{0,1},{1,0},{2,3},{3,2},{4,5},{5,4},{6,7},{7,6},{8,9},{9,8},{10,11... | collective-permute-start | bytes 24584 | tf_op jit(solution)/shard_map/ppermute | solution.py:407
  40.3 1.0 %window3.1.r_7_ = f32[40,1024]{1,0:T(8,128)S(1)} custom-call(f32[40,1024]{1,0:T(8,128)S(1)} %get-tuple-element.123.r_0_, f32[40,1024]{1,0:T(8,128)S(1)} %get-tuple-element.112.r_4_.r_1_, f32[40,512]{1,0:T(8,128)S(1)} %get-tuple-element.124.r_2_, f32[64,1024]{1,0:T(8,128)S(1)} %get-tuple-element.125.r_3_, ...), custom_call_target="tpu_custom_call" | custom-call | flops 268435456 | bytes 65536 | tf_op jit(solution)/shard_map/window3/pallas_call | solution.py:389
  41.3 0.1 collective-permute-done.15.r_1_
  41.4 0.5 %collective-permute-done.16.r_2_ = f32[16,128]{1,0:T(8,128)S(1)} collective-permute-done((f32[16,128]{1,0:T(8,128)S(1)}, f32[16,128]{1,0:T(8,128)S(1)}, u32[]{:S(2)}, u32[]{:S(2)}) %collective-permute-start.16) | collective-permute-done | bytes 8224 | tf_op jit(solution)/shard_map/ppermute | solution.py:411
  41.9 0.1 collective-permute-done.17.r_3_
  41.9 0.0 collective-permute-done.18.r_4_
  41.9 0.0 collective-permute-done.19.r_5_
  42.0 1.3 %last.1 = f32[140,256]{1,0:T(8,128)} custom-call(f32[8,128]{1,0:T(8,128)S(1)} %get-tuple-element.66.r_0_, f32[16,128]{1,0:T(8,128)S(1)} %collective-permute-done.15.r_1_, f32[16,128]{1,0:T(8,128)S(1)} %collective-permute-done.16.r_2_, f32[16,128]{1,0:T(8,128)S(1)} %collective-permute-done.17.r_3_, f32[64,128]{1,0:T(8,128)S(1)} %collective-permute-done.18.r_4_, ...), custom_call_target="tpu_custom_call" | custom-call | bytes 65536 | tf_op jit(solution)/shard_map/last/pallas_call | solution.py:389
Async XLA Ops:
  2.6 11.6 %collective-permute-start.3 = (f32[64,128]{1,0:T(8,128)S(1)}, f32[64,128]{1,0:T(8,128)S(1)}, u32[]{:S(2)}, u32[]{:S(2)}) collective-permute-start(f32[64,128]{1,0:T(8,128)S(1)} %get-tuple-element.70), channel_id=1, source_target_pairs={{0,28},{4,8},{8,4},{12,16},{16,12},{20,24},{24,20},{28,0},{1,29},{... | collective-permute-start | bytes 98312 | tf_op jit(solution)/shard_map/ppermute | solution.py:410
  6.0 8.2 %collective-permute-start.4 = (f32[64,128]{1,0:T(8,128)S(1)}, f32[64,128]{1,0:T(8,128)S(1)}, u32[]{:S(2)}, u32[]{:S(2)}) collective-permute-start(f32[64,128]{1,0:T(8,128)S(1)} %get-tuple-element.71), channel_id=1, source_target_pairs={{0,4},{4,0},{8,12},{12,8},{16,20},{20,16},{24,28},{28,24},{1,5},{5... | collective-permute-start | bytes 98312 | tf_op jit(solution)/shard_map/ppermute | solution.py:408
  6.0 5.6 %collective-permute-start = (f32[16,128]{1,0:T(8,128)S(1)}, f32[16,128]{1,0:T(8,128)S(1)}, u32[]{:S(2)}, u32[]{:S(2)}) collective-permute-start(f32[16,128]{1,0:T(8,128)S(1)} %get-tuple-element.67), channel_id=1, source_target_pairs={{0,3},{1,2},{2,1},{3,0},{4,7},{5,6},{6,5},{7,4},{8,11},{9,10},{10,... | collective-permute-start | bytes 24584 | tf_op jit(solution)/shard_map/ppermute | solution.py:409
  9.6 4.5 %collective-permute-start.1 = (f32[16,128]{1,0:T(8,128)S(1)}, f32[16,128]{1,0:T(8,128)S(1)}, u32[]{:S(2)}, u32[]{:S(2)}) collective-permute-start(f32[16,128]{1,0:T(8,128)S(1)} %get-tuple-element.68), channel_id=1, source_target_pairs={{0,2},{1,3},{2,0},{3,1},{4,6},{5,7},{6,4},{7,5},{8,10},{9,11},{10,... | collective-permute-start | bytes 24584 | tf_op jit(solution)/shard_map/ppermute | solution.py:411
  9.6 4.5 %collective-permute-start.2 = (f32[16,128]{1,0:T(8,128)S(1)}, f32[16,128]{1,0:T(8,128)S(1)}, u32[]{:S(2)}, u32[]{:S(2)}) collective-permute-start(f32[16,128]{1,0:T(8,128)S(1)} %get-tuple-element.69), channel_id=1, source_target_pairs={{0,1},{1,0},{2,3},{3,2},{4,5},{5,4},{6,7},{7,6},{8,9},{9,8},{10,11... | collective-permute-start | bytes 24584 | tf_op jit(solution)/shard_map/ppermute | solution.py:407
  15.8 7.5 %collective-permute-start.8 = (f32[64,128]{1,0:T(8,128)S(1)}, f32[64,128]{1,0:T(8,128)S(1)}, u32[]{:S(2)}, u32[]{:S(2)}) collective-permute-start(f32[64,128]{1,0:T(8,128)S(1)} %get-tuple-element.92), channel_id=1, source_target_pairs={{0,28},{4,8},{8,4},{12,16},{16,12},{20,24},{24,20},{28,0},{1,29},{... | collective-permute-start | bytes 98312 | tf_op jit(solution)/shard_map/ppermute | solution.py:410
  15.8 7.4 %collective-permute-start.9 = (f32[64,128]{1,0:T(8,128)S(1)}, f32[64,128]{1,0:T(8,128)S(1)}, u32[]{:S(2)}, u32[]{:S(2)}) collective-permute-start(f32[64,128]{1,0:T(8,128)S(1)} %get-tuple-element.93), channel_id=1, source_target_pairs={{0,4},{4,0},{8,12},{12,8},{16,20},{20,16},{24,28},{28,24},{1,5},{5... | collective-permute-start | bytes 98312 | tf_op jit(solution)/shard_map/ppermute | solution.py:408
  17.2 5.7 %collective-permute-start.5 = (f32[16,128]{1,0:T(8,128)S(1)}, f32[16,128]{1,0:T(8,128)S(1)}, u32[]{:S(2)}, u32[]{:S(2)}) collective-permute-start(f32[16,128]{1,0:T(8,128)S(1)} %get-tuple-element.89), channel_id=1, source_target_pairs={{0,3},{1,2},{2,1},{3,0},{4,7},{5,6},{6,5},{7,4},{8,11},{9,10},{10,... | collective-permute-start | bytes 24584 | tf_op jit(solution)/shard_map/ppermute | solution.py:409
  18.6 4.6 %collective-permute-start.6 = (f32[16,128]{1,0:T(8,128)S(1)}, f32[16,128]{1,0:T(8,128)S(1)}, u32[]{:S(2)}, u32[]{:S(2)}) collective-permute-start(f32[16,128]{1,0:T(8,128)S(1)} %get-tuple-element.90), channel_id=1, source_target_pairs={{0,2},{1,3},{2,0},{3,1},{4,6},{5,7},{6,4},{7,5},{8,10},{9,11},{10,... | collective-permute-start | bytes 24584 | tf_op jit(solution)/shard_map/ppermute | solution.py:411
  19.2 4.1 %collective-permute-start.7 = (f32[16,128]{1,0:T(8,128)S(1)}, f32[16,128]{1,0:T(8,128)S(1)}, u32[]{:S(2)}, u32[]{:S(2)}) collective-permute-start(f32[16,128]{1,0:T(8,128)S(1)} %get-tuple-element.91), channel_id=1, source_target_pairs={{0,1},{1,0},{2,3},{3,2},{4,5},{5,4},{6,7},{7,6},{8,9},{9,8},{10,11... | collective-permute-start | bytes 24584 | tf_op jit(solution)/shard_map/ppermute | solution.py:407
  24.8 8.8 %collective-permute-start.13 = (f32[64,128]{1,0:T(8,128)S(1)}, f32[64,128]{1,0:T(8,128)S(1)}, u32[]{:S(2)}, u32[]{:S(2)}) collective-permute-start(f32[64,128]{1,0:T(8,128)S(1)} %get-tuple-element.106), channel_id=1, source_target_pairs={{0,28},{4,8},{8,4},{12,16},{16,12},{20,24},{24,20},{28,0},{1,29},{... | collective-permute-start | bytes 98312 | tf_op jit(solution)/shard_map/ppermute | solution.py:410
  25.1 8.6 %collective-permute-start.14 = (f32[64,128]{1,0:T(8,128)S(1)}, f32[64,128]{1,0:T(8,128)S(1)}, u32[]{:S(2)}, u32[]{:S(2)}) collective-permute-start(f32[64,128]{1,0:T(8,128)S(1)} %get-tuple-element.107), channel_id=1, source_target_pairs={{0,4},{4,0},{8,12},{12,8},{16,20},{20,16},{24,28},{28,24},{1,5},{5... | collective-permute-start | bytes 98312 | tf_op jit(solution)/shard_map/ppermute | solution.py:408
  26.5 5.4 %collective-permute-start.10 = (f32[16,128]{1,0:T(8,128)S(1)}, f32[16,128]{1,0:T(8,128)S(1)}, u32[]{:S(2)}, u32[]{:S(2)}) collective-permute-start(f32[16,128]{1,0:T(8,128)S(1)} %get-tuple-element.103), channel_id=1, source_target_pairs={{0,3},{1,2},{2,1},{3,0},{4,7},{5,6},{6,5},{7,4},{8,11},{9,10},{10,... | collective-permute-start | bytes 24584 | tf_op jit(solution)/shard_map/ppermute | solution.py:409
  29.0 4.6 %collective-permute-start.11 = (f32[16,128]{1,0:T(8,128)S(1)}, f32[16,128]{1,0:T(8,128)S(1)}, u32[]{:S(2)}, u32[]{:S(2)}) collective-permute-start(f32[16,128]{1,0:T(8,128)S(1)} %get-tuple-element.104), channel_id=1, source_target_pairs={{0,2},{1,3},{2,0},{3,1},{4,6},{5,7},{6,4},{7,5},{8,10},{9,11},{10,... | collective-permute-start | bytes 24584 | tf_op jit(solution)/shard_map/ppermute | solution.py:411
  29.9 3.7 %collective-permute-start.12 = (f32[16,128]{1,0:T(8,128)S(1)}, f32[16,128]{1,0:T(8,128)S(1)}, u32[]{:S(2)}, u32[]{:S(2)}) collective-permute-start(f32[16,128]{1,0:T(8,128)S(1)} %get-tuple-element.105), channel_id=1, source_target_pairs={{0,1},{1,0},{2,3},{3,2},{4,5},{5,4},{6,7},{7,6},{8,9},{9,8},{10,11... | collective-permute-start | bytes 24584 | tf_op jit(solution)/shard_map/ppermute | solution.py:407
  35.3 6.7 %collective-permute-start.18 = (f32[64,128]{1,0:T(8,128)S(1)}, f32[64,128]{1,0:T(8,128)S(1)}, u32[]{:S(2)}, u32[]{:S(2)}) collective-permute-start(f32[64,128]{1,0:T(8,128)S(1)} %get-tuple-element.120), channel_id=1, source_target_pairs={{0,28},{4,8},{8,4},{12,16},{16,12},{20,24},{24,20},{28,0},{1,29},{... | collective-permute-start | bytes 98312 | tf_op jit(solution)/shard_map/ppermute | solution.py:410
  35.4 6.6 %collective-permute-start.19 = (f32[64,128]{1,0:T(8,128)S(1)}, f32[64,128]{1,0:T(8,128)S(1)}, u32[]{:S(2)}, u32[]{:S(2)}) collective-permute-start(f32[64,128]{1,0:T(8,128)S(1)} %get-tuple-element.121), channel_id=1, source_target_pairs={{0,4},{4,0},{8,12},{12,8},{16,20},{20,16},{24,28},{28,24},{1,5},{5... | collective-permute-start | bytes 98312 | tf_op jit(solution)/shard_map/ppermute | solution.py:408
  35.9 5.4 %collective-permute-start.15 = (f32[16,128]{1,0:T(8,128)S(1)}, f32[16,128]{1,0:T(8,128)S(1)}, u32[]{:S(2)}, u32[]{:S(2)}) collective-permute-start(f32[16,128]{1,0:T(8,128)S(1)} %get-tuple-element.117), channel_id=1, source_target_pairs={{0,3},{1,2},{2,1},{3,0},{4,7},{5,6},{6,5},{7,4},{8,11},{9,10},{10,... | collective-permute-start | bytes 24584 | tf_op jit(solution)/shard_map/ppermute | solution.py:409
  37.3 4.5 %collective-permute-start.16 = (f32[16,128]{1,0:T(8,128)S(1)}, f32[16,128]{1,0:T(8,128)S(1)}, u32[]{:S(2)}, u32[]{:S(2)}) collective-permute-start(f32[16,128]{1,0:T(8,128)S(1)} %get-tuple-element.118), channel_id=1, source_target_pairs={{0,2},{1,3},{2,0},{3,1},{4,6},{5,7},{6,4},{7,5},{8,10},{9,11},{10,... | collective-permute-start | bytes 24584 | tf_op jit(solution)/shard_map/ppermute | solution.py:411
  38.3 3.7 %collective-permute-start.17 = (f32[16,128]{1,0:T(8,128)S(1)}, f32[16,128]{1,0:T(8,128)S(1)}, u32[]{:S(2)}, u32[]{:S(2)}) collective-permute-start(f32[16,128]{1,0:T(8,128)S(1)} %get-tuple-element.119), channel_id=1, source_target_pairs={{0,1},{1,0},{2,3},{3,2},{4,5},{5,4},{6,7},{7,6},{8,9},{9,8},{10,11... | collective-permute-start | bytes 24584 | tf_op jit(solution)/shard_map/ppermute | solution.py:407

commit v4 on v3

--- a/solution.py
+++ b/solution.py
@@ -121,21 +121,34 @@
 
 def write_parts(refs, sent):
     m_a, m_w, m_1, m_2, m_3, m_own = refs
-    m_a[...] = sent[:, :LANES]
-    m_w[...] = sent[:, LANES:2 * LANES]
+    for i, ref in ((0, m_a), (1, m_w)):
+        part = sent[:, i * LANES:(i + 1) * LANES]
+        for q in range(3):
+            row = part[q * KR:(q + 1) * KR]
+            ref[q * KR:(q + 1) * KR] = jnp.where(block_mask(row.shape, 3), turn(part[3 * KR:], 3 - q), row)
     sub = sent[:, 2 * LANES:]
     for k, ref in ((1, m_1), (2, m_2), (3, m_3)):
         msg = turn(sub[:KR], -k)
         for q in range(1, NQ):
             msg = jnp.where(block_mask(msg.shape, q), turn(sub[q * KR:(q + 1) * KR], q - k), msg)
-        ref[...] = msg
+        ref[:KR] = msg
     m_own[...] = sub
 
 
+def unpack(msg):
+    last = turn(msg[2 * KR:], -1)
+    for q in (1, 0):
+        last = jnp.where(block_mask(last.shape, q), turn(msg[q * KR:(q + 1) * KR], q - 3), last)
+    return jnp.concatenate([msg, last], axis=0)
+
+
 def received(refs, inner):
-    a, w, s1, s2, s3 = [refs[TAKEN.index(i)][...] for i in range(5)]
+    a, w, s1, s2, s3 = [refs[TAKEN.index(i)] for i in range(5)]
     own = refs[5][...]
+    a = unpack(a[...])
+    w = unpack(w[...])
     w = jnp.where(inner[0:1] > 0.5, w, jnp.zeros_like(w))
+    s1, s2, s3 = s1[:KR], s2[:KR], s3[:KR]
     rows = []
     for q in range(NQ):
         row = own[q * KR:(q + 1) * KR]
@@ -398,7 +411,7 @@
     )(*ops)
 
 
-TAKEN = (4, 3, 2, 1, 0)
+TAKEN = (4, 3, 1, 2, 0)
 
 
 def exchange(parts, n_dom):
@@ -420,6 +433,7 @@
              cluster, pml_flags, neighbours, dom_send, sub_send):
         n_elem = start_dofs.shape[1]
         n_halo = dom_send.shape[1]
+        assert n_halo <= 96
         n_face = 4 * n_elem
         wide = ((BR, NQ * n_elem), f32)
         slim = ((BR, NQ * LANES), f32)
@@ -427,8 +441,9 @@
         listed = ((4 * KR, 3 * LANES), f32)
         msg = ((4 * KR, LANES), f32)
         small = ((KR, LANES), f32)
+        dom_msg = ((3 * KR, LANES), f32)
         msg_row = ((8, LANES), f32)
-        msgs = [msg, msg, small, small, small, msg]
+        msgs = [dom_msg, dom_msg, dom_msg, small, small, msg]
         half = ((n_face + 3 * LANES, 4 * LANES), bf16)
         rest = ((n_face + 3 * LANES, 4 * (n_elem - LANES)), bf16)
         raw = [start_dofs, inv_jac, normals, bulk_modulus, density, deriv_mats,
@@ -448,7 +463,7 @@
         got = exchange(first[16:], n_dom)
         roh, base, t_c, s_c = call(
             lambda *r: window0_kernel(n_elem, *r), "window0", [half, slim, trace, listed],
-            [at, xh, total, c1, t, soh, coef, jac, ld, dj, pf, lf], flops=1 << 28,
+            [at, xh, total, c1, t, soh, coef, jac, ld, dj, pf, lf], flops=1 << 36,
         )
         roh2 = None
         for s in range(SUBSTEPS - 1):
@@ -463,14 +478,14 @@
             if last:
                 (base,) = call(
                     lambda *r: window3_kernel(n_elem, *r), "window3", [wide],
-                    [x, cs, total, t, roh, roh2, coef, jac, ld, dj, lf], flops=1 << 28,
+                    [x, cs, total, t, roh, roh2, coef, jac, ld, dj, lf], flops=1 << 36,
                 )
             else:
                 res = call(
                     lambda *r, s=s: window_kernel(n_elem, s == 0, *r), "window",
                     [slim, trace, listed] + ([rest] if s == 0 else []),
                     [at, outs[8], outs[9], t, (c2, cs)[s], roh, soh, coef, jac, ld, dj, pf, lf],
-                    flops=1 << 28,
+                    flops=1 << 36,
                 )
                 base, t_c, s_c = res[:3]
                 if s == 0:

time: 43.4 us -> 41.3 us (0.952)
  starting transfers between devices: 24.7 us -> 22.2 us
    ppermute x4, starting transfers between devices: 8.93 us -> 12.2 us  [exchange(): r3 = lax.ppermute(s3, 'sub', [(i, i ^ 3) for i in range(4)])]
    ppermute x4, starting transfers between devices: 3.3 us -> 0.61 us  [exchange(): ra = lax.ppermute(a, 'dom', [(i, i ^ 1) for i in range(n_dom)])]
    ppermute x4, starting transfers between devices: 6.14 us -> 4.95 us  [exchange(): r1 = lax.ppermute(s1, 'sub', [(i, i ^ 1) for i in range(4)])]
    ppermute x4, waiting for transfers between devices: 5.01 us -> 3.84 us  [exchange(): r2 = lax.ppermute(s2, 'sub', [(i, i ^ 2) for i in range(4)])]
    ppermute x4, waiting for transfers between devices: 0.25 us -> 1.38 us  [exchange(): r1 = lax.ppermute(s1, 'sub', [(i, i ^ 1) for i in range(4)])]
    ppermute x4, starting transfers between devices: 3.8 us -> 2.83 us  [exchange(): rw = lax.ppermute(w, 'dom', other)]
    ppermute x4, starting transfers between devices: 2.47 us -> 1.6 us  [exchange(): r2 = lax.ppermute(s2, 'sub', [(i, i ^ 2) for i in range(4)])]
    ppermute x4, waiting for transfers between devices: 0.01 us -> 0.45 us  [exchange(): rw = lax.ppermute(w, 'dom', other)]
  transfers between devices with their start and end apart: 20 -> 20, of which waited for: 9 -> 9; matrix products, arithmetic and copies ran while one was open for 0% -> 0% of each run, Pallas kernels for 10% -> 11%
where the time goes in v4:
time: 41.3 us; the launch traced here: 41.1 us
  starting transfers between devices  22.2 us (54%)
  Pallas kernels  13.1 us (32%)
  waiting for transfers between devices  5.69 us (14%)
    pallas_call x9, Pallas kernels, call(): pl.pallas_call(kernel, in_specs=specs, out_specs=[vm] * len(shapes), out_...  13.1 us
    ppermute x4, starting transfers between devices, exchange(): r3 = lax.ppermute(s3, 'sub', [(i, i ^ 3) for i in range(4)])  12.2 us
    ppermute x4, starting transfers between devices, exchange(): r1 = lax.ppermute(s1, 'sub', [(i, i ^ 1) for i in range(4)])  4.95 us
    ppermute x4, waiting for transfers between devices, exchange(): r2 = lax.ppermute(s2, 'sub', [(i, i ^ 2) for i in range(4)])  3.84 us
    ppermute x4, starting transfers between devices, exchange(): rw = lax.ppermute(w, 'dom', other)  2.83 us
    ppermute x4, starting transfers between devices, exchange(): r2 = lax.ppermute(s2, 'sub', [(i, i ^ 2) for i in range(4)])  1.6 us
    ppermute x4, waiting for transfers between devices, exchange(): r1 = lax.ppermute(s1, 'sub', [(i, i ^ 1) for i in range(4)])  1.38 us
  transfers between devices with their start and end apart: 20, of which 9 were waited for; matrix products, arithmetic and copies ran while one was open for 0% of the time, Pallas kernels for 11%

profile of v4, /device:TPU:0, one launch (start us, length us, event | category | flops | bytes accessed | tf_op | source)
XLA Modules:
  0.0 41.1 jit_solution(11877958532157763375)
XLA Ops:
  0.0 2.6 %first.1 = (bf16[128,128]{1,0:T(8,128)(2,1)S(1)}, bf16[48,384]{1,0:T(8,128)(2,1)S(1)}, bf16[64,128]{1,0:T(8,128)(2,1)S(1)}, bf16[48,256]{1,0:T(8,128)(2,1)S(1)},...) custom-call(f32[140,256]{1,0:T(8,128)} %r_0_.1, ...), custom_call_target="tpu_custom_call" | custom-call | bytes 65536 | tf_op jit(solution)/shard_map/first/pallas_call | solution.py:402
  2.6 5.1 %collective-permute-start = (f32[16,128]{1,0:T(8,128)S(1)}, f32[16,128]{1,0:T(8,128)S(1)}, u32[]{:S(2)}, u32[]{:S(2)}) collective-permute-start(f32[16,128]{1,0:T(8,128)S(1)} %get-tuple-element.67), channel_id=1, source_target_pairs={{0,3},{1,2},{2,1},{3,0},{4,7},{5,6},{6,5},{7,4},{8,11},{9,10},{10,... | collective-permute-start | bytes 24584 | tf_op jit(solution)/shard_map/ppermute | solution.py:422
  7.7 0.0 collective-permute-start.1
  7.7 1.6 %collective-permute-start.2 = (f32[48,128]{1,0:T(8,128)S(1)}, f32[48,128]{1,0:T(8,128)S(1)}, u32[]{:S(2)}, u32[]{:S(2)}) collective-permute-start(f32[48,128]{1,0:T(8,128)S(1)} %get-tuple-element.69), channel_id=1, source_target_pairs={{0,28},{4,8},{8,4},{12,16},{16,12},{20,24},{24,20},{28,0},{1,29},{... | collective-permute-start | bytes 73736 | tf_op jit(solution)/shard_map/ppermute | solution.py:423
  9.3 0.6 %collective-permute-start.3 = (f32[48,128]{1,0:T(8,128)S(1)}, f32[48,128]{1,0:T(8,128)S(1)}, u32[]{:S(2)}, u32[]{:S(2)}) collective-permute-start(f32[48,128]{1,0:T(8,128)S(1)} %get-tuple-element.70), channel_id=1, source_target_pairs={{0,1},{1,0},{2,3},{3,2},{4,5},{5,4},{6,7},{7,6},{8,9},{9,8},{10,11... | collective-permute-start | bytes 73736 | tf_op jit(solution)/shard_map/ppermute | solution.py:420
  10.0 0.0 collective-permute-start.4
  10.0 1.2 %window0.1 = (bf16[1408,512]{1,0:T(8,128)(2,1)S(1)}, f32[40,512]{1,0:T(8,128)S(1)}, f32[64,1024]{1,0:T(8,128)S(1)}, f32[64,384]{1,0:T(8,128)S(1)}) custom-call(s32[4,256]{1,0:T(4,128)S(1)} %get-tuple-element.73.r_0_, f32[40,512]{1,0:T(8,128)S(1)} %get-tuple-element.74.r_1_, f32[40,512]{1,0:T(8,128)S(1)} %get-tuple-element.75.r_2_.r_8_, ...), custom_call_target="tpu_custom_call" | custom-call | flops 68719476736 | bytes 65536 | tf_op jit(solution)/shard_map/window0/pallas_call | solution.py:402
  11.2 0.0 collective-permute-done.r_1_
  11.2 1.1 %collective-permute-done.1.r_2_ = f32[16,128]{1,0:T(8,128)S(1)} collective-permute-done((f32[16,128]{1,0:T(8,128)S(1)}, f32[16,128]{1,0:T(8,128)S(1)}, u32[]{:S(2)}, u32[]{:S(2)}) %collective-permute-start.1) | collective-permute-done | bytes 8224 | tf_op jit(solution)/shard_map/ppermute | solution.py:424
  12.3 0.0 collective-permute-done.2.r_3_
  12.3 0.9 %collective-permute-done.3.r_4_ = f32[48,128]{1,0:T(8,128)S(1)} collective-permute-done((f32[48,128]{1,0:T(8,128)S(1)}, f32[48,128]{1,0:T(8,128)S(1)}, u32[]{:S(2)}, u32[]{:S(2)}) %collective-permute-start.3) | collective-permute-done | bytes 24608 | tf_op jit(solution)/shard_map/ppermute | solution.py:420
  13.2 0.0 collective-permute-done.4.r_5_
  13.2 1.6 %step.3 = (f32[40,512]{1,0:T(8,128)S(1)}, f32[64,1024]{1,0:T(8,128)S(1)}, f32[48,128]{1,0:T(8,128)S(1)}, f32[48,128]{1,0:T(8,128)S(1)}, f32[48,128]{1,0:T(8,128)...) custom-call(f32[8,128]{1,0:T(8,128)S(1)} %get-tuple-element.66.r_0_,, ...), custom_call_target="tpu_custom_call" | custom-call | bytes 65536 | tf_op jit(solution)/shard_map/step/pallas_call | solution.py:402
  14.8 2.1 %collective-permute-start.5 = (f32[16,128]{1,0:T(8,128)S(1)}, f32[16,128]{1,0:T(8,128)S(1)}, u32[]{:S(2)}, u32[]{:S(2)}) collective-permute-start(f32[16,128]{1,0:T(8,128)S(1)} %get-tuple-element.89), channel_id=1, source_target_pairs={{0,3},{1,2},{2,1},{3,0},{4,7},{5,6},{6,5},{7,4},{8,11},{9,10},{10,... | collective-permute-start | bytes 24584 | tf_op jit(solution)/shard_map/ppermute | solution.py:422
  16.9 0.6 %collective-permute-start.6 = (f32[16,128]{1,0:T(8,128)S(1)}, f32[16,128]{1,0:T(8,128)S(1)}, u32[]{:S(2)}, u32[]{:S(2)}) collective-permute-start(f32[16,128]{1,0:T(8,128)S(1)} %get-tuple-element.90), channel_id=1, source_target_pairs={{0,2},{1,3},{2,0},{3,1},{4,6},{5,7},{6,4},{7,5},{8,10},{9,11},{10,... | collective-permute-start | bytes 24584 | tf_op jit(solution)/shard_map/ppermute | solution.py:424
  17.6 0.0 collective-permute-start.7
  17.6 1.6 %collective-permute-start.8 = (f32[48,128]{1,0:T(8,128)S(1)}, f32[48,128]{1,0:T(8,128)S(1)}, u32[]{:S(2)}, u32[]{:S(2)}) collective-permute-start(f32[48,128]{1,0:T(8,128)S(1)} %get-tuple-element.92), channel_id=1, source_target_pairs={{0,1},{1,0},{2,3},{3,2},{4,5},{5,4},{6,7},{7,6},{8,9},{9,8},{10,11... | collective-permute-start | bytes 73736 | tf_op jit(solution)/shard_map/ppermute | solution.py:420
  19.3 0.5 %collective-permute-start.9 = (f32[48,128]{1,0:T(8,128)S(1)}, f32[48,128]{1,0:T(8,128)S(1)}, u32[]{:S(2)}, u32[]{:S(2)}) collective-permute-start(f32[48,128]{1,0:T(8,128)S(1)} %get-tuple-element.93), channel_id=1, source_target_pairs={{0,4},{4,0},{8,12},{12,8},{16,20},{20,16},{24,28},{28,24},{1,5},{5... | collective-permute-start | bytes 73736 | tf_op jit(solution)/shard_map/ppermute | solution.py:421
  19.7 1.2 %window.2 = (f32[40,512]{1,0:T(8,128)S(1)}, f32[64,1024]{1,0:T(8,128)S(1)}, f32[64,384]{1,0:T(8,128)S(1)}, bf16[1408,512]{1,0:T(8,128)(2,1)S(1)}) custom-call(s32[4,256]{1,0:T(4,128)S(1)} %get-tuple-element.73.r_0_, f32[40,512]{1,0:T(8,128)S(1)} %get-tuple-element.95.r_1_, f32[40,512]{1,0:T(8,128)S(1)} %get-tuple-element.96.r_2_, ...), custom_call_target="tpu_custom_call" | custom-call | flops 68719476736 | bytes 65536 | tf_op jit(solution)/shard_map/window/pallas_call | solution.py:402
  21.0 0.0 collective-permute-done.5.r_1_
  21.0 0.6 %collective-permute-done.6.r_2_ = f32[16,128]{1,0:T(8,128)S(1)} collective-permute-done((f32[16,128]{1,0:T(8,128)S(1)}, f32[16,128]{1,0:T(8,128)S(1)}, u32[]{:S(2)}, u32[]{:S(2)}) %collective-permute-start.6) | collective-permute-done | bytes 8224 | tf_op jit(solution)/shard_map/ppermute | solution.py:424
  21.5 0.2 collective-permute-done.7.r_3_
  21.7 0.0 collective-permute-done.8.r_4_
  21.7 0.0 collective-permute-done.9.r_5_
  21.7 1.6 %step.4 = (f32[40,512]{1,0:T(8,128)S(1)}, f32[64,1024]{1,0:T(8,128)S(1)}, f32[48,128]{1,0:T(8,128)S(1)}, f32[48,128]{1,0:T(8,128)S(1)}, f32[48,128]{1,0:T(8,128)...) custom-call(f32[8,128]{1,0:T(8,128)S(1)} %get-tuple-element.66.r_0_,, ...), custom_call_target="tpu_custom_call" | custom-call | bytes 65536 | tf_op jit(solution)/shard_map/step/pallas_call | solution.py:402
  23.4 2.9 %collective-permute-start.10 = (f32[16,128]{1,0:T(8,128)S(1)}, f32[16,128]{1,0:T(8,128)S(1)}, u32[]{:S(2)}, u32[]{:S(2)}) collective-permute-start(f32[16,128]{1,0:T(8,128)S(1)} %get-tuple-element.103), channel_id=1, source_target_pairs={{0,3},{1,2},{2,1},{3,0},{4,7},{5,6},{6,5},{7,4},{8,11},{9,10},{10,... | collective-permute-start | bytes 24584 | tf_op jit(solution)/shard_map/ppermute | solution.py:422
  26.3 0.3 collective-permute-start.11
  26.6 0.6 %collective-permute-start.12 = (f32[48,128]{1,0:T(8,128)S(1)}, f32[48,128]{1,0:T(8,128)S(1)}, u32[]{:S(2)}, u32[]{:S(2)}) collective-permute-start(f32[48,128]{1,0:T(8,128)S(1)} %get-tuple-element.105), channel_id=1, source_target_pairs={{0,28},{4,8},{8,4},{12,16},{16,12},{20,24},{24,20},{28,0},{1,29},{... | collective-permute-start | bytes 73736 | tf_op jit(solution)/shard_map/ppermute | solution.py:423
  27.2 1.3 %collective-permute-start.13 = (f32[48,128]{1,0:T(8,128)S(1)}, f32[48,128]{1,0:T(8,128)S(1)}, u32[]{:S(2)}, u32[]{:S(2)}) collective-permute-start(f32[48,128]{1,0:T(8,128)S(1)} %get-tuple-element.106), channel_id=1, source_target_pairs={{0,1},{1,0},{2,3},{3,2},{4,5},{5,4},{6,7},{7,6},{8,9},{9,8},{10,11... | collective-permute-start | bytes 73736 | tf_op jit(solution)/shard_map/ppermute | solution.py:420
  28.5 0.1 collective-permute-start.14
  28.6 0.9 %window.3 = (f32[40,512]{1,0:T(8,128)S(1)}, f32[64,1024]{1,0:T(8,128)S(1)}, f32[64,384]{1,0:T(8,128)S(1)}) custom-call(s32[4,256]{1,0:T(4,128)S(1)} %get-tuple-element.73.r_0_, f32[40,512]{1,0:T(8,128)S(1)} %get-tuple-element.109.r_1_, f32[40,512]{1,0:T(8,128)S(1)} %get-tuple-element.110.r_2_, f32[64,1024]{1,0:T(8,128)S(1)} %get-tuple-element.111.r_3_, ...), custom_call_target="tpu_custom_call" | custom-call | flops 68719476736 | bytes 65536 | tf_op jit(solution)/shard_map/window/pallas_call | solution.py:402
  29.6 0.0 collective-permute-done.10.r_1_
  29.6 1.3 %collective-permute-done.11.r_2_ = f32[16,128]{1,0:T(8,128)S(1)} collective-permute-done((f32[16,128]{1,0:T(8,128)S(1)}, f32[16,128]{1,0:T(8,128)S(1)}, u32[]{:S(2)}, u32[]{:S(2)}) %collective-permute-start.11) | collective-permute-done | bytes 8224 | tf_op jit(solution)/shard_map/ppermute | solution.py:424
  30.8 0.0 collective-permute-done.12.r_3_
  30.8 0.3 collective-permute-done.13.r_4_
  31.1 0.0 collective-permute-done.14.r_5_
  31.1 1.6 %step.5 = (f32[40,512]{1,0:T(8,128)S(1)}, f32[64,1024]{1,0:T(8,128)S(1)}, f32[48,128]{1,0:T(8,128)S(1)}, f32[48,128]{1,0:T(8,128)S(1)}, f32[48,128]{1,0:T(8,128)...) custom-call(f32[8,128]{1,0:T(8,128)S(1)} %get-tuple-element.66.r_0_, ...), custom_call_target="tpu_custom_call" | custom-call | bytes 65536 | tf_op jit(solution)/shard_map/step/pallas_call | solution.py:402
  32.7 2.1 %collective-permute-start.15 = (f32[16,128]{1,0:T(8,128)S(1)}, f32[16,128]{1,0:T(8,128)S(1)}, u32[]{:S(2)}, u32[]{:S(2)}) collective-permute-start(f32[16,128]{1,0:T(8,128)S(1)} %get-tuple-element.117), channel_id=1, source_target_pairs={{0,3},{1,2},{2,1},{3,0},{4,7},{5,6},{6,5},{7,4},{8,11},{9,10},{10,... | collective-permute-start | bytes 24584 | tf_op jit(solution)/shard_map/ppermute | solution.py:422
  34.8 0.7 %collective-permute-start.16 = (f32[16,128]{1,0:T(8,128)S(1)}, f32[16,128]{1,0:T(8,128)S(1)}, u32[]{:S(2)}, u32[]{:S(2)}) collective-permute-start(f32[16,128]{1,0:T(8,128)S(1)} %get-tuple-element.118), channel_id=1, source_target_pairs={{0,2},{1,3},{2,0},{3,1},{4,6},{5,7},{6,4},{7,5},{8,10},{9,11},{10,... | collective-permute-start | bytes 24584 | tf_op jit(solution)/shard_map/ppermute | solution.py:424
  35.4 0.6 %collective-permute-start.17 = (f32[48,128]{1,0:T(8,128)S(1)}, f32[48,128]{1,0:T(8,128)S(1)}, u32[]{:S(2)}, u32[]{:S(2)}) collective-permute-start(f32[48,128]{1,0:T(8,128)S(1)} %get-tuple-element.119), channel_id=1, source_target_pairs={{0,28},{4,8},{8,4},{12,16},{16,12},{20,24},{24,20},{28,0},{1,29},{... | collective-permute-start | bytes 73736 | tf_op jit(solution)/shard_map/ppermute | solution.py:423
  36.0 1.4 %collective-permute-start.18 = (f32[48,128]{1,0:T(8,128)S(1)}, f32[48,128]{1,0:T(8,128)S(1)}, u32[]{:S(2)}, u32[]{:S(2)}) collective-permute-start(f32[48,128]{1,0:T(8,128)S(1)} %get-tuple-element.120), channel_id=1, source_target_pairs={{0,1},{1,0},{2,3},{3,2},{4,5},{5,4},{6,7},{7,6},{8,9},{9,8},{10,11... | collective-permute-start | bytes 73736 | tf_op jit(solution)/shard_map/ppermute | solution.py:420
  37.4 0.0 collective-permute-start.19
  37.4 1.0 %window3.1.r_7_ = f32[40,1024]{1,0:T(8,128)S(1)} custom-call(f32[40,1024]{1,0:T(8,128)S(1)} %get-tuple-element.123.r_0_, f32[40,1024]{1,0:T(8,128)S(1)} %get-tuple-element.112.r_4_.r_1_, f32[40,512]{1,0:T(8,128)S(1)} %get-tuple-element.124.r_2_, f32[64,1024]{1,0:T(8,128)S(1)} %get-tuple-element.125.r_3_, ...), custom_call_target="tpu_custom_call" | custom-call | flops 68719476736 | bytes 65536 | tf_op jit(solution)/shard_map/window3/pallas_call | solution.py:402
  38.4 0.0 collective-permute-done.15.r_1_
  38.4 0.9 %collective-permute-done.16.r_2_ = f32[16,128]{1,0:T(8,128)S(1)} collective-permute-done((f32[16,128]{1,0:T(8,128)S(1)}, f32[16,128]{1,0:T(8,128)S(1)}, u32[]{:S(2)}, u32[]{:S(2)}) %collective-permute-start.16) | collective-permute-done | bytes 8224 | tf_op jit(solution)/shard_map/ppermute | solution.py:424
  39.3 0.3 collective-permute-done.17.r_3_
  39.6 0.2 collective-permute-done.18.r_4_
  39.8 0.0 collective-permute-done.19.r_5_
  39.8 1.3 %last.1 = f32[140,256]{1,0:T(8,128)} custom-call(f32[8,128]{1,0:T(8,128)S(1)} %get-tuple-element.66.r_0_, f32[16,128]{1,0:T(8,128)S(1)} %collective-permute-done.15.r_1_, f32[16,128]{1,0:T(8,128)S(1)} %collective-permute-done.16.r_2_, f32[48,128]{1,0:T(8,128)S(1)} %collective-permute-done.17.r_3_, f32[48,128]{1,0:T(8,128)S(1)} %collective-permute-done.18.r_4_, ...), custom_call_target="tpu_custom_call" | custom-call | bytes 65536 | tf_op jit(solution)/shard_map/last/pallas_call | solution.py:402
Async XLA Ops:
  2.6 8.6 %collective-permute-start = (f32[16,128]{1,0:T(8,128)S(1)}, f32[16,128]{1,0:T(8,128)S(1)}, u32[]{:S(2)}, u32[]{:S(2)}) collective-permute-start(f32[16,128]{1,0:T(8,128)S(1)} %get-tuple-element.67), channel_id=1, source_target_pairs={{0,3},{1,2},{2,1},{3,0},{4,7},{5,6},{6,5},{7,4},{8,11},{9,10},{10,... | collective-permute-start | bytes 24584 | tf_op jit(solution)/shard_map/ppermute | solution.py:422
  7.7 4.6 %collective-permute-start.1 = (f32[16,128]{1,0:T(8,128)S(1)}, f32[16,128]{1,0:T(8,128)S(1)}, u32[]{:S(2)}, u32[]{:S(2)}) collective-permute-start(f32[16,128]{1,0:T(8,128)S(1)} %get-tuple-element.68), channel_id=1, source_target_pairs={{0,2},{1,3},{2,0},{3,1},{4,6},{5,7},{6,4},{7,5},{8,10},{9,11},{10,... | collective-permute-start | bytes 24584 | tf_op jit(solution)/shard_map/ppermute | solution.py:424
  7.7 4.6 %collective-permute-start.2 = (f32[48,128]{1,0:T(8,128)S(1)}, f32[48,128]{1,0:T(8,128)S(1)}, u32[]{:S(2)}, u32[]{:S(2)}) collective-permute-start(f32[48,128]{1,0:T(8,128)S(1)} %get-tuple-element.69), channel_id=1, source_target_pairs={{0,28},{4,8},{8,4},{12,16},{16,12},{20,24},{24,20},{28,0},{1,29},{... | collective-permute-start | bytes 73736 | tf_op jit(solution)/shard_map/ppermute | solution.py:423
  9.3 3.8 %collective-permute-start.3 = (f32[48,128]{1,0:T(8,128)S(1)}, f32[48,128]{1,0:T(8,128)S(1)}, u32[]{:S(2)}, u32[]{:S(2)}) collective-permute-start(f32[48,128]{1,0:T(8,128)S(1)} %get-tuple-element.70), channel_id=1, source_target_pairs={{0,1},{1,0},{2,3},{3,2},{4,5},{5,4},{6,7},{7,6},{8,9},{9,8},{10,11... | collective-permute-start | bytes 73736 | tf_op jit(solution)/shard_map/ppermute | solution.py:420
  10.0 3.2 %collective-permute-start.4 = (f32[48,128]{1,0:T(8,128)S(1)}, f32[48,128]{1,0:T(8,128)S(1)}, u32[]{:S(2)}, u32[]{:S(2)}) collective-permute-start(f32[48,128]{1,0:T(8,128)S(1)} %get-tuple-element.71), channel_id=1, source_target_pairs={{0,4},{4,0},{8,12},{12,8},{16,20},{20,16},{24,28},{28,24},{1,5},{5... | collective-permute-start | bytes 73736 | tf_op jit(solution)/shard_map/ppermute | solution.py:421
  14.8 6.2 %collective-permute-start.5 = (f32[16,128]{1,0:T(8,128)S(1)}, f32[16,128]{1,0:T(8,128)S(1)}, u32[]{:S(2)}, u32[]{:S(2)}) collective-permute-start(f32[16,128]{1,0:T(8,128)S(1)} %get-tuple-element.89), channel_id=1, source_target_pairs={{0,3},{1,2},{2,1},{3,0},{4,7},{5,6},{6,5},{7,4},{8,11},{9,10},{10,... | collective-permute-start | bytes 24584 | tf_op jit(solution)/shard_map/ppermute | solution.py:422
  16.9 4.6 %collective-permute-start.6 = (f32[16,128]{1,0:T(8,128)S(1)}, f32[16,128]{1,0:T(8,128)S(1)}, u32[]{:S(2)}, u32[]{:S(2)}) collective-permute-start(f32[16,128]{1,0:T(8,128)S(1)} %get-tuple-element.90), channel_id=1, source_target_pairs={{0,2},{1,3},{2,0},{3,1},{4,6},{5,7},{6,4},{7,5},{8,10},{9,11},{10,... | collective-permute-start | bytes 24584 | tf_op jit(solution)/shard_map/ppermute | solution.py:424
  17.6 4.2 %collective-permute-start.7 = (f32[48,128]{1,0:T(8,128)S(1)}, f32[48,128]{1,0:T(8,128)S(1)}, u32[]{:S(2)}, u32[]{:S(2)}) collective-permute-start(f32[48,128]{1,0:T(8,128)S(1)} %get-tuple-element.91), channel_id=1, source_target_pairs={{0,28},{4,8},{8,4},{12,16},{16,12},{20,24},{24,20},{28,0},{1,29},{... | collective-permute-start | bytes 73736 | tf_op jit(solution)/shard_map/ppermute | solution.py:423
  17.6 4.1 %collective-permute-start.8 = (f32[48,128]{1,0:T(8,128)S(1)}, f32[48,128]{1,0:T(8,128)S(1)}, u32[]{:S(2)}, u32[]{:S(2)}) collective-permute-start(f32[48,128]{1,0:T(8,128)S(1)} %get-tuple-element.92), channel_id=1, source_target_pairs={{0,1},{1,0},{2,3},{3,2},{4,5},{5,4},{6,7},{7,6},{8,9},{9,8},{10,11... | collective-permute-start | bytes 73736 | tf_op jit(solution)/shard_map/ppermute | solution.py:420
  19.3 2.5 %collective-permute-start.9 = (f32[48,128]{1,0:T(8,128)S(1)}, f32[48,128]{1,0:T(8,128)S(1)}, u32[]{:S(2)}, u32[]{:S(2)}) collective-permute-start(f32[48,128]{1,0:T(8,128)S(1)} %get-tuple-element.93), channel_id=1, source_target_pairs={{0,4},{4,0},{8,12},{12,8},{16,20},{20,16},{24,28},{28,24},{1,5},{5... | collective-permute-start | bytes 73736 | tf_op jit(solution)/shard_map/ppermute | solution.py:421
  23.4 6.2 %collective-permute-start.10 = (f32[16,128]{1,0:T(8,128)S(1)}, f32[16,128]{1,0:T(8,128)S(1)}, u32[]{:S(2)}, u32[]{:S(2)}) collective-permute-start(f32[16,128]{1,0:T(8,128)S(1)} %get-tuple-element.103), channel_id=1, source_target_pairs={{0,3},{1,2},{2,1},{3,0},{4,7},{5,6},{6,5},{7,4},{8,11},{9,10},{10,... | collective-permute-start | bytes 24584 | tf_op jit(solution)/shard_map/ppermute | solution.py:422
  26.3 4.6 %collective-permute-start.11 = (f32[16,128]{1,0:T(8,128)S(1)}, f32[16,128]{1,0:T(8,128)S(1)}, u32[]{:S(2)}, u32[]{:S(2)}) collective-permute-start(f32[16,128]{1,0:T(8,128)S(1)} %get-tuple-element.104), channel_id=1, source_target_pairs={{0,2},{1,3},{2,0},{3,1},{4,6},{5,7},{6,4},{7,5},{8,10},{9,11},{10,... | collective-permute-start | bytes 24584 | tf_op jit(solution)/shard_map/ppermute | solution.py:424
  26.6 4.3 %collective-permute-start.12 = (f32[48,128]{1,0:T(8,128)S(1)}, f32[48,128]{1,0:T(8,128)S(1)}, u32[]{:S(2)}, u32[]{:S(2)}) collective-permute-start(f32[48,128]{1,0:T(8,128)S(1)} %get-tuple-element.105), channel_id=1, source_target_pairs={{0,28},{4,8},{8,4},{12,16},{16,12},{20,24},{24,20},{28,0},{1,29},{... | collective-permute-start | bytes 73736 | tf_op jit(solution)/shard_map/ppermute | solution.py:423
  27.2 3.9 %collective-permute-start.13 = (f32[48,128]{1,0:T(8,128)S(1)}, f32[48,128]{1,0:T(8,128)S(1)}, u32[]{:S(2)}, u32[]{:S(2)}) collective-permute-start(f32[48,128]{1,0:T(8,128)S(1)} %get-tuple-element.106), channel_id=1, source_target_pairs={{0,1},{1,0},{2,3},{3,2},{4,5},{5,4},{6,7},{7,6},{8,9},{9,8},{10,11... | collective-permute-start | bytes 73736 | tf_op jit(solution)/shard_map/ppermute | solution.py:420
  28.5 2.6 %collective-permute-start.14 = (f32[48,128]{1,0:T(8,128)S(1)}, f32[48,128]{1,0:T(8,128)S(1)}, u32[]{:S(2)}, u32[]{:S(2)}) collective-permute-start(f32[48,128]{1,0:T(8,128)S(1)} %get-tuple-element.107), channel_id=1, source_target_pairs={{0,4},{4,0},{8,12},{12,8},{16,20},{20,16},{24,28},{28,24},{1,5},{5... | collective-permute-start | bytes 73736 | tf_op jit(solution)/shard_map/ppermute | solution.py:421
  32.7 5.7 %collective-permute-start.15 = (f32[16,128]{1,0:T(8,128)S(1)}, f32[16,128]{1,0:T(8,128)S(1)}, u32[]{:S(2)}, u32[]{:S(2)}) collective-permute-start(f32[16,128]{1,0:T(8,128)S(1)} %get-tuple-element.117), channel_id=1, source_target_pairs={{0,3},{1,2},{2,1},{3,0},{4,7},{5,6},{6,5},{7,4},{8,11},{9,10},{10,... | collective-permute-start | bytes 24584 | tf_op jit(solution)/shard_map/ppermute | solution.py:422
  34.8 4.5 %collective-permute-start.16 = (f32[16,128]{1,0:T(8,128)S(1)}, f32[16,128]{1,0:T(8,128)S(1)}, u32[]{:S(2)}, u32[]{:S(2)}) collective-permute-start(f32[16,128]{1,0:T(8,128)S(1)} %get-tuple-element.118), channel_id=1, source_target_pairs={{0,2},{1,3},{2,0},{3,1},{4,6},{5,7},{6,4},{7,5},{8,10},{9,11},{10,... | collective-permute-start | bytes 24584 | tf_op jit(solution)/shard_map/ppermute | solution.py:424
  35.4 4.2 %collective-permute-start.17 = (f32[48,128]{1,0:T(8,128)S(1)}, f32[48,128]{1,0:T(8,128)S(1)}, u32[]{:S(2)}, u32[]{:S(2)}) collective-permute-start(f32[48,128]{1,0:T(8,128)S(1)} %get-tuple-element.119), channel_id=1, source_target_pairs={{0,28},{4,8},{8,4},{12,16},{16,12},{20,24},{24,20},{28,0},{1,29},{... | collective-permute-start | bytes 73736 | tf_op jit(solution)/shard_map/ppermute | solution.py:423
  36.0 3.8 %collective-permute-start.18 = (f32[48,128]{1,0:T(8,128)S(1)}, f32[48,128]{1,0:T(8,128)S(1)}, u32[]{:S(2)}, u32[]{:S(2)}) collective-permute-start(f32[48,128]{1,0:T(8,128)S(1)} %get-tuple-element.120), channel_id=1, source_target_pairs={{0,1},{1,0},{2,3},{3,2},{4,5},{5,4},{6,7},{7,6},{8,9},{9,8},{10,11... | collective-permute-start | bytes 73736 | tf_op jit(solution)/shard_map/ppermute | solution.py:420
  37.4 2.4 %collective-permute-start.19 = (f32[48,128]{1,0:T(8,128)S(1)}, f32[48,128]{1,0:T(8,128)S(1)}, u32[]{:S(2)}, u32[]{:S(2)}) collective-permute-start(f32[48,128]{1,0:T(8,128)S(1)} %get-tuple-element.121), channel_id=1, source_target_pairs={{0,4},{4,0},{8,12},{12,8},{16,20},{20,16},{24,28},{28,24},{1,5},{5... | collective-permute-start | bytes 73736 | tf_op jit(solution)/shard_map/ppermute | solution.py:421

commit v5 on v4

--- a/solution.py
+++ b/solution.py
@@ -160,9 +160,12 @@
 
 def first_kernel(n_elem, n_dom, *refs):
     raw = refs[:13]
-    (o_ld, o_dj, o_pf, o_lf, o_coef, o_jac, o_soh, o_at, o_in, o_x, o_xh, o_ph, o_c1, o_c2, o_cs,
-     o_t0, m_a, m_w, m_1, m_2, m_3, m_own) = refs[13:35]
-    held, sem, pad, lists = refs[35:48], refs[48], refs[49], refs[50]
+    (o_ld, o_dj, o_pf, o_norm, o_lift, o_nbr, o_jac, o_soh, o_in, o_xh, o_ph, o_x, o_x1, o_x2,
+     o_x3, o_x4, o_t0, m_a, m_w, m_1, m_2, m_3, m_own) = refs[13:36]
+    held, sem, pad, lists = list(refs[36:46]), refs[46], refs[47], refs[48]
+    held.insert(2, o_norm)
+    held.insert(7, o_lift)
+    held.insert(10, o_nbr)
     copies = [
         pltpu.make_async_copy(src, dst, sem.at[i]) for i, (src, dst) in enumerate(zip(raw, held))
     ]
@@ -191,16 +194,9 @@
         pad[f * KR:f * KR + NF, :NB] = proj[:, f, :]
     hi, lo = hi_lo(pad[:4 * KR])
     pf = (hi + pltpu.roll(hi, BR, 1) + pltpu.roll(lo, 2 * BR, 1)).astype(bf16)
-    pad[...] = jnp.zeros_like(pad)
-    for f in range(4):
-        pad[f * KR:f * KR + NF, :NB] = liftm[:, f, :]
-    full = jnp.transpose(pad[:LANES])[:48]
-    hi, lo = hi_lo(full)
-    lf = jnp.concatenate([hi + pltpu.roll(hi, 64, 1), lo], axis=1).astype(bf16)
     o_ld[...] = ld
     o_dj[...] = dj
     o_pf[...] = pf
-    o_lf[...] = lf
     bulk_row = bulk[...].reshape(1, n_elem)
     dens_row = density[...].reshape(1, n_elem)
     fine = jnp.where(cluster[...].reshape(1, n_elem) == 1, 1.0, 0.0).astype(f32)
@@ -210,28 +206,20 @@
     o_jac[9:18] = -jac_in / dens_row
     o_jac[18:19] = damp
     o_jac[19:20] = fine
-    o_jac[20:24] = jnp.zeros((4, n_elem), f32)
-    speed = jnp.sqrt(bulk_row / dens_row)
-    for f in range(4):
-        n = normals[3 * f:3 * f + 3]
-        lanes = pl.ds(f * n_elem, n_elem)
-        o_coef[0:3, lanes] = 0.5 * bulk_row * n
-        o_coef[3:6, lanes] = 0.5 * n / dens_row
-        o_coef[6:7, lanes] = 0.5 * speed * jnp.sqrt(jnp.sum(n * n, axis=0, keepdims=True))
-        o_coef[7:8, lanes] = jnp.zeros((1, n_elem), f32)
+    o_jac[20:21] = bulk_row
+    o_jac[21:22] = dens_row
+    o_jac[22:24] = jnp.zeros((2, n_elem), f32)
     for q in range(NQ):
         o_x[:NB, q * n_elem:(q + 1) * n_elem] = start[q * NB:(q + 1) * NB]
     x = o_x[...]
     jac = o_jac[...]
     terms = [x]
-    for _ in range(ORDER - 1):
+    for ref in (o_x1, o_x2, o_x3, o_x4):
         terms.append(apply_l(terms[-1], jac, ld, dj, n_elem))
+        ref[...] = terms[-1]
     p0 = combine(terms, 0.0, SUB_DT)
     o_xh[...] = head(x, n_elem)
     o_ph[...] = head(p0, n_elem)
-    o_c1[...] = combine(terms, SUB_DT, 2 * SUB_DT)
-    o_c2[...] = combine(terms, 2 * SUB_DT, 3 * SUB_DT)
-    o_cs[...] = combine(terms, 0.0, step_size)
     t0 = jnp.concatenate(traces(p0, pf, n_elem), axis=1)
     o_t0[...] = t0
     lists[...] = jnp.full(lists.shape, -1, jnp.int32)
@@ -249,11 +237,41 @@
         row = j + lax.broadcasted_iota(jnp.int32, (step, 3 * LANES), 0)
         o_soh[j:j + step] = jnp.where(row == names, 1.0, 0.0).astype(bf16)
     write_parts((m_a, m_w, m_1, m_2, m_3, m_own), gather(t0, o_soh[...]))
-    nbr = neighbours[...]
+
+
+def fine_base(state, pub, t, roh, coef, jac, ld, dj, lf, n_elem):
+    tile = LANES
+    got = gather(t, roh[:4 * n_elem])
+    jumps = [
+        got[:, f * tile:(f + 1) * tile] - t[:, f * n_elem:f * n_elem + tile] for f in range(4)
+    ]
+    corr = lift(jumps, coef, lf, tile, n_elem)
+    return state + apply_l(pub, jac, ld, dj, tile) - corr
+
+
+def head(x, n_elem):
+    return jnp.concatenate(
+        [x[:, q * n_elem:q * n_elem + LANES] for q in range(NQ)], axis=1
+    )
+
+
+def table(at, roh, n_elem, first, count):
+    step = 128
+    for f in range(4):
+        col = at[f:f + 1, first:first + count]
+        for j in range(0, roh.shape[0], step):
+            row = j + lax.broadcasted_iota(jnp.int32, (step, count), 0)
+            roh[j:j + step, f * count:(f + 1) * count] = jnp.where(row == col, 1.0, 0.0).astype(bf16)
+
+
+def remap(nbr, n_elem, n_halo):
+    n_face = 4 * n_elem
+    even = lax.axis_index("dom") % 2 == 0
+    sub_id = lax.axis_index("sub")
     before_at = jnp.where(even, n_face + LANES, n_face)
     after_at = jnp.where(even, n_face, n_face + LANES)
     slot = nbr - (n_face + 2 * n_halo)
-    o_at[...] = jnp.where(
+    return jnp.where(
         nbr < n_face,
         nbr,
         jnp.where(
@@ -268,57 +286,55 @@
     )
 
 
-def fine_base(state, pub, t, roh, coef, jac, ld, dj, lf, n_elem):
-    tile = LANES
-    jumps = []
-    for f in range(4):
-        own = t[:, f * n_elem:f * n_elem + tile]
-        got = gather(t, roh[:4 * n_elem, f * tile:(f + 1) * tile])
-        jumps.append(got - own)
-    corr = lift(jumps, coef, lf, tile, n_elem)
-    return state + apply_l(pub, jac, ld, dj, tile) - corr
-
-
-def head(x, n_elem):
-    return jnp.concatenate(
-        [x[:, q * n_elem:q * n_elem + LANES] for q in range(NQ)], axis=1
-    )
-
-
-def table(at, roh, n_elem, first, count):
-    step = 128
-    for f in range(4):
-        col = at[f:f + 1, first:first + count]
-        for j in range(0, roh.shape[0], step):
-            row = j + lax.broadcasted_iota(jnp.int32, (step, count), 0)
-            roh[j:j + step, f * count:(f + 1) * count] = jnp.where(row == col, 1.0, 0.0).astype(bf16)
+def lift_setup(normals, liftm, jac, o_lf, o_coef, pad, n_elem):
+    pad[...] = jnp.zeros_like(pad)
+    for f in range(4):
+        pad[f * KR:f * KR + NF, :NB] = liftm[:, f, :]
+    full = jnp.transpose(pad[...])[:48]
+    hi, lo = hi_lo(full)
+    o_lf[...] = jnp.concatenate([hi + pltpu.roll(hi, 64, 1), lo], axis=1).astype(bf16)
+    bulk_row, dens_row = jac[20:21], jac[21:22]
+    speed = jnp.sqrt(bulk_row / dens_row)
+    for f in range(4):
+        n = normals[3 * f:3 * f + 3]
+        lanes = pl.ds(f * n_elem, n_elem)
+        o_coef[0:3, lanes] = 0.5 * bulk_row * n
+        o_coef[3:6, lanes] = 0.5 * n / dens_row
+        o_coef[6:7, lanes] = 0.5 * speed * jnp.sqrt(jnp.sum(n * n, axis=0, keepdims=True))
+        o_coef[7:8, lanes] = jnp.zeros((1, n_elem), f32)
 
 
 def coarse_traces(c, soh, jac, pf, o_t, o_s, n_elem):
     fine4 = jnp.concatenate([jac[19:20]] * 4, axis=1)
-    t = jnp.concatenate(traces(c[...], pf[...], n_elem), axis=1)
+    t = jnp.concatenate(traces(c, pf[...], n_elem), axis=1)
     t = jnp.where(fine4 > 0.5, 0.0, t)
     o_t[...] = t
     o_s[...] = gather(t, soh[...])
 
 
-def window0_kernel(n_elem, at, xh, ph, c1, t0, soh, coef, jac, ld, dj, pf, lf,
-                   roh, o_base, o_t1, o_s1):
-    table(at, roh, n_elem, 0, LANES)
-    o_base[...] = fine_base(xh[...], ph[...], t0[...], roh, coef[...], jac[:, :LANES], ld[...],
-                            dj[...], lf[...], n_elem)
-    coarse_traces(c1, soh, jac, pf, o_t1, o_s1, n_elem)
+def window0_kernel(n_elem, n_halo, nbr, normals, liftm, xh, ph, x, x1, x2, x3, x4, t0, soh, jac,
+                   ld, dj, pf, roh, sfh, o_at, o_coef, o_lf, o_base, o_t1, o_s1, pad):
+    for f in range(4):
+        sfh[f * LANES:(f + 1) * LANES] = soh[f * n_elem:f * n_elem + LANES]
+    lift_setup(normals, liftm, jac, o_lf, o_coef, pad, n_elem)
+    o_at[...] = remap(nbr[...], n_elem, n_halo)
+    table(o_at, roh, n_elem, 0, LANES)
+    o_base[...] = fine_base(xh[...], ph[...], t0[...], roh, o_coef[...], jac[:, :LANES], ld[...],
+                            dj[...], o_lf[...], n_elem)
+    c = combine([t[...] for t in (x, x1, x2, x3, x4)], SUB_DT, 2 * SUB_DT)
+    coarse_traces(c, soh, jac, pf, o_t1, o_s1, n_elem)
 
 
 def step_kernel(n_elem, last,
-                inner, r_a, r_w, r_1, r_2, r_3, r_own, base, p_sum, t_coarse, s_coarse,
-                roh, soh, coef, jac, ld, dj, pf, lf,
+                inner, r_a, r_w, r_1, r_2, r_3, r_own, base, p_sum, s_coarse,
+                roh, sfh, coef, jac, ld, dj, pf, lf,
                 *outs):
     o_sum, o_t, m_a, m_w, m_1, m_2, m_3, m_own = outs[:8]
     n_face = 4 * n_elem
     tile = LANES
     got = received((r_a, r_w, r_1, r_2, r_3, r_own), inner[...])
-    jumps = [gather(got, roh[n_face:, f * tile:(f + 1) * tile]) for f in range(4)]
+    got = gather(got, roh[n_face:])
+    jumps = [got[:, f * tile:(f + 1) * tile] for f in range(4)]
     state = base[...] - lift(jumps, coef[...], lf[...], tile, n_elem)
     jac_h = jac[:, :tile]
     terms = [state]
@@ -333,33 +349,48 @@
     fine = jac_h[19:20] > 0.5
     zero = jnp.zeros((4 * KR, tile), f32)
     fine_t = [jnp.where(fine, t, zero) for t in traces(total if last else pub, pf[...], tile)]
-    o_t[...] = t_coarse[...]
-    for f in range(4):
-        o_t[:, f * n_elem:f * n_elem + tile] += fine_t[f]
-    sent = s_coarse[...]
-    for f in range(4):
-        sent = sent + gather(fine_t[f], soh[f * n_elem:f * n_elem + tile])
+    fine_t = jnp.concatenate(fine_t, axis=1)
+    o_t[...] = fine_t
+    sent = s_coarse[...] + gather(fine_t, sfh[...])
     write_parts((m_a, m_w, m_1, m_2, m_3, m_own), sent)
 
 
-def window_kernel(n_elem, tabled, at, state, pub, t, c, roh, soh, coef, jac, ld, dj, pf, lf,
-                  o_base, o_t, o_s, *o_roh):
-    o_base[...] = fine_base(state[...], pub[...], t[...], roh, coef[...], jac[:, :LANES], ld[...],
+def whole_traces(t_coarse, fine_t, n_elem):
+    parts = []
+    for f in range(4):
+        c = t_coarse[:, f * n_elem:(f + 1) * n_elem]
+        parts.append(c[:, :LANES] + fine_t[:, f * LANES:(f + 1) * LANES])
+        parts.append(c[:, LANES:])
+    return jnp.concatenate(parts, axis=1)
+
+
+def window_kernel(n_elem, more, at, state, pub, t_c, t_f, x, x1, x2, x3, x4, roh, soh, coef, jac, ld,
+                  dj, pf, lf, o_base, o_t, o_s, o_more):
+    t = whole_traces(t_c, t_f, n_elem)
+    o_base[...] = fine_base(state[...], pub[...], t, roh, coef[...], jac[:, :LANES], ld[...],
                             dj[...], lf[...], n_elem)
+    terms = [r[...] for r in (x, x1, x2, x3, x4)]
+    if more == "table":
+        c = combine(terms, 2 * SUB_DT, 3 * SUB_DT)
+        table(at, o_more, n_elem, LANES, n_elem - LANES)
+    else:
+        c = combine(terms, 0.0, step_size)
+        o_more[...] = c
     coarse_traces(c, soh, jac, pf, o_t, o_s, n_elem)
-    if tabled:
-        table(at, o_roh[0], n_elem, LANES, n_elem - LANES)
-
-
-def split_gather(x, roh, roh2, rows, f, n_elem):
+
+
+def all_faces(x, roh, roh2, rows, n_elem):
     rest = n_elem - LANES
-    return jnp.concatenate(
-        [gather(x, roh[rows, f * LANES:(f + 1) * LANES]), gather(x, roh2[rows, f * rest:(f + 1) * rest])],
-        axis=1,
-    )
-
-
-def window3_kernel(n_elem, x, cs, total, t, roh, roh2, coef, jac, ld, dj, lf, o_base):
+    one, two = gather(x, roh[rows]), gather(x, roh2[rows])
+    return [
+        jnp.concatenate(
+            [one[:, f * LANES:(f + 1) * LANES], two[:, f * rest:(f + 1) * rest]], axis=1
+        )
+        for f in range(4)
+    ]
+
+
+def window3_kernel(n_elem, x, cs, total, t_c, t_f, roh, roh2, coef, jac, ld, dj, lf, o_base):
     fine = jac[19:20, :LANES] > 0.5
     parts = []
     for q in range(NQ):
@@ -367,11 +398,11 @@
         parts.append(jnp.where(fine, total[:, q * LANES:(q + 1) * LANES], c[:, :LANES]))
         parts.append(c[:, LANES:])
     pub = jnp.concatenate(parts, axis=1)
-    tv = t[...]
+    tv = whole_traces(t_c, t_f, n_elem)
     rows = slice(0, 4 * n_elem)
     jumps = [
-        split_gather(tv, roh, roh2, rows, f, n_elem) - tv[:, f * n_elem:(f + 1) * n_elem]
-        for f in range(4)
+        g - tv[:, f * n_elem:(f + 1) * n_elem]
+        for f, g in enumerate(all_faces(tv, roh, roh2, rows, n_elem))
     ]
     corr = lift(jumps, coef[...], lf[...], n_elem, n_elem)
     o_base[...] = x[...] + apply_l(pub, jac[...], ld[...], dj[...], n_elem) - corr
@@ -380,7 +411,7 @@
 def last_kernel(n_elem, inner, r_a, r_w, r_1, r_2, r_3, r_own, base, roh, roh2, coef, lf, out):
     got = received((r_a, r_w, r_1, r_2, r_3, r_own), inner[...])
     rows = slice(4 * n_elem, 4 * n_elem + 3 * LANES)
-    jumps = [split_gather(got, roh, roh2, rows, f, n_elem) for f in range(4)]
+    jumps = all_faces(got, roh, roh2, rows, n_elem)
     res = base[...] - lift(jumps, coef[...], lf[...], n_elem, n_elem)
     for q in range(NQ):
         out[q * NB:(q + 1) * NB] = res[:NB, q * n_elem:(q + 1) * n_elem]
@@ -438,6 +469,7 @@
         wide = ((BR, NQ * n_elem), f32)
         slim = ((BR, NQ * LANES), f32)
         trace = ((4 * KR, n_face), f32)
+        fine_trace = ((4 * KR, 4 * LANES), f32)
         listed = ((4 * KR, 3 * LANES), f32)
         msg = ((4 * KR, LANES), f32)
         small = ((KR, LANES), f32)
@@ -451,45 +483,51 @@
                cluster, pml_flags, neighbours, dom_send, sub_send]
         first = call(
             lambda *r: first_kernel(n_elem, n_dom, *r), "first",
-            [((128, 128), bf16), ((48, 384), bf16), ((64, 128), bf16), ((48, 256), bf16),
-             ((8, n_face), f32), ((24, n_elem), f32), ((n_face, 3 * LANES), bf16),
-             ((4, n_elem), jnp.int32), msg_row, wide, slim, slim, wide, wide, wide, trace] + msgs,
+            [((128, 128), bf16), ((48, 384), bf16), ((64, 128), bf16)]
+            + [(raw[i].shape, raw[i].dtype) for i in (2, 7, 10)]
+            + [((24, n_elem), f32), ((n_face, 3 * LANES), bf16), msg_row, slim, slim]
+            + [wide] * 5 + [trace] + msgs,
             raw, raw=range(13),
-            scratch=[pltpu.VMEM(a.shape, a.dtype) for a in raw]
+            scratch=[pltpu.VMEM(a.shape, a.dtype) for i, a in enumerate(raw) if i not in (2, 7, 10)]
             + [pltpu.SemaphoreType.DMA((len(raw),)), pltpu.VMEM((128, LANES), f32),
                pltpu.VMEM((8, 3 * LANES), jnp.int32)],
         )
-        ld, dj, pf, lf, coef, jac, soh, at, inner, x, xh, total, c1, c2, cs, t = first[:16]
-        got = exchange(first[16:], n_dom)
-        roh, base, t_c, s_c = call(
-            lambda *r: window0_kernel(n_elem, *r), "window0", [half, slim, trace, listed],
-            [at, xh, total, c1, t, soh, coef, jac, ld, dj, pf, lf], flops=1 << 36,
+        ld, dj, pf, norm, liftm, nbr, jac, soh, inner, xh, total, *terms, t = first[:17]
+        got = exchange(first[17:], n_dom)
+        roh, sfh, at, coef, lf, base, t_c, s_c = call(
+            lambda *r: window0_kernel(n_elem, n_halo, *r), "window0",
+            [half, ((4 * LANES, 3 * LANES), bf16), ((4, n_elem), jnp.int32), ((8, n_face), f32), ((48, 256), bf16), slim, trace,
+             listed],
+            [nbr, norm, liftm, xh, total, *terms, t, soh, jac, ld, dj, pf],
+            scratch=[pltpu.VMEM((LANES, LANES), f32)], flops=1 << 36,
         )
-        roh2 = None
+        roh2 = cs = None
         for s in range(SUBSTEPS - 1):
             last = s == SUBSTEPS - 2
             outs = call(
                 lambda *r, last=last: step_kernel(n_elem, last, *r), "step",
-                [slim, trace] + msgs + ([] if last else [slim] * 2),
-                [inner, *got, base, total, t_c, s_c, roh, soh, coef, jac, ld, dj, pf, lf],
+                [slim, fine_trace] + msgs + ([] if last else [slim] * 2),
+                [inner, *got, base, total, s_c, roh, sfh, coef, jac, ld, dj, pf, lf],
             )
             total, t = outs[:2]
             got = exchange(outs[2:8], n_dom)
             if last:
                 (base,) = call(
                     lambda *r: window3_kernel(n_elem, *r), "window3", [wide],
-                    [x, cs, total, t, roh, roh2, coef, jac, ld, dj, lf], flops=1 << 36,
+                    [terms[0], cs, total, t_c, t, roh, roh2, coef, jac, ld, dj, lf], flops=1 << 36,
                 )
             else:
-                res = call(
-                    lambda *r, s=s: window_kernel(n_elem, s == 0, *r), "window",
-                    [slim, trace, listed] + ([rest] if s == 0 else []),
-                    [at, outs[8], outs[9], t, (c2, cs)[s], roh, soh, coef, jac, ld, dj, pf, lf],
+                more = ("table", "sum")[s]
+                base, t_c, s_c, extra = call(
+                    lambda *r, more=more: window_kernel(n_elem, more, *r), "window",
+                    [slim, trace, listed, rest if s == 0 else wide],
+                    [at, outs[8], outs[9], t_c, t, *terms, roh, soh, coef, jac, ld, dj, pf, lf],
                     flops=1 << 36,
                 )
-                base, t_c, s_c = res[:3]
                 if s == 0:
-                    roh2 = res[3]
+                    roh2 = extra
+                else:
+                    cs = extra
         (out,) = call(
             lambda *r: last_kernel(n_elem, *r), "last",
             [((NQ * NB, n_elem), f32)], [inner, *got, base, roh, roh2, coef, lf], hbm_out=True,

time: 41.3 us -> 40.9 us (level)
  Pallas kernels: 13.1 us -> 12.2 us
  waiting for transfers between devices: 5.69 us -> 6.18 us
    pallas_call x9, Pallas kernels: 13.1 us -> 12.2 us  [call(): pl.pallas_call(kernel, in_specs=specs, out_specs=[vm] * len(shapes), out_...]
    ppermute x4, waiting for transfers between devices: 3.84 us -> 4.37 us  [exchange(): r2 = lax.ppermute(s2, 'sub', [(i, i ^ 2) for i in range(4)])]
  transfers between devices with their start and end apart: 20 -> 20, of which waited for: 9 -> 10; matrix products, arithmetic and copies ran while one was open for 0% -> 0% of each run, Pallas kernels for 11% -> 10%
where the time goes in v5:
time: 40.9 us; the launch traced here: 40.7 us
  starting transfers between devices  22.2 us (54%)
  Pallas kernels  12.2 us (30%)
  waiting for transfers between devices  6.18 us (15%)
    pallas_call x9, Pallas kernels, call(): pl.pallas_call(kernel, in_specs=specs, out_specs=[vm] * len(shapes), out_...  12.2 us
    ppermute x4, starting transfers between devices, exchange(): r3 = lax.ppermute(s3, 'sub', [(i, i ^ 3) for i in range(4)])  12.2 us
    ppermute x4, starting transfers between devices, exchange(): r1 = lax.ppermute(s1, 'sub', [(i, i ^ 1) for i in range(4)])  4.9 us
    ppermute x4, waiting for transfers between devices, exchange(): r2 = lax.ppermute(s2, 'sub', [(i, i ^ 2) for i in range(4)])  4.37 us
    ppermute x4, starting transfers between devices, exchange(): rw = lax.ppermute(w, 'dom', other)  2.88 us
    ppermute x4, starting transfers between devices, exchange(): r2 = lax.ppermute(s2, 'sub', [(i, i ^ 2) for i in range(4)])  1.55 us
    ppermute x4, waiting for transfers between devices, exchange(): r1 = lax.ppermute(s1, 'sub', [(i, i ^ 1) for i in range(4)])  1.32 us
  transfers between devices with their start and end apart: 20, of which 10 were waited for; matrix products, arithmetic and copies ran while one was open for 0% of the time, Pallas kernels for 10%

profile of v5, /device:TPU:0, one launch (start us, length us, event | category | flops | bytes accessed | tf_op | source)
XLA Modules:
  0.0 40.7 jit_solution(5260121393955194977)
XLA Ops:
  0.0 2.5 %first.1 = (bf16[128,128]{1,0:T(8,128)(2,1)S(1)}, bf16[48,384]{1,0:T(8,128)(2,1)S(1)}, bf16[64,128]{1,0:T(8,128)(2,1)S(1)}, f32[12,256]{1,0:T(8,128)S(1)}, f32[1...) custom-call(f32[140,256]{1,0:T(8,128)} %r_0_.1, ...), custom_call_target="tpu_custom_call" | custom-call | bytes 65536 | tf_op jit(solution)/shard_map/first/pallas_call | solution.py:433
  2.5 5.1 %collective-permute-start = (f32[16,128]{1,0:T(8,128)S(1)}, f32[16,128]{1,0:T(8,128)S(1)}, u32[]{:S(2)}, u32[]{:S(2)}) collective-permute-start(f32[16,128]{1,0:T(8,128)S(1)} %get-tuple-element.73), channel_id=1, source_target_pairs={{0,3},{1,2},{2,1},{3,0},{4,7},{5,6},{6,5},{7,4},{8,11},{9,10},{10,... | collective-permute-start | bytes 24584 | tf_op jit(solution)/shard_map/ppermute | solution.py:453
  7.6 0.0 collective-permute-start.1
  7.6 1.6 %collective-permute-start.2 = (f32[48,128]{1,0:T(8,128)S(1)}, f32[48,128]{1,0:T(8,128)S(1)}, u32[]{:S(2)}, u32[]{:S(2)}) collective-permute-start(f32[48,128]{1,0:T(8,128)S(1)} %get-tuple-element.75), channel_id=1, source_target_pairs={{0,28},{4,8},{8,4},{12,16},{16,12},{20,24},{24,20},{28,0},{1,29},{... | collective-permute-start | bytes 73736 | tf_op jit(solution)/shard_map/ppermute | solution.py:454
  9.2 0.6 %collective-permute-start.3 = (f32[48,128]{1,0:T(8,128)S(1)}, f32[48,128]{1,0:T(8,128)S(1)}, u32[]{:S(2)}, u32[]{:S(2)}) collective-permute-start(f32[48,128]{1,0:T(8,128)S(1)} %get-tuple-element.76), channel_id=1, source_target_pairs={{0,1},{1,0},{2,3},{3,2},{4,5},{5,4},{6,7},{7,6},{8,9},{9,8},{10,11... | collective-permute-start | bytes 73736 | tf_op jit(solution)/shard_map/ppermute | solution.py:451
  9.9 0.0 collective-permute-start.4
  9.9 1.2 %window0.1 = (bf16[1408,512]{1,0:T(8,128)(2,1)S(1)}, bf16[512,384]{1,0:T(8,128)(2,1)S(1)}, s32[4,256]{1,0:T(4,128)S(1)}, f32[8,1024]{1,0:T(8,128)S(1)}, bf16[48,...) custom-call(s32[4,256]{1,0:T(4,128)S(1)} %get-tuple-element.79.r_0_, ...), custom_call_target="tpu_custom_call" | custom-call | flops 68719476736 | bytes 65536 | tf_op jit(solution)/shard_map/window0/pallas_call | solution.py:433
  11.0 0.0 collective-permute-done.r_1_
  11.1 1.1 %collective-permute-done.1.r_2_ = f32[16,128]{1,0:T(8,128)S(1)} collective-permute-done((f32[16,128]{1,0:T(8,128)S(1)}, f32[16,128]{1,0:T(8,128)S(1)}, u32[]{:S(2)}, u32[]{:S(2)}) %collective-permute-start.1) | collective-permute-done | bytes 8224 | tf_op jit(solution)/shard_map/ppermute | solution.py:455
  12.2 0.0 collective-permute-done.2.r_3_
  12.2 0.9 %collective-permute-done.3.r_4_ = f32[48,128]{1,0:T(8,128)S(1)} collective-permute-done((f32[48,128]{1,0:T(8,128)S(1)}, f32[48,128]{1,0:T(8,128)S(1)}, u32[]{:S(2)}, u32[]{:S(2)}) %collective-permute-start.3) | collective-permute-done | bytes 24608 | tf_op jit(solution)/shard_map/ppermute | solution.py:451
  13.1 0.0 collective-permute-done.4.r_5_
  13.1 1.5 %step.3 = (f32[40,512]{1,0:T(8,128)S(1)}, f32[64,512]{1,0:T(8,128)S(1)}, f32[48,128]{1,0:T(8,128)S(1)}, f32[48,128]{1,0:T(8,128)S(1)}, f32[48,128]{1,0:T(8,128)S...) custom-call(f32[8,128]{1,0:T(8,128)S(1)} %get-tuple-element.72.r_0_,, ...), custom_call_target="tpu_custom_call" | custom-call | bytes 65536 | tf_op jit(solution)/shard_map/step/pallas_call | solution.py:433
  14.6 2.1 %collective-permute-start.5 = (f32[16,128]{1,0:T(8,128)S(1)}, f32[16,128]{1,0:T(8,128)S(1)}, u32[]{:S(2)}, u32[]{:S(2)}) collective-permute-start(f32[16,128]{1,0:T(8,128)S(1)} %get-tuple-element.101), channel_id=1, source_target_pairs={{0,3},{1,2},{2,1},{3,0},{4,7},{5,6},{6,5},{7,4},{8,11},{9,10},{10,... | collective-permute-start | bytes 24584 | tf_op jit(solution)/shard_map/ppermute | solution.py:453
  16.8 0.6 %collective-permute-start.6 = (f32[16,128]{1,0:T(8,128)S(1)}, f32[16,128]{1,0:T(8,128)S(1)}, u32[]{:S(2)}, u32[]{:S(2)}) collective-permute-start(f32[16,128]{1,0:T(8,128)S(1)} %get-tuple-element.102), channel_id=1, source_target_pairs={{0,2},{1,3},{2,0},{3,1},{4,6},{5,7},{6,4},{7,5},{8,10},{9,11},{10,... | collective-permute-start | bytes 24584 | tf_op jit(solution)/shard_map/ppermute | solution.py:455
  17.4 0.1 collective-permute-start.7
  17.5 1.6 %collective-permute-start.8 = (f32[48,128]{1,0:T(8,128)S(1)}, f32[48,128]{1,0:T(8,128)S(1)}, u32[]{:S(2)}, u32[]{:S(2)}) collective-permute-start(f32[48,128]{1,0:T(8,128)S(1)} %get-tuple-element.104), channel_id=1, source_target_pairs={{0,1},{1,0},{2,3},{3,2},{4,5},{5,4},{6,7},{7,6},{8,9},{9,8},{10,11... | collective-permute-start | bytes 73736 | tf_op jit(solution)/shard_map/ppermute | solution.py:451
  19.1 0.5 %collective-permute-start.9 = (f32[48,128]{1,0:T(8,128)S(1)}, f32[48,128]{1,0:T(8,128)S(1)}, u32[]{:S(2)}, u32[]{:S(2)}) collective-permute-start(f32[48,128]{1,0:T(8,128)S(1)} %get-tuple-element.105), channel_id=1, source_target_pairs={{0,4},{4,0},{8,12},{12,8},{16,20},{20,16},{24,28},{28,24},{1,5},{5... | collective-permute-start | bytes 73736 | tf_op jit(solution)/shard_map/ppermute | solution.py:452
  19.5 1.2 %window.2 = (f32[40,512]{1,0:T(8,128)S(1)}, f32[64,1024]{1,0:T(8,128)S(1)}, f32[64,384]{1,0:T(8,128)S(1)}, bf16[1408,512]{1,0:T(8,128)(2,1)S(1)}) custom-call(s32[4,256]{1,0:T(4,128)S(1)} %get-tuple-element.107.r_0_, f32[40,512]{1,0:T(8,128)S(1)} %get-tuple-element.108.r_1_, f32[40,512]{1,0:T(8,128)S(1)} %get-tuple-element.109.r_2_, ...), custom_call_target="tpu_custom_call" | custom-call | flops 68719476736 | bytes 65536 | tf_op jit(solution)/shard_map/window/pallas_call | solution.py:433
  20.7 0.0 collective-permute-done.5.r_1_
  20.7 0.6 %collective-permute-done.6.r_2_ = f32[16,128]{1,0:T(8,128)S(1)} collective-permute-done((f32[16,128]{1,0:T(8,128)S(1)}, f32[16,128]{1,0:T(8,128)S(1)}, u32[]{:S(2)}, u32[]{:S(2)}) %collective-permute-start.6) | collective-permute-done | bytes 8224 | tf_op jit(solution)/shard_map/ppermute | solution.py:455
  21.4 0.2 collective-permute-done.7.r_3_
  21.5 0.0 collective-permute-done.8.r_4_
  21.6 0.0 collective-permute-done.9.r_5_
  21.6 1.5 %step.4 = (f32[40,512]{1,0:T(8,128)S(1)}, f32[64,512]{1,0:T(8,128)S(1)}, f32[48,128]{1,0:T(8,128)S(1)}, f32[48,128]{1,0:T(8,128)S(1)}, f32[48,128]{1,0:T(8,128)S...) custom-call(f32[8,128]{1,0:T(8,128)S(1)} %get-tuple-element.72.r_0_,, ...), custom_call_target="tpu_custom_call" | custom-call | bytes 65536 | tf_op jit(solution)/shard_map/step/pallas_call | solution.py:433
  23.1 2.9 %collective-permute-start.10 = (f32[16,128]{1,0:T(8,128)S(1)}, f32[16,128]{1,0:T(8,128)S(1)}, u32[]{:S(2)}, u32[]{:S(2)}) collective-permute-start(f32[16,128]{1,0:T(8,128)S(1)} %get-tuple-element.115), channel_id=1, source_target_pairs={{0,3},{1,2},{2,1},{3,0},{4,7},{5,6},{6,5},{7,4},{8,11},{9,10},{10,... | collective-permute-start | bytes 24584 | tf_op jit(solution)/shard_map/ppermute | solution.py:453
  26.0 0.3 collective-permute-start.11
  26.3 0.6 %collective-permute-start.12 = (f32[48,128]{1,0:T(8,128)S(1)}, f32[48,128]{1,0:T(8,128)S(1)}, u32[]{:S(2)}, u32[]{:S(2)}) collective-permute-start(f32[48,128]{1,0:T(8,128)S(1)} %get-tuple-element.117), channel_id=1, source_target_pairs={{0,28},{4,8},{8,4},{12,16},{16,12},{20,24},{24,20},{28,0},{1,29},{... | collective-permute-start | bytes 73736 | tf_op jit(solution)/shard_map/ppermute | solution.py:454
  26.9 1.3 %collective-permute-start.13 = (f32[48,128]{1,0:T(8,128)S(1)}, f32[48,128]{1,0:T(8,128)S(1)}, u32[]{:S(2)}, u32[]{:S(2)}) collective-permute-start(f32[48,128]{1,0:T(8,128)S(1)} %get-tuple-element.118), channel_id=1, source_target_pairs={{0,1},{1,0},{2,3},{3,2},{4,5},{5,4},{6,7},{7,6},{8,9},{9,8},{10,11... | collective-permute-start | bytes 73736 | tf_op jit(solution)/shard_map/ppermute | solution.py:451
  28.2 0.1 collective-permute-start.14
  28.3 0.8 %window.3 = (f32[40,512]{1,0:T(8,128)S(1)}, f32[64,1024]{1,0:T(8,128)S(1)}, f32[64,384]{1,0:T(8,128)S(1)}, f32[40,1024]{1,0:T(8,128)S(1)}) custom-call(s32[4,256]{1,0:T(4,128)S(1)} %get-tuple-element.107.r_0_, f32[40,512]{1,0:T(8,128)S(1)} %get-tuple-element.121.r_1_, f32[40,512]{1,0:T(8,128)S(1)} %get-tuple-element.122.r_2_, ...), custom_call_target="tpu_custom_call" | custom-call | flops 68719476736 | bytes 65536 | tf_op jit(solution)/shard_map/window/pallas_call | solution.py:433
  29.2 0.0 collective-permute-done.10.r_1_
  29.2 1.5 %collective-permute-done.11.r_2_ = f32[16,128]{1,0:T(8,128)S(1)} collective-permute-done((f32[16,128]{1,0:T(8,128)S(1)}, f32[16,128]{1,0:T(8,128)S(1)}, u32[]{:S(2)}, u32[]{:S(2)}) %collective-permute-start.11) | collective-permute-done | bytes 8224 | tf_op jit(solution)/shard_map/ppermute | solution.py:455
  30.7 0.0 collective-permute-done.12.r_3_
  30.7 0.1 collective-permute-done.13.r_4_
  30.8 0.0 collective-permute-done.14.r_5_
  30.8 1.5 %step.5 = (f32[40,512]{1,0:T(8,128)S(1)}, f32[64,512]{1,0:T(8,128)S(1)}, f32[48,128]{1,0:T(8,128)S(1)}, f32[48,128]{1,0:T(8,128)S(1)}, f32[48,128]{1,0:T(8,128)S...) custom-call(f32[8,128]{1,0:T(8,128)S(1)} %get-tuple-element.72.r_0_, ...), custom_call_target="tpu_custom_call" | custom-call | bytes 65536 | tf_op jit(solution)/shard_map/step/pallas_call | solution.py:433
  32.4 2.1 %collective-permute-start.15 = (f32[16,128]{1,0:T(8,128)S(1)}, f32[16,128]{1,0:T(8,128)S(1)}, u32[]{:S(2)}, u32[]{:S(2)}) collective-permute-start(f32[16,128]{1,0:T(8,128)S(1)} %get-tuple-element.128), channel_id=1, source_target_pairs={{0,3},{1,2},{2,1},{3,0},{4,7},{5,6},{6,5},{7,4},{8,11},{9,10},{10,... | collective-permute-start | bytes 24584 | tf_op jit(solution)/shard_map/ppermute | solution.py:453
  34.4 0.6 %collective-permute-start.16 = (f32[16,128]{1,0:T(8,128)S(1)}, f32[16,128]{1,0:T(8,128)S(1)}, u32[]{:S(2)}, u32[]{:S(2)}) collective-permute-start(f32[16,128]{1,0:T(8,128)S(1)} %get-tuple-element.129), channel_id=1, source_target_pairs={{0,2},{1,3},{2,0},{3,1},{4,6},{5,7},{6,4},{7,5},{8,10},{9,11},{10,... | collective-permute-start | bytes 24584 | tf_op jit(solution)/shard_map/ppermute | solution.py:455
  35.1 0.6 %collective-permute-start.17 = (f32[48,128]{1,0:T(8,128)S(1)}, f32[48,128]{1,0:T(8,128)S(1)}, u32[]{:S(2)}, u32[]{:S(2)}) collective-permute-start(f32[48,128]{1,0:T(8,128)S(1)} %get-tuple-element.130), channel_id=1, source_target_pairs={{0,28},{4,8},{8,4},{12,16},{16,12},{20,24},{24,20},{28,0},{1,29},{... | collective-permute-start | bytes 73736 | tf_op jit(solution)/shard_map/ppermute | solution.py:454
  35.7 1.4 %collective-permute-start.18 = (f32[48,128]{1,0:T(8,128)S(1)}, f32[48,128]{1,0:T(8,128)S(1)}, u32[]{:S(2)}, u32[]{:S(2)}) collective-permute-start(f32[48,128]{1,0:T(8,128)S(1)} %get-tuple-element.131), channel_id=1, source_target_pairs={{0,1},{1,0},{2,3},{3,2},{4,5},{5,4},{6,7},{7,6},{8,9},{9,8},{10,11... | collective-permute-start | bytes 73736 | tf_op jit(solution)/shard_map/ppermute | solution.py:451
  37.1 0.0 collective-permute-start.19
  37.1 0.7 %window3.1.r_7_ = f32[40,1024]{1,0:T(8,128)S(1)} custom-call(f32[40,1024]{1,0:T(8,128)S(1)} %get-tuple-element.84.r_5_.r_0_, f32[40,1024]{1,0:T(8,128)S(1)} %get-tuple-element.134.r_1_, f32[40,512]{1,0:T(8,128)S(1)} %get-tuple-element.135.r_2_, f32[64,1024]{1,0:T(8,128)S(1)} %get-tuple-element.136.r_3_, f32[64,512]{1,0:T(8,128)S(1)} %get-tuple-element.137.r_4_, ...), custom_call_target="tpu_custom_call" | custom-call | flops 68719476736 | bytes 65536 | tf_op jit(solution)/shard_map/window3/pallas_call | solution.py:433
  37.8 0.1 collective-permute-done.15.r_1_
  37.9 1.1 %collective-permute-done.16.r_2_ = f32[16,128]{1,0:T(8,128)S(1)} collective-permute-done((f32[16,128]{1,0:T(8,128)S(1)}, f32[16,128]{1,0:T(8,128)S(1)}, u32[]{:S(2)}, u32[]{:S(2)}) %collective-permute-start.16) | collective-permute-done | bytes 8224 | tf_op jit(solution)/shard_map/ppermute | solution.py:455
  39.0 0.2 collective-permute-done.17.r_3_
  39.2 0.3 collective-permute-done.18.r_4_
  39.5 0.0 collective-permute-done.19.r_5_
  39.5 1.2 %last.1 = f32[140,256]{1,0:T(8,128)} custom-call(f32[8,128]{1,0:T(8,128)S(1)} %get-tuple-element.72.r_0_, f32[16,128]{1,0:T(8,128)S(1)} %collective-permute-done.15.r_1_, f32[16,128]{1,0:T(8,128)S(1)} %collective-permute-done.16.r_2_, f32[48,128]{1,0:T(8,128)S(1)} %collective-permute-done.17.r_3_, f32[48,128]{1,0:T(8,128)S(1)} %collective-permute-done.18.r_4_, ...), custom_call_target="tpu_custom_call" | custom-call | bytes 65536 | tf_op jit(solution)/shard_map/last/pallas_call | solution.py:433
Async XLA Ops:
  2.5 8.5 %collective-permute-start = (f32[16,128]{1,0:T(8,128)S(1)}, f32[16,128]{1,0:T(8,128)S(1)}, u32[]{:S(2)}, u32[]{:S(2)}) collective-permute-start(f32[16,128]{1,0:T(8,128)S(1)} %get-tuple-element.73), channel_id=1, source_target_pairs={{0,3},{1,2},{2,1},{3,0},{4,7},{5,6},{6,5},{7,4},{8,11},{9,10},{10,... | collective-permute-start | bytes 24584 | tf_op jit(solution)/shard_map/ppermute | solution.py:453
  7.6 4.6 %collective-permute-start.1 = (f32[16,128]{1,0:T(8,128)S(1)}, f32[16,128]{1,0:T(8,128)S(1)}, u32[]{:S(2)}, u32[]{:S(2)}) collective-permute-start(f32[16,128]{1,0:T(8,128)S(1)} %get-tuple-element.74), channel_id=1, source_target_pairs={{0,2},{1,3},{2,0},{3,1},{4,6},{5,7},{6,4},{7,5},{8,10},{9,11},{10,... | collective-permute-start | bytes 24584 | tf_op jit(solution)/shard_map/ppermute | solution.py:455
  7.6 4.6 %collective-permute-start.2 = (f32[48,128]{1,0:T(8,128)S(1)}, f32[48,128]{1,0:T(8,128)S(1)}, u32[]{:S(2)}, u32[]{:S(2)}) collective-permute-start(f32[48,128]{1,0:T(8,128)S(1)} %get-tuple-element.75), channel_id=1, source_target_pairs={{0,28},{4,8},{8,4},{12,16},{16,12},{20,24},{24,20},{28,0},{1,29},{... | collective-permute-start | bytes 73736 | tf_op jit(solution)/shard_map/ppermute | solution.py:454
  9.2 3.8 %collective-permute-start.3 = (f32[48,128]{1,0:T(8,128)S(1)}, f32[48,128]{1,0:T(8,128)S(1)}, u32[]{:S(2)}, u32[]{:S(2)}) collective-permute-start(f32[48,128]{1,0:T(8,128)S(1)} %get-tuple-element.76), channel_id=1, source_target_pairs={{0,1},{1,0},{2,3},{3,2},{4,5},{5,4},{6,7},{7,6},{8,9},{9,8},{10,11... | collective-permute-start | bytes 73736 | tf_op jit(solution)/shard_map/ppermute | solution.py:451
  9.9 3.2 %collective-permute-start.4 = (f32[48,128]{1,0:T(8,128)S(1)}, f32[48,128]{1,0:T(8,128)S(1)}, u32[]{:S(2)}, u32[]{:S(2)}) collective-permute-start(f32[48,128]{1,0:T(8,128)S(1)} %get-tuple-element.77), channel_id=1, source_target_pairs={{0,4},{4,0},{8,12},{12,8},{16,20},{20,16},{24,28},{28,24},{1,5},{5... | collective-permute-start | bytes 73736 | tf_op jit(solution)/shard_map/ppermute | solution.py:452
  14.6 6.1 %collective-permute-start.5 = (f32[16,128]{1,0:T(8,128)S(1)}, f32[16,128]{1,0:T(8,128)S(1)}, u32[]{:S(2)}, u32[]{:S(2)}) collective-permute-start(f32[16,128]{1,0:T(8,128)S(1)} %get-tuple-element.101), channel_id=1, source_target_pairs={{0,3},{1,2},{2,1},{3,0},{4,7},{5,6},{6,5},{7,4},{8,11},{9,10},{10,... | collective-permute-start | bytes 24584 | tf_op jit(solution)/shard_map/ppermute | solution.py:453
  16.8 4.6 %collective-permute-start.6 = (f32[16,128]{1,0:T(8,128)S(1)}, f32[16,128]{1,0:T(8,128)S(1)}, u32[]{:S(2)}, u32[]{:S(2)}) collective-permute-start(f32[16,128]{1,0:T(8,128)S(1)} %get-tuple-element.102), channel_id=1, source_target_pairs={{0,2},{1,3},{2,0},{3,1},{4,6},{5,7},{6,4},{7,5},{8,10},{9,11},{10,... | collective-permute-start | bytes 24584 | tf_op jit(solution)/shard_map/ppermute | solution.py:455
  17.4 4.2 %collective-permute-start.7 = (f32[48,128]{1,0:T(8,128)S(1)}, f32[48,128]{1,0:T(8,128)S(1)}, u32[]{:S(2)}, u32[]{:S(2)}) collective-permute-start(f32[48,128]{1,0:T(8,128)S(1)} %get-tuple-element.103), channel_id=1, source_target_pairs={{0,28},{4,8},{8,4},{12,16},{16,12},{20,24},{24,20},{28,0},{1,29},{... | collective-permute-start | bytes 73736 | tf_op jit(solution)/shard_map/ppermute | solution.py:454
  17.5 4.1 %collective-permute-start.8 = (f32[48,128]{1,0:T(8,128)S(1)}, f32[48,128]{1,0:T(8,128)S(1)}, u32[]{:S(2)}, u32[]{:S(2)}) collective-permute-start(f32[48,128]{1,0:T(8,128)S(1)} %get-tuple-element.104), channel_id=1, source_target_pairs={{0,1},{1,0},{2,3},{3,2},{4,5},{5,4},{6,7},{7,6},{8,9},{9,8},{10,11... | collective-permute-start | bytes 73736 | tf_op jit(solution)/shard_map/ppermute | solution.py:451
  19.1 2.5 %collective-permute-start.9 = (f32[48,128]{1,0:T(8,128)S(1)}, f32[48,128]{1,0:T(8,128)S(1)}, u32[]{:S(2)}, u32[]{:S(2)}) collective-permute-start(f32[48,128]{1,0:T(8,128)S(1)} %get-tuple-element.105), channel_id=1, source_target_pairs={{0,4},{4,0},{8,12},{12,8},{16,20},{20,16},{24,28},{28,24},{1,5},{5... | collective-permute-start | bytes 73736 | tf_op jit(solution)/shard_map/ppermute | solution.py:452
  23.1 6.1 %collective-permute-start.10 = (f32[16,128]{1,0:T(8,128)S(1)}, f32[16,128]{1,0:T(8,128)S(1)}, u32[]{:S(2)}, u32[]{:S(2)}) collective-permute-start(f32[16,128]{1,0:T(8,128)S(1)} %get-tuple-element.115), channel_id=1, source_target_pairs={{0,3},{1,2},{2,1},{3,0},{4,7},{5,6},{6,5},{7,4},{8,11},{9,10},{10,... | collective-permute-start | bytes 24584 | tf_op jit(solution)/shard_map/ppermute | solution.py:453
  26.0 4.7 %collective-permute-start.11 = (f32[16,128]{1,0:T(8,128)S(1)}, f32[16,128]{1,0:T(8,128)S(1)}, u32[]{:S(2)}, u32[]{:S(2)}) collective-permute-start(f32[16,128]{1,0:T(8,128)S(1)} %get-tuple-element.116), channel_id=1, source_target_pairs={{0,2},{1,3},{2,0},{3,1},{4,6},{5,7},{6,4},{7,5},{8,10},{9,11},{10,... | collective-permute-start | bytes 24584 | tf_op jit(solution)/shard_map/ppermute | solution.py:455
  26.3 4.4 %collective-permute-start.12 = (f32[48,128]{1,0:T(8,128)S(1)}, f32[48,128]{1,0:T(8,128)S(1)}, u32[]{:S(2)}, u32[]{:S(2)}) collective-permute-start(f32[48,128]{1,0:T(8,128)S(1)} %get-tuple-element.117), channel_id=1, source_target_pairs={{0,28},{4,8},{8,4},{12,16},{16,12},{20,24},{24,20},{28,0},{1,29},{... | collective-permute-start | bytes 73736 | tf_op jit(solution)/shard_map/ppermute | solution.py:454
  26.9 3.9 %collective-permute-start.13 = (f32[48,128]{1,0:T(8,128)S(1)}, f32[48,128]{1,0:T(8,128)S(1)}, u32[]{:S(2)}, u32[]{:S(2)}) collective-permute-start(f32[48,128]{1,0:T(8,128)S(1)} %get-tuple-element.118), channel_id=1, source_target_pairs={{0,1},{1,0},{2,3},{3,2},{4,5},{5,4},{6,7},{7,6},{8,9},{9,8},{10,11... | collective-permute-start | bytes 73736 | tf_op jit(solution)/shard_map/ppermute | solution.py:451
  28.2 2.7 %collective-permute-start.14 = (f32[48,128]{1,0:T(8,128)S(1)}, f32[48,128]{1,0:T(8,128)S(1)}, u32[]{:S(2)}, u32[]{:S(2)}) collective-permute-start(f32[48,128]{1,0:T(8,128)S(1)} %get-tuple-element.119), channel_id=1, source_target_pairs={{0,4},{4,0},{8,12},{12,8},{16,20},{20,16},{24,28},{28,24},{1,5},{5... | collective-permute-start | bytes 73736 | tf_op jit(solution)/shard_map/ppermute | solution.py:452
  32.4 5.5 %collective-permute-start.15 = (f32[16,128]{1,0:T(8,128)S(1)}, f32[16,128]{1,0:T(8,128)S(1)}, u32[]{:S(2)}, u32[]{:S(2)}) collective-permute-start(f32[16,128]{1,0:T(8,128)S(1)} %get-tuple-element.128), channel_id=1, source_target_pairs={{0,3},{1,2},{2,1},{3,0},{4,7},{5,6},{6,5},{7,4},{8,11},{9,10},{10,... | collective-permute-start | bytes 24584 | tf_op jit(solution)/shard_map/ppermute | solution.py:453
  34.4 4.5 %collective-permute-start.16 = (f32[16,128]{1,0:T(8,128)S(1)}, f32[16,128]{1,0:T(8,128)S(1)}, u32[]{:S(2)}, u32[]{:S(2)}) collective-permute-start(f32[16,128]{1,0:T(8,128)S(1)} %get-tuple-element.129), channel_id=1, source_target_pairs={{0,2},{1,3},{2,0},{3,1},{4,6},{5,7},{6,4},{7,5},{8,10},{9,11},{10,... | collective-permute-start | bytes 24584 | tf_op jit(solution)/shard_map/ppermute | solution.py:455
  35.1 4.2 %collective-permute-start.17 = (f32[48,128]{1,0:T(8,128)S(1)}, f32[48,128]{1,0:T(8,128)S(1)}, u32[]{:S(2)}, u32[]{:S(2)}) collective-permute-start(f32[48,128]{1,0:T(8,128)S(1)} %get-tuple-element.130), channel_id=1, source_target_pairs={{0,28},{4,8},{8,4},{12,16},{16,12},{20,24},{24,20},{28,0},{1,29},{... | collective-permute-start | bytes 73736 | tf_op jit(solution)/shard_map/ppermute | solution.py:454
  35.7 3.8 %collective-permute-start.18 = (f32[48,128]{1,0:T(8,128)S(1)}, f32[48,128]{1,0:T(8,128)S(1)}, u32[]{:S(2)}, u32[]{:S(2)}) collective-permute-start(f32[48,128]{1,0:T(8,128)S(1)} %get-tuple-element.131), channel_id=1, source_target_pairs={{0,1},{1,0},{2,3},{3,2},{4,5},{5,4},{6,7},{7,6},{8,9},{9,8},{10,11... | collective-permute-start | bytes 73736 | tf_op jit(solution)/shard_map/ppermute | solution.py:451
  37.1 2.4 %collective-permute-start.19 = (f32[48,128]{1,0:T(8,128)S(1)}, f32[48,128]{1,0:T(8,128)S(1)}, u32[]{:S(2)}, u32[]{:S(2)}) collective-permute-start(f32[48,128]{1,0:T(8,128)S(1)} %get-tuple-element.132), channel_id=1, source_target_pairs={{0,4},{4,0},{8,12},{12,8},{16,20},{20,16},{24,28},{28,24},{1,5},{5... | collective-permute-start | bytes 73736 | tf_op jit(solution)/shard_map/ppermute | solution.py:452
